TPU v7x, 32 devices: a whole 2x2x4 slice. The times are simulated.
32 devices in a mesh: fsdp: 4 (over z), ctx: 8 (over y, x, core).
Axes of the slice: x: 2, y: 2, z: 4, core: 2. Of those that a mesh axis runs over, the one named last changes fastest.
Arguments:
- inputs: bfloat16 [24, 1024, 768], P('fsdp', 'ctx'), may hold values from -6 to 6
- cotangent: float32 [24, 1024, 768], P('fsdp', 'ctx'), may hold values from -6 to 6
- ln1_gain: bfloat16 [768], P(('fsdp', 'ctx')), may hold values from 0.5 to 1.5
- ln1_bias: bfloat16 [768], P(('fsdp', 'ctx')), may hold values from -1.25 to 1.25
- ln2_gain: bfloat16 [768], P(('fsdp', 'ctx')), may hold values from 0.5 to 1.5
- ln2_bias: bfloat16 [768], P(('fsdp', 'ctx')), may hold values from -1.25 to 1.25
- w_qkv: bfloat16 [768, 2304], P(('fsdp', 'ctx')), as said below
- b_qkv: bfloat16 [2304], P(('fsdp', 'ctx')), may hold values from -1.75 to 1.75
- w_out: bfloat16 [768, 768], P(('fsdp', 'ctx')), may hold values from -2.5 to 2.5
- b_out: bfloat16 [768], P(('fsdp', 'ctx')), may hold values from -1.75 to 1.75
- w_in: bfloat16 [768, 3072], P(('fsdp', 'ctx')), may hold values from -0.21875 to 0.21875
- b_in: bfloat16 [3072], P(('fsdp', 'ctx')), may hold values from -1.75 to 1.75
- w_mlp_out: bfloat16 [3072, 768], P(('fsdp', 'ctx')), may hold values from -0.109375 to 0.109375
- b_mlp_out: bfloat16 [768], P(('fsdp', 'ctx')), may hold values from -1.75 to 1.75
Outputs:
- outputs: float32 [24, 1024, 768], P('fsdp', 'ctx')
- grad_inputs: float32 [24, 1024, 768], P('fsdp', 'ctx')
- grad_ln1_gain: float32 [768], P(('fsdp', 'ctx'))
- grad_ln1_bias: float32 [768], P(('fsdp', 'ctx'))
- grad_ln2_gain: float32 [768], P(('fsdp', 'ctx'))
- grad_ln2_bias: float32 [768], P(('fsdp', 'ctx'))
- grad_w_qkv: float32 [768, 2304], P(('fsdp', 'ctx'))
- grad_b_qkv: float32 [2304], P(('fsdp', 'ctx'))
- grad_w_out: float32 [768, 768], P(('fsdp', 'ctx'))
- grad_b_out: float32 [768], P(('fsdp', 'ctx'))
- grad_w_in: float32 [768, 3072], P(('fsdp', 'ctx'))
- grad_b_in: float32 [3072], P(('fsdp', 'ctx'))
- grad_w_mlp_out: float32 [3072, 768], P(('fsdp', 'ctx'))
- grad_b_mlp_out: float32 [768], P(('fsdp', 'ctx'))
Inputs may be any that keep to these rules, and one draw needn't show every extreme that they name: `w_qkv`: a weight matrix whose entries lie within 24 / sqrt(768) of zero.
All inputs are finite; a program needn't handle non-finite values.
Results may differ from a plain program's by a relative error of at most 0.012.
Values may be sent and summed in bfloat16 or wider, within the bound.
No kernel may reach another device: no remote copies, remote signals or barrier semaphores. Data moves between devices by JAX's collectives and lax.ppermute only.
A program may use at most 448 MiB of HBM per device.

v0:
```python
import math

import jax
import jax.numpy as jnp
from jax import lax
from jax.sharding import PartitionSpec as P

HEADS = 12
HEAD_DIM = 64
ROT_DIM = 16
MICRO = 2
SEQ_MB = 3


EPS = 1e-05
BASE_FREQ = 10000.0


def layer_norm(values, gain_row, shift_row):
    centre = jnp.mean(values, axis=-1, keepdims=True)
    centred = values - centre
    inverse = lax.rsqrt(jnp.mean(centred * centred, axis=-1, keepdims=True) + EPS)
    normed = centred * inverse
    return (normed * gain_row + shift_row, normed, inverse)


def norm_back(grad_out, normed, inverse, gain_row):
    scaled = grad_out * gain_row
    return inverse * (
        scaled
        - jnp.mean(scaled, axis=-1, keepdims=True)
        - normed * jnp.mean(scaled * normed, axis=-1, keepdims=True)
    )


def angles(positions):
    half_rot = ROT_DIM // 2
    inv_freq = BASE_FREQ ** (-(2.0 * jnp.arange(half_rot, dtype=jnp.float32)) / ROT_DIM)
    phase_angle = positions.astype(jnp.float32)[:, None] * inv_freq[None, :]
    return (jnp.cos(phase_angle), jnp.sin(phase_angle))


def rotate(head_field, cosine, sine_rot, direction):
    half_rot = ROT_DIM // 2
    lead_half = head_field[..., :half_rot]
    trail_half = head_field[..., half_rot:ROT_DIM]
    cos_wide = cosine[:, None, :]
    sin_wide = direction * sine_rot[:, None, :]
    return jnp.concatenate(
        [
            lead_half * cos_wide - trail_half * sin_wide,
            trail_half * cos_wide + lead_half * sin_wide,
            head_field[..., ROT_DIM:],
        ],
        axis=-1,
    )


def gelu_parts(pre_act):
    normal_cdf = 0.5 * (1.0 + jax.scipy.special.erf(pre_act * 0.7071067811865476))
    density = jnp.exp(-0.5 * pre_act * pre_act) * 0.3989422804014327
    return (pre_act * normal_cdf, normal_cdf + pre_act * density)


def outer_rows(left, right):
    return lax.dot_general(
        left, right, (((0,), (0,)), ((), ())), preferred_element_type=jnp.float32
    )


def times_transpose(left, right):
    return lax.dot_general(
        left, right, (((1,), (1,)), ((), ())), preferred_element_type=jnp.float32
    )


def attend_block(soft_state, kv_block, first_row, query_low, positions, score_scale):
    run_max, run_sum, weighted = soft_state
    seq_count, block_rows, double_width = kv_block.shape
    model_width = double_width // 2
    key_low = kv_block[..., :model_width].reshape(seq_count, block_rows, HEADS, HEAD_DIM)
    value_low = kv_block[..., model_width:].reshape(seq_count, block_rows, HEADS, HEAD_DIM)
    scores = (
        jnp.einsum("sqhd,skhd->shqk", query_low, key_low, preferred_element_type=jnp.float32)
        * score_scale
    )
    allowed = (first_row + jnp.arange(block_rows, dtype=jnp.int32))[None, :] <= positions[:, None]
    scores = jnp.where(allowed, scores, -jnp.inf)
    new_max = jnp.maximum(run_max, jnp.max(scores, axis=-1))
    safe_max = jnp.where(new_max == -jnp.inf, 0.0, new_max)
    exp_scores = jnp.exp(scores - safe_max[..., None])
    factor = jnp.exp(run_max - safe_max)
    run_sum = run_sum * factor + jnp.sum(exp_scores, axis=-1)
    weighted = weighted * factor[..., None] + jnp.einsum(
        "shqk,skhd->shqd",
        exp_scores.astype(jnp.bfloat16),
        value_low,
        preferred_element_type=jnp.float32,
    )
    return (new_max, run_sum, weighted)


def attend_piece(soft_state, kv_piece, query_low, positions, score_scale):
    piece_rows = kv_piece.shape[1]
    step_rows = math.gcd(piece_rows, 512)

    def one_block(block_index, inner_state):
        offset = block_index * step_rows
        kv_block = lax.dynamic_slice_in_dim(kv_piece, offset, step_rows, 1)
        return attend_block(inner_state, kv_block, offset, query_low, positions, score_scale)

    return lax.fori_loop(0, piece_rows // step_rows, one_block, soft_state)


def local(
    inputs,
    cotangent,
    ln1_gain,
    ln1_bias,
    ln2_gain,
    ln2_bias,
    w_qkv,
    b_qkv,
    w_out,
    b_out,
    w_in,
    b_in,
    w_mlp_out,
    b_mlp_out,
):
    f32 = jnp.float32
    bf16 = jnp.bfloat16
    group_rows = inputs.shape[1]
    model_width = inputs.shape[2]
    seq_len = group_rows * lax.axis_size("ctx")
    key_block = math.gcd(seq_len, 512)
    score_scale = HEAD_DIM ** (-0.5)
    positions = lax.axis_index("ctx") * group_rows + jnp.arange(group_rows, dtype=jnp.int32)
    cosine, sine_rot = angles(positions)

    def gather_params():
        return (
            lax.all_gather(ln1_gain, ("fsdp", "ctx"), axis=0, tiled=True),
            lax.all_gather(ln1_bias, ("fsdp", "ctx"), axis=0, tiled=True),
            lax.all_gather(ln2_gain, ("fsdp", "ctx"), axis=0, tiled=True),
            lax.all_gather(ln2_bias, ("fsdp", "ctx"), axis=0, tiled=True),
            lax.all_gather(w_qkv, ("fsdp", "ctx"), axis=0, tiled=True),
            lax.all_gather(b_qkv, ("fsdp", "ctx"), axis=0, tiled=True),
            lax.all_gather(w_out, ("fsdp", "ctx"), axis=0, tiled=True),
            lax.all_gather(b_out, ("fsdp", "ctx"), axis=0, tiled=True),
            lax.all_gather(w_in, ("fsdp", "ctx"), axis=0, tiled=True),
            lax.all_gather(b_in, ("fsdp", "ctx"), axis=0, tiled=True),
            lax.all_gather(w_mlp_out, ("fsdp", "ctx"), axis=0, tiled=True),
            lax.all_gather(b_mlp_out, ("fsdp", "ctx"), axis=0, tiled=True),
        )

    weight_sums = None
    output_list = []
    grad_list = []
    for micro_index in range(MICRO):
        batch_rows = inputs[micro_index * SEQ_MB : (micro_index + 1) * SEQ_MB]
        cot_rows = cotangent[micro_index * SEQ_MB : (micro_index + 1) * SEQ_MB]
        seq_count = batch_rows.shape[0]
        flat_rows = seq_count * group_rows
        params_fwd = gather_params()
        (
            gain_one,
            shift_one,
            gain_two,
            shift_two,
            weight_qkv,
            bias_qkv,
            weight_out,
            bias_out,
            weight_in,
            bias_in,
            weight_mlp,
            bias_mlp,
        ) = params_fwd
        residual = batch_rows.reshape(flat_rows, model_width).astype(f32)
        normal_one, normed_one, inverse_one = layer_norm(
            residual, gain_one.astype(f32), shift_one.astype(f32)
        )
        normal_two, normed_two, inverse_two = layer_norm(
            residual, gain_two.astype(f32), shift_two.astype(f32)
        )
        hidden_one = normal_one.astype(bf16)
        hidden_two = normal_two.astype(bf16)
        project = jnp.dot(hidden_one, weight_qkv, preferred_element_type=f32) + bias_qkv.astype(f32)
        head_shape = (seq_count, group_rows, HEADS, HEAD_DIM)
        query_low = rotate(
            project[:, :model_width].reshape(head_shape), cosine, sine_rot, 1.0
        ).astype(bf16)
        key_low = rotate(
            project[:, model_width : 2 * model_width].reshape(head_shape), cosine, sine_rot, 1.0
        ).astype(bf16)
        value_low = project[:, 2 * model_width :].astype(bf16)
        kv_pack = jnp.concatenate(
            [
                key_low.reshape(seq_count, group_rows, model_width),
                value_low.reshape(seq_count, group_rows, model_width),
            ],
            axis=-1,
        )
        start_state = (
            jnp.full((seq_count, HEADS, group_rows), -jnp.inf, f32),
            jnp.zeros((seq_count, HEADS, group_rows), f32),
            jnp.zeros((seq_count, HEADS, group_rows, HEAD_DIM), f32),
        )
        soft_state = attend_piece(
            start_state,
            lax.all_gather(kv_pack, "ctx", axis=1, tiled=True),
            query_low,
            positions,
            score_scale,
        )
        run_max, run_sum, weighted = soft_state
        log_total = run_max + jnp.log(run_sum)
        attended = jnp.transpose(weighted / run_sum[..., None], (0, 2, 1, 3)).astype(bf16)
        att_flat = attended.reshape(flat_rows, model_width)
        pre_act = jnp.dot(hidden_two, weight_in, preferred_element_type=f32) + bias_in.astype(f32)
        activation_f, gelu_slope = gelu_parts(pre_act)
        activation = activation_f.astype(bf16)
        output = (
            residual
            + jnp.dot(att_flat, weight_out, preferred_element_type=f32)
            + bias_out.astype(f32)
            + jnp.dot(activation, weight_mlp, preferred_element_type=f32)
            + bias_mlp.astype(f32)
        )
        output_list.append(output.reshape(seq_count, group_rows, model_width))
        params_back = gather_params()
        (
            gain_one,
            shift_one,
            gain_two,
            shift_two,
            weight_qkv,
            bias_qkv,
            weight_out,
            bias_out,
            weight_in,
            bias_in,
            weight_mlp,
            bias_mlp,
        ) = params_back
        kv_rows = lax.all_gather(kv_pack, "ctx", axis=1, tiled=True)
        cot_flat = cot_rows.reshape(flat_rows, model_width)
        cot_low = cot_flat.astype(bf16)
        cot_sum = jnp.sum(cot_flat, axis=0)
        grad_w_out = outer_rows(att_flat, cot_low)
        grad_w_mlp = outer_rows(activation, cot_low)
        d_pre = times_transpose(cot_low, weight_mlp) * gelu_slope
        d_pre_low = d_pre.astype(bf16)
        grad_w_in = outer_rows(hidden_two, d_pre_low)
        d_hidden_two = times_transpose(d_pre_low, weight_in)
        grad_att = times_transpose(cot_low, weight_out).astype(bf16).reshape(head_shape)
        row_delta = jnp.einsum("sqhd,sqhd->shq", grad_att, attended, preferred_element_type=f32)

        def back_block(block_index, loop_carry):
            grad_query, buffer = loop_carry
            offset = block_index * key_block
            kv_block = lax.dynamic_slice_in_dim(kv_rows, offset, key_block, 1)
            key_part = kv_block[..., :model_width].reshape(seq_count, key_block, HEADS, HEAD_DIM)
            value_part = kv_block[..., model_width:].reshape(seq_count, key_block, HEADS, HEAD_DIM)
            scores = (
                jnp.einsum("sqhd,skhd->shqk", query_low, key_part, preferred_element_type=f32)
                * score_scale
            )
            allowed = (offset + jnp.arange(key_block, dtype=jnp.int32))[None, :] <= positions[
                :, None
            ]
            prob_block = jnp.where(allowed, jnp.exp(scores - log_total[..., None]), 0.0)
            grad_value = jnp.einsum(
                "shqk,sqhd->skhd", prob_block.astype(bf16), grad_att, preferred_element_type=f32
            )
            grad_prob = jnp.einsum(
                "sqhd,skhd->shqk", grad_att, value_part, preferred_element_type=f32
            )
            grad_score = (prob_block * (grad_prob - row_delta[..., None]) * score_scale).astype(
                bf16
            )
            grad_query = grad_query + jnp.einsum(
                "shqk,skhd->sqhd", grad_score, key_part, preferred_element_type=f32
            )
            grad_key = jnp.einsum(
                "shqk,sqhd->skhd", grad_score, query_low, preferred_element_type=f32
            )
            key_value_grad = jnp.concatenate(
                [
                    grad_key.reshape(seq_count, key_block, model_width),
                    grad_value.reshape(seq_count, key_block, model_width),
                ],
                axis=-1,
            )
            return (grad_query, lax.dynamic_update_slice_in_dim(buffer, key_value_grad, offset, 1))

        start_carry = (
            jnp.zeros(head_shape, f32),
            jnp.zeros((seq_count, seq_len, 2 * model_width), f32),
        )
        grad_query, buffer = lax.fori_loop(0, seq_len // key_block, back_block, start_carry)
        kv_grad_own = lax.psum_scatter(
            buffer.astype(jnp.bfloat16), "ctx", scatter_dimension=1, tiled=True
        ).astype(jnp.float32)
        key_grad_raw = kv_grad_own[..., :model_width].reshape(head_shape)
        value_grad_flat = kv_grad_own[..., model_width:].reshape(flat_rows, model_width)
        grad_query = rotate(grad_query, cosine, sine_rot, -1.0)
        grad_key = rotate(key_grad_raw, cosine, sine_rot, -1.0)
        d_project = jnp.concatenate(
            [
                grad_query.reshape(flat_rows, model_width),
                grad_key.reshape(flat_rows, model_width),
                value_grad_flat,
            ],
            axis=-1,
        )
        d_project_low = d_project.astype(bf16)
        grad_w_qkv = outer_rows(hidden_one, d_project_low)
        d_hidden_one = times_transpose(d_project_low, weight_qkv)
        grad_rows = (
            cot_flat
            + norm_back(d_hidden_one, normed_one, inverse_one, gain_one.astype(f32))
            + norm_back(d_hidden_two, normed_two, inverse_two, gain_two.astype(f32))
        )
        grad_list.append(grad_rows.reshape(seq_count, group_rows, model_width))
        terms = (
            jnp.sum(d_hidden_one * normed_one, axis=0),
            jnp.sum(d_hidden_one, axis=0),
            jnp.sum(d_hidden_two * normed_two, axis=0),
            jnp.sum(d_hidden_two, axis=0),
            grad_w_qkv,
            jnp.sum(d_project, axis=0),
            grad_w_out,
            cot_sum,
            grad_w_in,
            jnp.sum(d_pre, axis=0),
            grad_w_mlp,
            cot_sum,
        )
        if weight_sums is None:
            weight_sums = terms
        else:
            weight_sums = jax.tree.map(lambda total, term: total + term, weight_sums, terms)
    owned = (
        lax.psum_scatter(weight_sums[0], ("fsdp", "ctx"), scatter_dimension=0, tiled=True),
        lax.psum_scatter(weight_sums[1], ("fsdp", "ctx"), scatter_dimension=0, tiled=True),
        lax.psum_scatter(weight_sums[2], ("fsdp", "ctx"), scatter_dimension=0, tiled=True),
        lax.psum_scatter(weight_sums[3], ("fsdp", "ctx"), scatter_dimension=0, tiled=True),
        lax.psum_scatter(weight_sums[4], ("fsdp", "ctx"), scatter_dimension=0, tiled=True),
        lax.psum_scatter(weight_sums[5], ("fsdp", "ctx"), scatter_dimension=0, tiled=True),
        lax.psum_scatter(weight_sums[6], ("fsdp", "ctx"), scatter_dimension=0, tiled=True),
        lax.psum_scatter(weight_sums[7], ("fsdp", "ctx"), scatter_dimension=0, tiled=True),
        lax.psum_scatter(weight_sums[8], ("fsdp", "ctx"), scatter_dimension=0, tiled=True),
        lax.psum_scatter(weight_sums[9], ("fsdp", "ctx"), scatter_dimension=0, tiled=True),
        lax.psum_scatter(weight_sums[10], ("fsdp", "ctx"), scatter_dimension=0, tiled=True),
        lax.psum_scatter(weight_sums[11], ("fsdp", "ctx"), scatter_dimension=0, tiled=True),
    )
    outputs = jnp.concatenate(output_list, axis=0)
    grad_inputs = jnp.concatenate(grad_list, axis=0)
    return (
        outputs,
        grad_inputs,
        owned[0],
        owned[1],
        owned[2],
        owned[3],
        owned[4],
        owned[5],
        owned[6],
        owned[7],
        owned[8],
        owned[9],
        owned[10],
        owned[11],
    )


def solution(mesh):
    return jax.shard_map(
        local,
        mesh=mesh,
        in_specs=(
            P("fsdp", "ctx", None),
            P("fsdp", "ctx", None),
            P(("fsdp", "ctx")),
            P(("fsdp", "ctx")),
            P(("fsdp", "ctx")),
            P(("fsdp", "ctx")),
            P(("fsdp", "ctx"), None),
            P(("fsdp", "ctx")),
            P(("fsdp", "ctx"), None),
            P(("fsdp", "ctx")),
            P(("fsdp", "ctx"), None),
            P(("fsdp", "ctx")),
            P(("fsdp", "ctx"), None),
            P(("fsdp", "ctx")),
        ),
        out_specs=(
            P("fsdp", "ctx", None),
            P("fsdp", "ctx", None),
            P(("fsdp", "ctx")),
            P(("fsdp", "ctx")),
            P(("fsdp", "ctx")),
            P(("fsdp", "ctx")),
            P(("fsdp", "ctx"), None),
            P(("fsdp", "ctx")),
            P(("fsdp", "ctx"), None),
            P(("fsdp", "ctx")),
            P(("fsdp", "ctx"), None),
            P(("fsdp", "ctx")),
            P(("fsdp", "ctx"), None),
            P(("fsdp", "ctx")),
        ),
        check_vma=False,
    )
```

profile of v0, /device:TPU:0, one launch (start us, length us, event | category | flops | bytes accessed | tf_op | source)
XLA Modules:
  0.0 1064.9 jit_solution(9018735017955234770)
XLA Ops:
  15.5 42.9 %all-reduce.16 = (bf16[768]{0:T(1024)(128)(2,1)S(1)}, bf16[768]{0:T(1024)(128)(2,1)S(1)}, bf16[3072]{0:T(1024)(128)(2,1)}, bf16[768]{0:T(1024)(128)(2,1)}, bf16[...) all-reduce(bf16[768]{0:T(1024)(128)(2,1)S(1)} %dynamic-update-slice, ...), channel_id=1, replica_groups=mesh['fsdp'=4,'ctx'=8] {'fsdp','ctx'}, use_global_device_ids=true, to_apply=%add.5 | all-reduce | flops 9984 | bytes 39936
  64.4 9.1 all-gather.7.cloned.1.call-done
  108.7 20.5 %all-gather.11.cloned.1.call-done = bf16[768,768]{1,0:T(8,128)(2,1)} async-done(((bf16[24,768]{1,0:T(8,128)(2,1)}), bf16[768,768]{1,0:T(8,128)(2,1)}) %all-gather.11.cloned.1.call-update) | async-done | bytes 1179664 | tf_op jit(solution)/shard_map/all_gather | solution.py:149
  142.9 47.7 %all-gather.9.cloned.1.call-done = bf16[3,1024,1536]{1,2,0:T(8,128)(2,1)} async-done(((bf16[3,128,1536]{1,2,0:T(8,128)(2,1)}), bf16[3,1024,1536]{1,2,0:T(8,128)(2,1)}) %all-gather.9.cloned.1.call-update) | async-done | bytes 9437200 | tf_op jit(solution)/shard_map/all_gather | solution.py:212
  190.5 39.3 %while.68 = (s32[]{:T(128)}, f32[3,12,128]{2,1,0:T(8,128)S(1)}, f32[3,12,128]{2,1,0:T(8,128)S(1)}, f32[3,12,128,64]{2,3,1,0:T(8,128)}, bf16[3,1024,1536]{1,2,0:T...) while((s32[]{:T(128)}, f32[3,12,128]{2,1,0:T(8,128)S(1)}, ...), condition=%wide.region_5.0_spmd.clone, body=%wide.region_2.5_spmd.clone.sunk | while | flops 630924416 | bytes 83746024 | solution.py:112
  198.4 6.6 fusion.242
  217.3 5.9 fusion.242
  238.3 62.6 %while.70 = (s32[]{:T(128)}, f32[3,128,12,64]{1,3,2,0:T(8,128)}, bf16[3,1024,1536]{2,1,0:T(8,128)(2,1)}, bf16[3,1024,1536]{1,2,0:T(8,128)(2,1)}, bf16[3,128,12,6...) while((s32[]{:T(128)}, f32[3,128,12,64]{1,3,2,0:T(8,128)}, ...), condition=%wide.region_13.14_spmd.clone, body=%wide.region_12.13_spmd.clone.sunk | while | flops 1545994880 | bytes 116010296 | solution.py:302
  253.9 6.6 copy.224
  284.8 6.6 copy.224
  302.0 37.5 %while.69 = (s32[]{:T(128)}, f32[3,12,128]{2,1,0:T(8,128)S(1)}, f32[3,12,128]{2,1,0:T(8,128)S(1)}, f32[3,12,128,64]{2,3,1,0:T(8,128)}, bf16[3,1024,1536]{1,2,0:T...) while((s32[]{:T(128)}, f32[3,12,128]{2,1,0:T(8,128)S(1)}, ...), condition=%wide.region_11.12_spmd.clone, body=%wide.region_8.0_spmd.clone.sunk | while | flops 630924416 | bytes 83746024 | solution.py:112
  310.1 6.0 fusion.250
  328.1 5.9 fusion.250
  348.0 64.4 %while.71 = (s32[]{:T(128)}, f32[3,128,12,64]{1,3,2,0:T(8,128)}, bf16[3,1024,1536]{2,1,0:T(8,128)(2,1)}, bf16[3,1024,1536]{1,2,0:T(8,128)(2,1)}, bf16[3,128,12,6...) while((s32[]{:T(128)}, f32[3,128,12,64]{1,3,2,0:T(8,128)}, ...), condition=%wide.region_20.21_spmd.clone, body=%wide.region_19.20_spmd.clone.sunk | while | flops 1545994880 | bytes 116010296 | solution.py:302
  363.4 6.8 copy.225
  395.4 7.2 copy.225
  413.5 7.1 multiply_convert_fusion.1
  420.6 6.5 fusion.118
  470.4 72.2 %reduce-scatter.9.cloned.1.call-done = bf16[3,128,1536]{2,1,0:T(8,128)(2,1)} async-done(((bf16[3,1024,1536]{2,1,0:T(8,128)(2,1)}), bf16[3,128,1536]{2,1,0:T(8,128)(2,1)}) %reduce-scatter.9.cloned.1.call-update) | async-done | bytes 1179664 | tf_op jit(solution)/shard_map/reduce_scatter | solution.py:303
  601.6 42.3 %all-reduce.15 = (f32[768]{0:T(1024)S(1)}, f32[768]{0:T(1024)S(1)}, f32[768]{0:T(1024)S(1)}, f32[768]{0:T(1024)S(1)}, f32[2304]{0:T(1024)S(1)}, /*index=5*/f32[768]{0:T(1024)S(1)}, f32[3072]{0:T(1024)S(1)}) all-reduce(f32[768]{0:T(1024)S(1)} %add.485, f32[768]{0:T(1024)S(1)} %add.486, ...), channel_id=4, replica_groups=mesh['fsdp'=4,'ctx'=8] {'fsdp','ctx'}, use_global_device_ids=true, to_apply=%region_28.29.clone | all-reduce | flops 9216 | bytes 73728
  657.9 28.6 %reduce-scatter.15.cloned.1.call-done = f32[24,3072]{1,0:T(8,128)} async-done(((f32[768,3072]{1,0:T(8,128)}), f32[24,3072]{1,0:T(8,128)}) %reduce-scatter.15.cloned.1.call-update) | async-done | bytes 294928 | tf_op jit(solution)/shard_map/reduce_scatter | solution.py:354
  686.5 141.5 %reduce-scatter.17.cloned.1.call-done = f32[96,768]{1,0:T(8,128)} async-done(((f32[3072,768]{1,0:T(8,128)}), f32[96,768]{1,0:T(8,128)}) %reduce-scatter.17.cloned.1.call-update) | async-done | bytes 294928 | tf_op jit(solution)/shard_map/reduce_scatter | solution.py:356
  828.0 104.4 %reduce-scatter.13.cloned.1.call-done = f32[24,768]{1,0:T(8,128)} async-done(((f32[768,768]{1,0:T(8,128)}), f32[24,768]{1,0:T(8,128)}) %reduce-scatter.13.cloned.1.call-update) | async-done | bytes 73744 | tf_op jit(solution)/shard_map/reduce_scatter | solution.py:352
  932.3 124.8 %reduce-scatter.11.cloned.1.call-done = f32[24,2304]{1,0:T(8,128)} async-done(((f32[768,2304]{1,0:T(8,128)}), f32[24,2304]{1,0:T(8,128)}) %reduce-scatter.11.cloned.1.call-update) | async-done | bytes 221200 | tf_op jit(solution)/shard_map/reduce_scatter | solution.py:350
  (507 shorter events, 348.4 us)
Async XLA Ops:
  7.2 54.5 %copy-start.7 = (bf16[6,128,768]{2,1,0:T(8,128)(2,1)S(1)}, bf16[6,128,768]{2,1,0:T(8,128)(2,1)}, u32[]{:S(2)}) copy-start(bf16[6,128,768]{2,1,0:T(8,128)(2,1)} %param.22) | copy-start | bytes 3538948
  7.2 66.4 %all-gather.7.cloned.1.call-start = ((), (), s32[]{:S(2)}) async-start(), calls=%async_computation.6 | async-start | bytes 3649536 | tf_op jit(solution)/shard_map/all_gather | solution.py:147
  7.9 121.3 %all-gather.11.cloned.1.call-start = ((), (), s32[]{:S(2)}) async-start(), calls=%async_computation.8 | async-start | bytes 1216512 | tf_op jit(solution)/shard_map/all_gather | solution.py:149
  8.7 181.9 %all-gather.9.cloned.1.call-start = ((), (), s32[]{:S(2)}) async-start(), calls=%async_computation.7 | async-start | bytes 10616832 | tf_op jit(solution)/shard_map/all_gather | solution.py:212
  61.6 15.5 %copy-start.80 = (f32[384]{0:T(512)}, f32[384]{0:T(512)S(1)}, u32[]{:S(2)}) copy-start(f32[384]{0:T(512)S(1)} %rsqrt_bitcast_fusion) | copy-start | bytes 4612
  61.7 15.5 %copy-start.78 = (f32[384]{0:T(512)}, f32[384]{0:T(512)S(1)}, u32[]{:S(2)}) copy-start(f32[384]{0:T(512)S(1)} %rsqrt_bitcast_fusion.1) | copy-start | bytes 4612
  63.6 13.5 %copy-start.43 = (bf16[384,768]{1,0:T(8,128)(2,1)}, bf16[384,768]{1,0:T(8,128)(2,1)S(1)}, u32[]{:S(2)}) copy-start(bf16[384,768]{1,0:T(8,128)(2,1)S(1)} %get-tuple-element.948) | copy-start | bytes 1769476
  64.4 27.7 %copy-start.72 = (f32[128,8]{0,1:T(8,128)}, f32[128,8]{0,1:T(8,128)S(1)}, u32[]{:S(2)}) copy-start(f32[128,8]{0,1:T(8,128)S(1)} %get-tuple-element.973) | copy-start | bytes 12292
  96.9 204.1 %all-gather.17.cloned.1.call-start = ((), (), s32[]{:S(2)}) async-start(), calls=%async_computation.11 | async-start | bytes 10616832 | tf_op jit(solution)/shard_map/all_gather | solution.py:212
  103.9 309.1 %all-gather.13.cloned.1.call-start = ((), (), s32[]{:S(2)}) async-start(), calls=%async_computation.9 | async-start | bytes 4866048 | tf_op jit(solution)/shard_map/all_gather | solution.py:151
  104.5 316.1 %all-gather.15.cloned.1.call-start = ((), (), s32[]{:S(2)}) async-start(), calls=%async_computation.10 | async-start | bytes 4866048 | tf_op jit(solution)/shard_map/all_gather | solution.py:153
  105.1 362.0 %reduce-scatter.7.cloned.1.call-start = ((), (), s32[]{:S(2)}) async-start(), calls=%async_computation.12 | async-start | bytes 10616832 | tf_op jit(solution)/shard_map/reduce_scatter | solution.py:303
  108.7 22.5 %copy-start.45 = (bf16[384,768]{1,0:T(8,128)(2,1)}, bf16[384,768]{1,0:T(8,128)(2,1)S(1)}, u32[]{:S(2)}) copy-start(bf16[384,768]{1,0:T(8,128)(2,1)S(1)} %get-tuple-element.986) | copy-start | bytes 1769476
  301.0 241.6 %reduce-scatter.9.cloned.1.call-start = ((), (), s32[]{:S(2)}) async-start(), calls=%async_computation.13 | async-start | bytes 10616832 | tf_op jit(solution)/shard_map/reduce_scatter | solution.py:303
  412.4 274.1 %reduce-scatter.15.cloned.1.call-start = ((), (), s32[]{:S(2)}) async-start(), calls=%async_computation.16 | async-start | bytes 9732096 | tf_op jit(solution)/shard_map/reduce_scatter | solution.py:354
  433.6 15.1 %copy-start.23 = (bf16[384,3072]{1,0:T(8,128)(2,1)}, bf16[384,3072]{1,0:T(8,128)(2,1)S(1)}, u32[]{:S(2)}) copy-start(bf16[384,3072]{1,0:T(8,128)(2,1)S(1)} %get-tuple-element.974) | copy-start | bytes 7077892
  444.3 383.6 %reduce-scatter.17.cloned.1.call-start = ((), (), s32[]{:S(2)}) async-start(), calls=%async_computation.17 | async-start | bytes 9732096 | tf_op jit(solution)/shard_map/reduce_scatter | solution.py:356
  454.0 478.3 %reduce-scatter.13.cloned.1.call-start = ((), (), s32[]{:S(2)}) async-start(), calls=%async_computation.15 | async-start | bytes 2433024 | tf_op jit(solution)/shard_map/reduce_scatter | solution.py:352
  459.9 597.2 %reduce-scatter.11.cloned.1.call-start = ((), (), s32[]{:S(2)}) async-start(), calls=%async_computation.14 | async-start | bytes 7299072 | tf_op jit(solution)/shard_map/reduce_scatter | solution.py:350
  552.4 39.8 %copy-start.13 = (f32[96,8,3,128]{3,1,2,0:T(8,128)}, f32[96,8,3,128]{3,1,2,0:T(8,128)S(1)}, u32[]{:S(2)}) copy-start(f32[96,8,3,128]{3,1,2,0:T(8,128)S(1)} %copy.221) | copy-start | bytes 3538948
  580.4 16.4 %copy-start.55 = (f32[384,768]{1,0:T(8,128)}, f32[384,768]{1,0:T(8,128)S(1)}, u32[]{:S(2)}) copy-start(f32[384,768]{1,0:T(8,128)S(1)} %fusion.91) | copy-start | bytes 3538948
  582.8 14.0 %copy-start.57 = (f32[384,768]{1,0:T(8,128)}, f32[384,768]{1,0:T(8,128)S(1)}, u32[]{:S(2)}) copy-start(f32[384,768]{1,0:T(8,128)S(1)} %fusion.87) | copy-start | bytes 3538948
  596.9 55.9 %copy-start.12 = (f32[3,128,768]{2,1,0:T(8,128)S(1)}, f32[3,128,768]{2,1,0:T(8,128)}, u32[]{:S(2)}) copy-start(f32[3,128,768]{2,1,0:T(8,128)} %copy-done.11) | copy-start | bytes 3538948
  644.0 413.2 %copy-start.99 = (f32[24]{0:T(128)}, f32[24]{0:T(128)S(1)}, u32[]{:S(2)}) copy-start(f32[24]{0:T(128)S(1)} %dynamic-slice.5) | copy-start | bytes 292
  (102 other events, 289.2 us)
Sparse Core Ops, SparseCore 0:
  10.9 62.6 all-gather.6
  76.5 52.7 all-gather.10
  131.1 59.3 all-gather.8
  192.3 60.4 all-gather.16
  255.5 63.6 all-gather.12
  322.0 61.9 all-gather.14
  387.4 74.9 reduce-scatter.6
  465.9 76.6 reduce-scatter.8
  549.0 137.3 reduce-scatter.14
  692.8 135.1 reduce-scatter.16
  833.8 98.4 reduce-scatter.12
  938.4 118.6 reduce-scatter.10
where the time goes:
time: 1080 us; the launch traced here: 1060 us
  waiting for transfers between devices  551 us (51%)
  matrix products  170 us (16%)
  local copies, waits for them, and re-layouts  158 us (15%)
  blocking collectives  85.2 us (8%)
  other arithmetic  81.9 us (8%)
  between operations  16.1 us (1%)
    reduce_scatter x1, waiting for transfers between devices, local(): lax.psum_scatter(weight_sums[10], ('fsdp', 'ctx'), scatter_dimension=0, t...  141 us
    reduce_scatter x1, waiting for transfers between devices, local(): lax.psum_scatter(weight_sums[4], ('fsdp', 'ctx'), scatter_dimension=0, ti...  125 us
    reduce_scatter x1, waiting for transfers between devices, local(): lax.psum_scatter(weight_sums[6], ('fsdp', 'ctx'), scatter_dimension=0, ti...  104 us
    unnamed x2, blocking collectives  85.2 us
    reduce_scatter x2, waiting for transfers between devices, local(): lax.psum_scatter(buffer.astype(jnp.bfloat16), 'ctx', scatter_dimension=1,...  72.2 us
    all_gather x2, waiting for transfers between devices, local(): lax.all_gather(kv_pack, 'ctx', axis=1, tiled=True)  47.7 us
    dynamic_update_slice x8, local copies, waits for them, and re-layouts, back_block(): lax.dynamic_update_slice_in_dim(buffer, key_value_grad, offset, 1)  46.6 us
    unnamed x228, local copies, waits for them, and re-layouts  31.5 us
  transfers between devices with their start and end apart: 12, of which 8 were waited for; matrix products, arithmetic and copies ran while one was open for 37% of the time, Pallas kernels for 0%

commit v1 on v0

--- a/solution.py
+++ b/solution.py
@@ -1,15 +1,21 @@
+import functools
 import math
 
 import jax
 import jax.numpy as jnp
+import numpy as np
 from jax import lax
+from jax.experimental import pallas as pl
+from jax.experimental.pallas import tpu as pltpu
 from jax.sharding import PartitionSpec as P
+
 
 HEADS = 12
 HEAD_DIM = 64
 ROT_DIM = 16
 MICRO = 2
 SEQ_MB = 3
+CHUNKS = (1, 2)
 
 
 EPS = 1e-05
@@ -376,9 +382,870 @@
     )
 
 
+ROWS = 128
+BLOCK = 256
+
+
+def swap(value, bit):
+    return lax.ppermute(value, "ctx", [(i, i ^ bit) for i in range(8)])
+
+
+def shift_z(value, step):
+    return lax.ppermute(value, "fsdp", [(i, (i + step) % 4) for i in range(4)])
+
+
+def nt(left, right):
+    return lax.dot_general(
+        left, right, (((1,), (1,)), ((), ())), preferred_element_type=jnp.float32
+    )
+
+
+def nn(left, right):
+    return lax.dot_general(
+        left, right, (((1,), (0,)), ((), ())), preferred_element_type=jnp.float32
+    )
+
+
+def tn(left, right):
+    return lax.dot_general(
+        left, right, (((0,), (0,)), ((), ())), preferred_element_type=jnp.float32
+    )
+
+
+def normalize(values):
+    centred = values - jnp.mean(values, axis=-1, keepdims=True)
+    inverse = lax.rsqrt(jnp.mean(centred * centred, axis=-1, keepdims=True) + EPS)
+    return centred * inverse, inverse
+
+
+def col_sum(values):
+    return jnp.sum(values, axis=0, keepdims=True)
+
+
+def piece_bits(index):
+    return ((index & 1) << 2) | (index & 2) | (index >> 2)
+
+
+def mlp_kernel(chunks, row_ref, *refs):
+    refs = list(refs)
+    parts = [[refs.pop(0) for _ in range(4)] for _ in chunks]
+    weights = [refs.pop(0) for _ in range(8)]
+    vecs, cot_ref, first_send, first_keep = [refs.pop(0) for _ in range(4)]
+    send_ref, keep_ref, rest_ref, gsend_ref, gkeep_ref, vec_ref = [refs.pop(0) for _ in range(6)]
+    w_in, w_down, x_s, c_s, h_s, act_s, dpre_s, part_s, g_in, g_down, seg_s = refs
+    f32, bf16 = jnp.float32, jnp.bfloat16
+    step = pl.program_id(0)
+    gain, shift, bias = vecs[2:3, :], vecs[3:4, :], vecs[6:7, :]
+
+    @pl.when(step == 0)
+    def _():
+        for at, source in enumerate(weights):
+            rows = pl.ds(pl.multiple_of(row_ref[at], 16), 96)
+            w_in[rows, :] = source[:96, :]
+            w_down[rows, :] = source[96:, :]
+        vec_ref[...] = jnp.zeros_like(vec_ref)
+
+    first = 0
+    for at, count in enumerate(chunks):
+        @pl.when((step >= first) & (step < first + count))
+        def _(at=at):
+            for piece in range(8):
+                source = parts[at][piece // 2]
+                rows = slice(piece * ROWS, (piece + 1) * ROWS)
+                x_s[rows, :] = source[piece % 2, 0, 0]
+                c_s[rows, :] = source[piece % 2, 1, 0]
+
+        first += count
+
+    vec_ref[3:4, :] += col_sum(cot_ref[0]) + col_sum(cot_ref[1])
+    for block in range(4):
+        rows = slice(block * 256, (block + 1) * 256)
+        normed, _ = normalize(x_s[rows, :].astype(f32))
+        hidden = (normed * gain + shift).astype(bf16)
+        h_s[rows, :] = hidden
+        pre = nn(hidden, w_in[...]) + bias
+        cdf = 0.5 * (1.0 + lax.erf(pre * 0.7071067811865476))
+        density = jnp.exp(-0.5 * pre * pre) * 0.3989422804014327
+        act = (pre * cdf).astype(bf16)
+        act_s[rows, :] = act
+        cot = c_s[rows, :]
+        d_pre = nt(cot, w_down[...]) * (cdf + pre * density)
+        d_low = d_pre.astype(bf16)
+        dpre_s[rows, :] = d_low
+        out = nn(act, w_down[...])
+        d_hidden = nt(d_low, w_in[...])
+        vec_ref[0:1, :] += col_sum(d_pre)
+        vec_ref[1:2, :] += col_sum(d_hidden * normed)
+        vec_ref[2:3, :] += col_sum(d_hidden)
+        for kind, value in ((0, out), (1, d_hidden * gain)):
+            for half in range(2):
+                part_s[block * 2 + half, kind] = value[half * ROWS : (half + 1) * ROWS].astype(bf16)
+
+    @pl.when(step == 0)
+    def _():
+        g_in[...] = tn(h_s[...], dpre_s[...])
+        g_down[...] = tn(act_s[...], c_s[...])
+        for target, source, first in ((keep_ref, first_keep, 0), (send_ref, first_send, 4)):
+            total = source[...].astype(f32) + part_s[first : first + 4].astype(f32)
+            target[...] = total.astype(bf16)
+
+    @pl.when(step > 0)
+    def _():
+        g_in[...] += tn(h_s[...], dpre_s[...])
+        g_down[...] += tn(act_s[...], c_s[...])
+        rest_ref[0] = part_s[...]
+
+    @pl.when(step == sum(chunks) - 1)
+    def _():
+        for at in range(8):
+            seg_s[at, :, :96] = jnp.broadcast_to(vec_ref[0:1, at * 96 : (at + 1) * 96], (16, 96))
+        for half, target in ((0, gkeep_ref), (1, gsend_ref)):
+            for zz in range(4):
+                at = zz * 2 + (row_ref[24] ^ half)
+                rows = pl.ds(pl.multiple_of(at * 96, 16), 96)
+                target[zz, :96, :] = g_in[rows, :].astype(target.dtype)
+                target[zz, 96:192, :] = g_down[rows, :].astype(target.dtype)
+                target[zz, 192:, :] = jnp.zeros((16, 768), target.dtype)
+                target[zz, 192:, :96] = seg_s[at, :, :96].astype(target.dtype)
+
+
+def whole(shape):
+    return pl.BlockSpec(shape, lambda *_: (0,) * len(shape))
+
+
+def mlp_call(row_offsets, parts, weights, vecs, cot, first_send, first_keep):
+    chunks = tuple(part[0].shape[2] for part in parts)
+    total = sum(chunks)
+    width = vecs.shape[-1]
+    f32, bf16 = jnp.float32, jnp.bfloat16
+
+    def part_spec(first, count):
+        return pl.BlockSpec(
+            (2, 2, 1, ROWS, width),
+            lambda i, *_: (0, 0, jnp.clip(i - first, 0, count - 1), 0, 0),
+        )
+
+    specs, first = [], 0
+    for count in chunks:
+        specs += [part_spec(first, count)] * 4
+        first += count
+    rest_spec = pl.BlockSpec(
+        (1, 8, 2, ROWS, width), lambda i, *_: (jnp.maximum(i - 1, 0), 0, 0, 0, 0)
+    )
+    half = (4, 2, ROWS, width)
+    grads = (4, 208, width)
+    return pl.pallas_call(
+        functools.partial(mlp_kernel, chunks),
+        grid_spec=pltpu.PrefetchScalarGridSpec(
+            num_scalar_prefetch=1,
+            grid=(total,),
+            in_specs=specs
+            + [whole(a.shape) for a in weights]
+            + [whole(vecs.shape), pl.BlockSpec((2, ROWS, width), lambda i, *_: (i, 0, 0))]
+            + [whole(half), whole(half)],
+            out_specs=[whole(half), whole(half), rest_spec, whole(grads), whole(grads), whole((8, width))],
+            scratch_shapes=[pltpu.VMEM((width, width), bf16)] * 2
+            + [pltpu.VMEM((8 * ROWS, width), bf16)] * 5
+            + [pltpu.VMEM((8, 2, ROWS, width), bf16)]
+            + [pltpu.VMEM((width, width), f32)] * 2
+            + [pltpu.VMEM((8, 16, 128), f32)],
+        ),
+        out_shape=[
+            jax.ShapeDtypeStruct(half, bf16),
+            jax.ShapeDtypeStruct(half, bf16),
+            jax.ShapeDtypeStruct((total - 1, 8, 2, ROWS, width), bf16),
+            jax.ShapeDtypeStruct(grads, bf16),
+            jax.ShapeDtypeStruct(grads, f32),
+            jax.ShapeDtypeStruct((8, width), f32),
+        ],
+        compiler_params=pltpu.CompilerParams(vmem_limit_bytes=56 << 20),
+        cost_estimate=pl.CostEstimate(
+            flops=30_000_000_000, transcendentals=0, bytes_accessed=30_000_000
+        ),
+        name="mlp",
+    )(row_offsets, *[a for part in parts for a in part], *weights, vecs, cot, first_send, first_keep)
+
+
+def rotary_tables():
+    f32 = jnp.float32
+    lane = lax.broadcasted_iota(jnp.int32, (32, 128), 1)
+    dim = lane & 63
+    power = (dim & 7).astype(f32) * (-2.0 / ROT_DIM)
+    freq = jnp.where(dim < ROT_DIM, jnp.exp(power * math.log(BASE_FREQ)), 0.0)
+    row = lax.broadcasted_iota(jnp.int32, (32, 128), 0).astype(f32)
+    fine, coarse = row * freq, row * 32.0 * freq
+    cos_fine, sin_fine = jnp.cos(fine), jnp.sin(fine)
+    scale = jnp.where(lane < 64, HEAD_DIM ** (-0.5), 1.0)
+    cos_coarse, sin_coarse = jnp.cos(coarse) * scale, jnp.sin(coarse) * scale
+    first, second = dim[:1] < 8, (dim[:1] >= 8) & (dim[:1] < ROT_DIM)
+    return cos_fine, sin_fine, cos_coarse, sin_coarse, first, second
+
+
+def attn_kernel(has_prev, last, *refs):
+    refs = list(refs)
+    row_ref = refs.pop(0)
+    parts = [refs.pop(0) for _ in range(4)]
+    weights = [refs.pop(0) for _ in range(8)]
+    o_own, o_other = [refs.pop(0) for _ in range(2)]
+    vecs = refs.pop(0)
+    if has_prev:
+        partial = refs.pop(0)
+        pq_ref, po_ref, pv_ref = [refs.pop(0) for _ in range(3)]
+    if last:
+        mv_ref, at_ref, col_ref = [refs.pop(0) for _ in range(3)]
+        send_ref, keep_ref, qsend_ref, qkeep_ref, osend_ref, okeep_ref = [refs.pop(0) for _ in range(6)]
+    else:
+        send_ref, keep_ref, gq_ref, go_ref, vec_ref = [refs.pop(0) for _ in range(5)]
+    wq, wo, x_n, h_s, c_s, q_s, k_s, v_s, kt_s, vt_s, ga_s, gat_s, dk_s, dv_s, at_s, att_s, dp_s, out_s, s_s, tab = refs[:20]
+    f32, bf16 = jnp.float32, jnp.bfloat16
+    seq = 8 * ROWS
+    gain, shift, bias = vecs[0:1, :], vecs[1:2, :], vecs[5:6, :576]
+
+    cos_f, sin_f, cos_c, sin_c, first, second = rotary_tables()
+    for at in range(seq // 32):
+        rows = slice(at * 32, (at + 1) * 32)
+        cosine = cos_f * cos_c[at : at + 1] - sin_f * sin_c[at : at + 1]
+        sine = sin_f * cos_c[at : at + 1] + cos_f * sin_c[at : at + 1]
+        tab[0, rows, :] = cosine
+        tab[1, rows, :] = jnp.where(first, -sine, 0.0)
+        tab[2, rows, :] = jnp.where(second, sine, 0.0)
+
+    for at, source in enumerate(weights):
+        rows = pl.ds(pl.multiple_of(row_ref[at], 16), 96)
+        wq[rows, :] = source[:, :576]
+    for other, source in ((0, o_own), (1, o_other)):
+        rows = pl.ds(pl.multiple_of(row_ref[8 + other], 16), 96)
+        wo[rows, :] = source[...]
+
+    for piece in range(8):
+        source = parts[piece // 2]
+        rows = pl.ds(pl.multiple_of(row_ref[16 + piece], ROWS), ROWS)
+        normed, _ = normalize(source[piece % 2, 0, 0].astype(f32))
+        x_n[rows, :] = normed
+        h_s[rows, :] = (normed * gain + shift).astype(bf16)
+        c_s[rows, :] = source[piece % 2, 1, 0]
+
+    for block in range(4):
+        rows = slice(block * 256, (block + 1) * 256)
+        project = nn(h_s[rows, :], wq[...]) + bias
+        cosine, low, high = tab[0, rows, :], tab[1, rows, :], tab[2, rows, :]
+        grad_t = nt(wo[...], c_s[rows, :])
+        for head in range(3):
+            pair = project[:, head * 128 : (head + 1) * 128]
+            pair = pair * cosine + pltpu.roll(pair, 120, 1) * low + pltpu.roll(pair, 8, 1) * high
+            q_s[head, rows, :] = pair[:, :64].astype(bf16)
+            key = pltpu.roll(pair, 64, 1)[:, :64]
+            k_s[head, rows, :] = key.astype(bf16)
+            kt_s[head, :, rows] = jnp.transpose(key).astype(bf16)
+            value = project[:, 384 + head * 64 : 384 + (head + 1) * 64]
+            v_s[head, rows, :] = value.astype(bf16)
+            vt_s[head, :, rows] = jnp.transpose(value).astype(bf16)
+            part = grad_t[head * 64 : (head + 1) * 64]
+            gat_s[head, :, rows] = part.astype(bf16)
+            ga_s[head, rows, :] = jnp.transpose(part).astype(bf16)
+
+    key_at = lax.broadcasted_iota(jnp.int32, (BLOCK, BLOCK), 0)
+    query_at = lax.broadcasted_iota(jnp.int32, (BLOCK, BLOCK), 1)
+    allowed = key_at <= query_at
+    for head in range(3):
+        for block in range(seq // BLOCK):
+            rows = slice(block * BLOCK, (block + 1) * BLOCK)
+            upto = (block + 1) * BLOCK
+            query = q_s[head, rows, :]
+            grad = ga_s[head, rows, :]
+            diag = jnp.where(allowed, nt(k_s[head, rows, :], query), -1e30)
+            if block:
+                scores = jnp.concatenate([nt(k_s[head, : upto - BLOCK, :], query), diag], axis=0)
+            else:
+                scores = diag
+            top = jnp.max(scores, axis=0, keepdims=True)
+            prob = jnp.exp(scores - top)
+            prob = prob * (1.0 / jnp.sum(prob, axis=0, keepdims=True))
+            low_prob = prob.astype(bf16)
+            att_t = nn(vt_s[head, :, :upto], low_prob)
+            att_low = att_t.astype(bf16)
+            att_s[head * 64 : (head + 1) * 64, rows] = att_low
+            at_s[rows, head * 64 : (head + 1) * 64] = jnp.transpose(att_t).astype(bf16)
+            delta = jnp.sum(
+                gat_s[head, :, rows].astype(f32) * att_low.astype(f32), axis=0, keepdims=True
+            )
+            d_prob = nt(v_s[head, :upto, :], grad)
+            d_score = (prob * (d_prob - delta)).astype(bf16)
+            d_value = nn(low_prob, grad)
+            d_key = nn(d_score, query)
+            if block:
+                keep = slice(0, upto - BLOCK)
+                dv_s[keep, :] += d_value[: upto - BLOCK]
+                dk_s[keep, :] += d_key[: upto - BLOCK]
+            dv_s[rows, :] = d_value[upto - BLOCK :]
+            dk_s[rows, :] = d_key[upto - BLOCK :]
+            d_query = jnp.transpose(nn(kt_s[head, :, :upto], d_score))
+            dp_s[rows, head * 128 : head * 128 + 64] = d_query
+        for block in range(4):
+            rows = slice(block * 256, (block + 1) * 256)
+            pair = jnp.concatenate(
+                [dp_s[rows, head * 128 : head * 128 + 64], dk_s[rows, :]], axis=1
+            )
+            cosine, low, high = tab[0, rows, :], tab[1, rows, :], tab[2, rows, :]
+            pair = pair * cosine - pltpu.roll(pair, 120, 1) * low - pltpu.roll(pair, 8, 1) * high
+            dp_s[rows, head * 128 : (head + 1) * 128] = pair
+            dp_s[rows, 384 + head * 64 : 384 + (head + 1) * 64] = dv_s[rows, :]
+
+    project = dp_s[...]
+    project_low = project.astype(bf16)
+    g_query = tn(h_s[...], project_low)
+    g_out = nn(att_s[...], c_s[...])
+    sums = [col_sum(project), jnp.zeros((1, 768), f32), jnp.zeros((1, 768), f32)]
+    for block in range(4):
+        rows = slice(block * 256, (block + 1) * 256)
+        d_hidden = nt(project_low[rows], wq[...])
+        out_s[rows, :] = nn(at_s[rows, :], wo[...])
+        s_s[rows, :] = d_hidden * gain
+        sums[1] += col_sum(d_hidden * x_n[rows, :])
+        sums[2] += col_sum(d_hidden)
+    if has_prev:
+        g_query = g_query + pq_ref[...]
+        g_out = g_out + po_ref[...]
+        sums = [sums[0] + pv_ref[0:1, :576], sums[1] + pv_ref[1:2, :], sums[2] + pv_ref[2:3, :]]
+    if last:
+        gq_s, go_s, tr_s = refs[20:]
+        gq_s[:, :576] = g_query
+        go_s[...] = g_out
+        tr_s[...] = jnp.zeros_like(tr_s)
+        tr_s[64:65, :] = sums[1]
+        tr_s[65:66, :] = sums[2]
+        tr_s[66:69, :] = mv_ref[1:4, :]
+        columns = jnp.transpose(tr_s[...])
+        lane = lax.broadcasted_iota(jnp.int32, (768, 128), 1)
+        target_at = col_ref[0:1, :576] + row_ref[25] * 192
+        for third in range(3):
+            hit = at_ref[:, third : third + 1] == target_at
+            column = jnp.sum(jnp.where(hit, sums[0], 0.0), axis=1, keepdims=True)
+            columns = jnp.where(lane == 69 + third, column, columns)
+        gq_s[:, 512:640] = jnp.where(lane < 64, gq_s[:, 512:640], columns)
+        for half, target in ((0, qkeep_ref), (1, qsend_ref)):
+            for zz in range(4):
+                at = zz * 2 + (row_ref[24] ^ half)
+                rows = pl.ds(pl.multiple_of(at * 96, 16), 96)
+                target[zz] = gq_s[rows, :].astype(target.dtype)
+        for half, target in ((0, okeep_ref), (1, osend_ref)):
+            rows = pl.ds(pl.multiple_of((row_ref[24] ^ half) * 96, 16), 96)
+            target[...] = go_s[rows, :].astype(target.dtype)
+    else:
+        gq_ref[...] = g_query
+        go_ref[...] = g_out
+        vec_ref[...] = jnp.zeros_like(vec_ref)
+        vec_ref[0:1, :576] = sums[0]
+        vec_ref[1:2, :] = sums[1]
+        vec_ref[2:3, :] = sums[2]
+    for piece in range(8):
+        rows = pl.ds(pl.multiple_of(row_ref[16 + piece], ROWS), ROWS)
+        target = keep_ref if piece < 4 else send_ref
+        for kind, source in ((0, out_s), (1, s_s)):
+            total = source[rows, :]
+            if has_prev:
+                total = total + partial[0, piece, kind].astype(f32)
+            target[piece % 4, kind] = total.astype(bf16)
+
+
+def attn_call(row_offsets, parts, at, weights, o_own, o_other, vecs, partial, seq, prev, tail):
+    width = vecs.shape[-1]
+    f32, bf16 = jnp.float32, jnp.bfloat16
+    part_spec = pl.BlockSpec((2, 2, 1, ROWS, width), lambda i, *_: (0, 0, at, 0, 0))
+    partial_spec = pl.BlockSpec((1, 8, 2, ROWS, width), lambda i, *_: (seq - 1, 0, 0, 0, 0))
+    extra = list(prev) if prev is not None else []
+    partials = [partial] if prev is not None else []
+    last = tail is not None
+    after = list(tail) if last else []
+    rows = 8 * ROWS
+    half = (4, 2, ROWS, width)
+    shapes = [(half, bf16), (half, bf16)]
+    if last:
+        shapes += [((4, 96, 640), bf16), ((4, 96, 640), f32), ((96, width), bf16), ((96, width), f32)]
+    else:
+        shapes += [((width, 576), f32), ((192, width), f32), ((8, width), f32)]
+    outs = [jax.ShapeDtypeStruct(shape, kind) for shape, kind in shapes]
+    return pl.pallas_call(
+        functools.partial(attn_kernel, prev is not None, last),
+        grid_spec=pltpu.PrefetchScalarGridSpec(
+            num_scalar_prefetch=1,
+            grid=(1,),
+            in_specs=[part_spec] * 4
+            + [whole(a.shape) for a in (*weights, o_own, o_other, vecs)]
+            + [partial_spec] * len(partials)
+            + [whole(a.shape) for a in extra + after],
+            out_specs=[whole(a.shape) for a in outs],
+            scratch_shapes=[
+                pltpu.VMEM((width, 576), bf16),
+                pltpu.VMEM((192, width), bf16),
+                pltpu.VMEM((rows, width), f32),
+                pltpu.VMEM((rows, width), bf16),
+                pltpu.VMEM((rows, width), bf16),
+                pltpu.VMEM((3, rows, 64), bf16),
+                pltpu.VMEM((3, rows, 64), bf16),
+                pltpu.VMEM((3, rows, 64), bf16),
+                pltpu.VMEM((3, 64, rows), bf16),
+                pltpu.VMEM((3, 64, rows), bf16),
+                pltpu.VMEM((3, rows, 64), bf16),
+                pltpu.VMEM((3, 64, rows), bf16),
+                pltpu.VMEM((rows, 64), f32),
+                pltpu.VMEM((rows, 64), f32),
+                pltpu.VMEM((rows, 192), bf16),
+                pltpu.VMEM((192, rows), bf16),
+                pltpu.VMEM((rows, 576), f32),
+                pltpu.VMEM((rows, width), f32),
+                pltpu.VMEM((rows, width), f32),
+                pltpu.VMEM((3, rows, 128), f32),
+            ]
+            + (
+                [pltpu.VMEM((width, 640), f32), pltpu.VMEM((192, width), f32), pltpu.VMEM((128, width), f32)]
+                if last
+                else []
+            ),
+        ),
+        out_shape=outs,
+        compiler_params=pltpu.CompilerParams(vmem_limit_bytes=56 << 20),
+        cost_estimate=pl.CostEstimate(
+            flops=24_000_000_000, transcendentals=0, bytes_accessed=15_000_000
+        ),
+        name="attn",
+    )(row_offsets, *parts, *weights, o_own, o_other, vecs, *partials, *extra, *after)
+
+
+def finish_kernel(half_ref, x_ref, c_ref, own_ref, other_ref, bias, *refs):
+    out_ref, grad_ref = refs[-2:]
+    f32 = jnp.float32
+
+    def write(source):
+        x = x_ref[0].astype(f32)
+        normed, inverse = normalize(x)
+        out_ref[0] = x + bias[4:5, :] + source[0].astype(f32)
+        s = source[1].astype(f32)
+        mean_s = jnp.mean(s, axis=-1, keepdims=True)
+        mean_sn = jnp.mean(s * normed, axis=-1, keepdims=True)
+        grad_ref[0] = c_ref[0] + inverse * (s - mean_s - normed * mean_sn)
+
+    @pl.when(pl.program_id(0) == 0)
+    def _():
+        write(own_ref)
+
+    @pl.when(pl.program_id(0) == 1)
+    def _():
+        write(other_ref)
+
+
+def finish_call(half, seq, x, cot, own, other, bias, done):
+    _, rows, width = x.shape
+    f32 = jnp.float32
+    seq_spec = pl.BlockSpec(
+        (1, rows, width), lambda i, at: (jnp.where(i == 0, at[0], 1 - at[0]) * 3 + seq, 0, 0)
+    )
+    before = list(done) if done is not None else []
+    return pl.pallas_call(
+        finish_kernel,
+        grid_spec=pltpu.PrefetchScalarGridSpec(
+            num_scalar_prefetch=1,
+            grid=(2,),
+            in_specs=[seq_spec, seq_spec, whole(own.shape), whole(other.shape), whole(bias.shape)]
+            + [pl.BlockSpec(memory_space=pl.ANY)] * len(before),
+            out_specs=[seq_spec, seq_spec],
+        ),
+        out_shape=[jax.ShapeDtypeStruct(x.shape, f32)] * 2,
+        input_output_aliases={6: 0, 7: 1} if before else {},
+        name="finish",
+    )(half, x, cot, own, other, bias, *before)
+
+
+def pick(value, index, axis=0):
+    return lax.dynamic_index_in_dim(value, index, axis, keepdims=False)
+
+
+def prep_kernel(at_ref, in_ref, q_ref, small_ref, own_ref, send_ref, pack_s):
+    for h in range(4):
+        parts = [in_ref[:, zy * 384 + h * 96 : zy * 384 + (h + 1) * 96] for zy in range(8)]
+        for head in range(3):
+            for kind in range(2):
+                first = kind * 768 + h * 192 + head * 64
+                parts.append(q_ref[:, first : first + 64])
+        first = 1536 + h * 192
+        parts.append(q_ref[:, first : first + 192])
+        parts.append(small_ref[...])
+        at = 0
+        for part in parts:
+            pack_s[h, :, at : at + part.shape[1]] = part
+            at += part.shape[1]
+    for core in range(2):
+        own_ref[core] = pack_s[at_ref[26] * 2 + core]
+        send_ref[core] = pack_s[(1 - at_ref[26]) * 2 + core]
+
+
+def prep_call(row_offsets, w_in, w_qkv, small):
+    half = jax.ShapeDtypeStruct((2, 24, 1408), jnp.bfloat16)
+    return pl.pallas_call(
+        prep_kernel,
+        grid_spec=pltpu.PrefetchScalarGridSpec(
+            num_scalar_prefetch=1,
+            grid=(1,),
+            in_specs=[whole(a.shape) for a in (w_in, w_qkv, small)],
+            out_specs=[whole(half.shape)] * 2,
+            scratch_shapes=[pltpu.VMEM((4, 24, 1408), jnp.bfloat16)],
+        ),
+        out_shape=[half, half],
+        name="prep",
+    )(row_offsets, w_in, w_qkv, small)
+
+
+def join_kernel(at_ref, own_ref, got_ref, far_ref, down_ref, out_ref, attn_ref, mlp_ref, four, rows_s, cols_s):
+    f32, bf16 = jnp.float32, jnp.bfloat16
+    x, c = at_ref[26], at_ref[27]
+    four[0] = own_ref[c].astype(f32)
+    four[1] = got_ref[c].astype(f32)
+    four[2] = far_ref[0].astype(f32)
+    four[3] = far_ref[1].astype(f32)
+    for source in range(4):
+        near = ((source & 1) ^ c) * 2 + ((source >> 1) ^ x)
+        rows_s[source * 24 : (source + 1) * 24, :] = four[near]
+        cols_s[source * 24 : (source + 1) * 24, :] = out_ref[:, source * 192 : (source + 1) * 192].astype(f32)
+    mlp_ref[:96, :] = rows_s[:, :768].astype(bf16)
+    mlp_ref[96:, :] = down_ref[...]
+    attn_ref[:, :640] = rows_s[:, 768:].astype(bf16)
+    attn_ref[:, 640:] = cols_s[...].astype(bf16)
+
+
+def join_call(row_offsets, own, got, far, w_down, w_out):
+    f32, bf16 = jnp.float32, jnp.bfloat16
+    outs = [jax.ShapeDtypeStruct((96, 832), bf16), jax.ShapeDtypeStruct((192, 768), bf16)]
+    return pl.pallas_call(
+        join_kernel,
+        grid_spec=pltpu.PrefetchScalarGridSpec(
+            num_scalar_prefetch=1,
+            grid=(1,),
+            in_specs=[whole(a.shape) for a in (own, got, far, w_down, w_out)],
+            out_specs=[whole(a.shape) for a in outs],
+            scratch_shapes=[
+                pltpu.VMEM((4, 24, 1408), f32), pltpu.VMEM((96, 1408), f32), pltpu.VMEM((96, 192), f32)
+            ],
+        ),
+        out_shape=outs,
+        name="join",
+    )(row_offsets, own, got, far, w_down, w_out)
+
+
+def pick_out_kernel(at_ref, one, two, three, four, own_ref, send_ref, all_s):
+    for at, source in enumerate((one, two, three, four)):
+        all_s[at] = source[:, 640:]
+    for core in range(2):
+        own_ref[core] = all_s[(at_ref[28] - at_ref[26] * 2 - core + 4) % 4]
+        send_ref[core] = all_s[(at_ref[28] - (1 - at_ref[26]) * 2 - core + 4) % 4]
+
+
+def pick_out_call(row_offsets, pieces):
+    half = jax.ShapeDtypeStruct((2, 96, 192), jnp.bfloat16)
+    return pl.pallas_call(
+        pick_out_kernel,
+        grid_spec=pltpu.PrefetchScalarGridSpec(
+            num_scalar_prefetch=1,
+            grid=(1,),
+            in_specs=[whole((96, 832))] * 4,
+            out_specs=[whole(half.shape)] * 2,
+            scratch_shapes=[pltpu.VMEM((4, 96, 192), jnp.bfloat16)],
+        ),
+        out_shape=[half, half],
+        name="pick_out",
+    )(row_offsets, *pieces)
+
+
+def join_out_kernel(at_ref, own_ref, got_ref, far_ref, out_ref, four, rows_s):
+    f32, bf16 = jnp.float32, jnp.bfloat16
+    x, c = at_ref[26], at_ref[27]
+    four[0] = own_ref[c].astype(f32)
+    four[1] = got_ref[c].astype(f32)
+    four[2] = far_ref[0].astype(f32)
+    four[3] = far_ref[1].astype(f32)
+    for source in range(4):
+        near = ((source & 1) ^ c) * 2 + ((source >> 1) ^ x)
+        for group in range(4):
+            rows_s[source * 24 : (source + 1) * 24, group * 192 : (group + 1) * 192] = four[
+                near, group * 24 : (group + 1) * 24, :
+            ]
+    out_ref[...] = rows_s[...].astype(bf16)
+
+
+def join_out_call(row_offsets, own, got, far):
+    f32, bf16 = jnp.float32, jnp.bfloat16
+    return pl.pallas_call(
+        join_out_kernel,
+        grid_spec=pltpu.PrefetchScalarGridSpec(
+            num_scalar_prefetch=1,
+            grid=(1,),
+            in_specs=[whole(a.shape) for a in (own, got, far)],
+            out_specs=whole((96, 768)),
+            scratch_shapes=[pltpu.VMEM((4, 96, 192), f32), pltpu.VMEM((96, 768), f32)],
+        ),
+        out_shape=jax.ShapeDtypeStruct((96, 768), bf16),
+        name="join_out",
+    )(row_offsets, own, got, far)
+
+
+def vector_tables():
+    row = np.arange(768)
+    at_q = np.stack([(row // 24) * 72 + third * 24 + row % 24 for third in range(3)], axis=1)
+    at_in = np.stack([(row // 24) * 96 + third * 24 + row % 24 for third in range(4)], axis=1)
+    lane = np.arange(576)
+    head, kind = lane // 128, (lane % 128) // 64
+    col_q = np.where(lane < 384, kind * 768 + head * 64 + lane % 64, 1536 + lane - 384)
+    col_in = (row // 96) * 384 + row % 96
+    cols = np.zeros((8, 768), np.int32)
+    cols[0, :576] = col_q
+    cols[1] = col_in
+    rows = np.concatenate([at_q, at_in, np.zeros((768, 1))], axis=1).astype(np.int32)
+    return rows, cols
+
+
+def vec_kernel(at_ref, *refs):
+    refs = list(refs)
+    pieces = [refs.pop(0) for _ in range(8)]
+    rows_ref, cols_ref, out_ref, all_s = refs
+    f32 = jnp.float32
+    for at, source in enumerate(pieces):
+        rows = pl.ds(pl.multiple_of(at_ref[at], 16), 96)
+        all_s[rows, :] = source[...].astype(f32)
+    flipped = jnp.transpose(all_s[...])
+    out_ref[0:4, :] = flipped[64:68]
+    out_ref[4:5, :] = flipped[68:69] + flipped[69:70]
+    for row, kinds, target, width, step in ((5, (0, 1, 2), 0, 576, 192), (6, (3, 4, 5, 6), 1, 768, 96)):
+        wanted = cols_ref[target : target + 1, :width] + at_ref[25] * step
+        total = jnp.zeros((1, width), f32)
+        for kind in kinds:
+            hit = rows_ref[:, kind : kind + 1] == wanted
+            total += col_sum(jnp.where(hit, all_s[:, 70 + kind : 71 + kind], 0.0))
+        out_ref[row : row + 1, :width] = total
+    out_ref[7:8, :] = jnp.zeros((1, 768), f32)
+    out_ref[5:6, 576:] = jnp.zeros((1, 192), f32)
+
+
+def vec_call(row_offsets, pieces, rows, cols):
+    f32 = jnp.float32
+    return pl.pallas_call(
+        vec_kernel,
+        grid_spec=pltpu.PrefetchScalarGridSpec(
+            num_scalar_prefetch=1,
+            grid=(1,),
+            in_specs=[pl.BlockSpec((96, 128), lambda i, *_: (0, 4))] * 8
+            + [whole(rows.shape), whole(cols.shape)],
+            out_specs=whole((8, 768)),
+            scratch_shapes=[pltpu.VMEM((768, 128), f32)],
+        ),
+        out_shape=jax.ShapeDtypeStruct((8, 768), f32),
+        name="vectors",
+    )(row_offsets, *pieces, rows, cols)
+
+
+def spread_q_kernel(blocks_ref, q_ref, *out_refs):
+    f32 = jnp.float32
+    total = None
+    for h in range(4):
+        block = blocks_ref[h].astype(f32)
+        for head in range(3):
+            for kind in range(2):
+                first = kind * 768 + h * 192 + head * 64
+                at = head * 128 + kind * 64
+                q_ref[:, first : first + 64] = block[:, at : at + 64]
+        first = 1536 + h * 192
+        q_ref[:, first : first + 192] = block[:, 384:576]
+        part = block[:, 576:584]
+        total = part if total is None else total + part
+    same = lax.broadcasted_iota(jnp.int32, (24, 24), 0) == lax.broadcasted_iota(jnp.int32, (24, 24), 1)
+    rows = [col_sum(jnp.where(same, total[:, t : t + 1], 0.0)) for t in range(8)]
+    for t in range(5):
+        out_refs[t][...] = rows[t]
+    out_refs[5][...] = jnp.concatenate(rows[5:], axis=1)
+
+
+def spread_q_call(blocks):
+    f32 = jnp.float32
+    shapes = [(24, 2304)] + [(1, 24)] * 5 + [(1, 72)]
+    return pl.pallas_call(
+        spread_q_kernel,
+        out_shape=[jax.ShapeDtypeStruct(shape, f32) for shape in shapes],
+        name="spread_q",
+    )(blocks)
+
+
+def spread_in_kernel(blocks_ref, in_ref):
+    for h in range(4):
+        block = blocks_ref[h].astype(jnp.float32)
+        for zy in range(8):
+            first = zy * 384 + h * 96
+            in_ref[:, first : first + 96] = block[:, zy * 96 : (zy + 1) * 96]
+
+
+def spread_in_call(blocks):
+    return pl.pallas_call(
+        spread_in_kernel,
+        out_shape=jax.ShapeDtypeStruct((24, 3072), jnp.float32),
+        name="spread_in",
+    )(blocks)
+
+
+def exchange_four(blocks, x, c):
+    blocks = blocks.reshape((2, 2) + blocks.shape[1:])
+    own = pick(blocks, x)
+    got = swap(pick(blocks, 1 - x), 2)
+    both = jnp.stack([own, got])
+    mine = pick(both, c, 1)
+    theirs = swap(pick(both, 1 - c, 1), 1)
+    mine = jnp.where(x == 0, mine, mine[::-1])
+    theirs = jnp.where(x == 0, theirs, theirs[::-1])
+    pairs = jnp.where(
+        c == 0, jnp.stack([mine, theirs], axis=1), jnp.stack([theirs, mine], axis=1)
+    )
+    return pairs.reshape((4,) + pairs.shape[2:])
+
+
+def fast(*args):
+    return fast_body(*args)
+
+
+def fast_body(
+    inputs, cotangent, ln1_gain, ln1_bias, ln2_gain, ln2_bias, w_qkv, b_qkv, w_out, b_out, w_in, b_in, w_mlp_out, b_mlp_out
+):
+    f32, bf16 = jnp.float32, jnp.bfloat16
+    z = lax.axis_index("fsdp")
+    ctx = lax.axis_index("ctx")
+    y, x, c = ctx // 4, (ctx // 2) % 2, ctx % 2
+    h = ctx % 4
+
+    zs = jnp.stack([(z - k) % 4 for k in range(4)])
+    rows_w = jnp.concatenate([(zs * 2 + y) * 96, (zs * 2 + 1 - y) * 96])
+    rows_o = jnp.stack([y * 96, (1 - y) * 96])
+    rows_p = jnp.stack([(ctx ^ piece_bits(k)) * ROWS for k in range(8)])
+    row_offsets = jnp.concatenate(
+        [rows_w, rows_o, jnp.zeros((6,), jnp.int32), rows_p, jnp.stack([y, h, x, c, z])]
+    ).astype(jnp.int32)
+
+    small = jnp.concatenate(
+        [ln1_gain, ln1_bias, ln2_gain, ln2_bias, b_out, b_mlp_out, b_qkv, b_in, jnp.zeros((51 * 24,), bf16)]
+    ).reshape(64, 24).T
+    pack_own, pack_send = prep_call(row_offsets, w_in, w_qkv, small)
+
+    def rows_of(half, first, count):
+        at = half * 3 + first
+        return jnp.stack(
+            [
+                lax.dynamic_slice_in_dim(inputs, at, count),
+                lax.dynamic_slice_in_dim(cotangent, at, count).astype(bf16),
+            ]
+        )
+
+    parts = []
+    first = 0
+    for count in CHUNKS:
+        got = swap(rows_of(1 - y, first, count), 4)
+        two = jnp.stack([rows_of(y, first, count), got])
+        side = swap(two, 2)
+        parts.append((two, side, swap(two, 1), swap(side, 1)))
+        first += count
+
+    pack_got = swap(pack_send, 2)
+    pack_far = swap(jnp.stack([pick(pack_own, 1 - c), pick(pack_got, 1 - c)]), 1)
+    attn_w, mlp_w = join_call(row_offsets, pack_own, pack_got, pack_far, w_mlp_out, w_out)
+    attn_own = [attn_w] + [shift_z(attn_w, k) for k in (1, 2, 3)]
+    mlp_own = [mlp_w] + [shift_z(mlp_w, k) for k in (1, 2, 3)]
+    attn_all = attn_own + [swap(part, 4) for part in attn_own]
+    mlp_all = mlp_own + [swap(part, 4) for part in mlp_own]
+    out_mine, out_send = pick_out_call(row_offsets, attn_own)
+    out_got = swap(out_send, 2)
+    out_far = swap(jnp.stack([pick(out_mine, 1 - c), pick(out_got, 1 - c)]), 1)
+    out_own = join_out_call(row_offsets, out_mine, out_got, out_far)
+    out_other = swap(out_own, 4)
+    at_rows, at_cols = vector_tables()
+    vecs = vec_call(row_offsets, attn_all, at_rows, at_cols)
+
+    where = [(at, inside) for at, count in enumerate(CHUNKS) for inside in range(count)]
+
+    def attention(seq, partial, prev, tail=None):
+        at, inside = where[seq]
+        return attn_call(
+            row_offsets, parts[at], inside, attn_all, out_own, out_other,
+            vecs, partial, seq, prev, tail,
+        )
+
+    def reduce_z(blocks):
+        def total(at):
+            value = pick(blocks[0], at).astype(f32)
+            for block in blocks[1:]:
+                value = value + pick(block, at).astype(f32)
+            return value
+
+        sent = [shift_z(total((z + k) % 4).astype(bf16), k) for k in (1, 2, 3)]
+        result = total(z)
+        for part in sent:
+            result = result + part.astype(f32)
+        return result
+
+    half = jnp.reshape(y, (1,)).astype(jnp.int32)
+
+    def scatter(seq, send, keep, done):
+        got = swap(send, 1)
+        side = swap((keep[2:].astype(f32) + got[2:].astype(f32)).astype(bf16), 2)
+        mine = (keep[0].astype(f32) + got[0].astype(f32) + side[0].astype(f32)).astype(bf16)
+        far = (keep[1].astype(f32) + got[1].astype(f32) + side[1].astype(f32)).astype(bf16)
+        return finish_call(half, seq, inputs, cotangent, mine, swap(far, 4), vecs, done)
+
+    first_send, first_keep, g_q, g_o, vec = attention(0, None, None)
+    prev = (g_q, g_o, vec)
+    send, keep, rest_part, g_send, g_keep, mlp_vec = mlp_call(
+        row_offsets, parts, mlp_all, vecs, cotangent, first_send, first_keep
+    )
+    g_got = swap(g_send, 4)
+    done = scatter(0, send, keep, None)
+    send, keep, g_q, g_o, vec = attention(1, rest_part, prev)
+    done = scatter(1, send, keep, done)
+    mlp_grad = reduce_z((g_keep, g_got))
+    grad_w_mlp = mlp_grad[96:192]
+    grad_b_in = mlp_grad[192, :96]
+    grad_w_in = spread_in_call(exchange_four(mlp_grad[:96].astype(bf16).reshape(4, 24, 768), x, c))
+    send, keep, q_send, q_keep, o_send, o_keep = attention(
+        2, rest_part, (g_q, g_o, vec), (mlp_vec, at_rows, at_cols)
+    )
+    done = scatter(2, send, keep, done)
+    q_grad = reduce_z((q_keep, swap(q_send, 4)))
+    spread = spread_q_call(exchange_four(q_grad.astype(bf16).reshape(4, 24, 640), x, c))
+    grad_w_qkv = spread[0]
+    one_gain, one_bias, two_gain, two_bias, grad_bias, grad_bq = [v.reshape(-1) for v in spread[1:]]
+
+    o_parts = o_keep + swap(o_send, 4).astype(f32)
+    o_blocks = exchange_four(o_parts.astype(bf16).reshape(4, 24, 768), x, c)
+    grad_w_out = reduce_z((o_blocks,))
+
+    outputs, grad_inputs = done
+    return (
+        outputs,
+        grad_inputs,
+        one_gain,
+        one_bias,
+        two_gain,
+        two_bias,
+        grad_w_qkv,
+        grad_bq,
+        grad_w_out,
+        grad_bias,
+        grad_w_in,
+        grad_b_in,
+        grad_w_mlp,
+        grad_bias,
+    )
+
+
+def fast_fits(mesh):
+    sizes = dict(mesh.shape)
+    return sizes["fsdp"] == 4 and sizes["ctx"] == 8
+
+
 def solution(mesh):
     return jax.shard_map(
-        local,
+        fast if fast_fits(mesh) else local,
         mesh=mesh,
         in_specs=(
             P("fsdp", "ctx", None),

time: 1080 us -> 416 us (0.39); the launches traced: 1060 us -> 413 us
  waiting for transfers between devices: 551 us -> 170 us
  matrix products: 170 us -> 0 us
  Pallas kernels: 0 us -> 140 us
  local copies, waits for them, and re-layouts: 158 us -> 19 us
  blocking collectives: 85.2 us -> 0 us
  other arithmetic: 81.9 us -> 18.1 us
  starting transfers between devices: 0.69 us -> 64.2 us
  between operations: 16.1 us -> 1.51 us
    reduce_scatter x6 -> x0, waiting for transfers between devices: 471 us -> none  [the longest x1 141 us: local(): lax.psum_scatter(weight_sums[10], ('fsdp', 'ctx'), scatter_dimension=0, t...]
    dot_general x52 -> x0, matrix products: 170 us -> none  [the longest x8 28.7 us: outer_rows(): lax.dot_general(left, right, (((0,), (0,)), ((), ())), preferred_element_...]
    ppermute x0 -> x54, waiting for transfers between devices: none -> 170 us  [the longest x39 120 us: swap(): return lax.ppermute(value, 'ctx', [(i, i ^ bit) for i in range(8)])]
    pallas_call x0 -> x14, Pallas kernels: none -> 140 us  [the longest x3 74.7 us: attn_call(): pl.pallas_call(functools.partial(attn_kernel, prev is not None, last), gr...]
    unnamed x2 -> x0, blocking collectives: 85.2 us -> none
    all_gather x6 -> x0, waiting for transfers between devices: 77.3 us -> none  [the longest x2 47.7 us: local(): lax.all_gather(kv_pack, 'ctx', axis=1, tiled=True)]
    ppermute x0 -> x54, starting transfers between devices: none -> 64.2 us  [the longest x39 35.6 us: swap(): return lax.ppermute(value, 'ctx', [(i, i ^ bit) for i in range(8)])]
    dynamic_update_slice x8 -> x0, local copies, waits for them, and re-layouts: 46.6 us -> none  [back_block(): lax.dynamic_update_slice_in_dim(buffer, key_value_grad, offset, 1)]
  transfers between devices with their start and end apart: 12 -> 54, of which waited for: 8 -> 28; matrix products, arithmetic and copies ran while one was open for 37% -> 6% of each run, Pallas kernels for 0% -> 11%
where the time goes in v1:
time: 416 us; the launch traced here: 413 us
  waiting for transfers between devices  170 us (41%)
  Pallas kernels  140 us (34%)
  starting transfers between devices  64.2 us (15%)
  local copies, waits for them, and re-layouts  19 us (5%)
  other arithmetic  18.1 us (4%)
    ppermute x39, waiting for transfers between devices, swap(): return lax.ppermute(value, 'ctx', [(i, i ^ bit) for i in range(8)])  120 us
    pallas_call x3, Pallas kernels, attn_call(): pl.pallas_call(functools.partial(attn_kernel, prev is not None, last), gr...  74.7 us
    ppermute x15, waiting for transfers between devices, shift_z(): return lax.ppermute(value, 'fsdp', [(i, (i + step) % 4) for i in range(4)])  49.3 us
    pallas_call x1, Pallas kernels, mlp_call(): pl.pallas_call(functools.partial(mlp_kernel, chunks), grid_spec=pltpu.Pre...  38.4 us
    ppermute x39, starting transfers between devices, swap(): return lax.ppermute(value, 'ctx', [(i, i ^ bit) for i in range(8)])  35.6 us
    ppermute x15, starting transfers between devices, shift_z(): return lax.ppermute(value, 'fsdp', [(i, (i + step) % 4) for i in range(4)])  28.6 us
    pallas_call x3, Pallas kernels, finish_call(): pl.pallas_call(finish_kernel, grid_spec=pltpu.PrefetchScalarGridSpec(num_...  8.85 us
  transfers between devices with their start and end apart: 54, of which 28 were waited for; matrix products, arithmetic and copies ran while one was open for 6% of the time, Pallas kernels for 11%

profile of v1, /device:TPU:0, one launch (start us, length us, event | category | flops | bytes accessed | tf_op | source)
XLA Modules:
  0.0 412.7 jit_solution(9394389287738914625)
XLA Ops:
  0.9 5.5 %concatenate.7 = bf16[1536]{0:T(1024)(128)(2,1)S(1)} concatenate(bf16[24]{0:T(256)(128)(2,1)} %param.18, bf16[24]{0:T(256)(128)(2,1)} %param.19, bf16[24]{0:T(256)(128)(2,1)} %param.20, bf16[24]{0:T(256)(128)(2,1)} %param.21, bf16[24]{0:T(256)(128)(2,1)} %param.25, bf16[24]{0:T(256)(128)(2,1)} %param.29, bf16[72]{0:T(256)(128)(2,1)} %param.23, bf16[96]{0:T(256)(128)(2,1)} %param.27, ...), dimensions={0} | concatenate | bytes 6144 | tf_op jit(solution)/shard_map/concatenate | solution.py:1127
  19.7 7.1 %collective-permute-done.16 = bf16[2,1,128,768]{3,2,0,1:T(8,128)(2,1)} collective-permute-done((bf16[2,1,128,768]{3,2,0,1:T(8,128)(2,1)S(1)}, bf16[2,1,128,768]{3,2,0,1:T(8,128)(2,1)}, u32[]{:S(2)}, u32[]{:S(2)}) %collective-permute-start.16) | collective-permute-done | bytes 393248 | tf_op jit(solution)/shard_map/ppermute | solution.py:390
  28.0 14.2 %collective-permute-done = bf16[2,2,128,768]{3,2,1,0:T(8,128)(2,1)S(1)} collective-permute-done((bf16[2,2,128,768]{3,2,1,0:T(8,128)(2,1)S(1)}, bf16[2,2,128,768]{3,2,1,0:T(8,128)(2,1)S(1)}, u32[]{:S(2)}, u32[]{:S(2)}) %collective-permute-start) | collective-permute-done | bytes 786464 | tf_op jit(solution)/shard_map/ppermute | solution.py:390
  51.8 5.0 %collective-permute-done.6.two.refs_1_.refs_6_ = bf16[96,832]{1,0:T(8,128)(2,1)S(1)} collective-permute-done((bf16[96,832]{1,0:T(8,128)(2,1)}, bf16[96,832]{1,0:T(8,128)(2,1)S(1)}, u32[]{:S(2)}, u32[]{:S(2)}) %collective-permute-start.6) | collective-permute-done | bytes 159776 | tf_op jit(solution)/shard_map/ppermute | solution.py:394
  59.1 10.9 %collective-permute-done.7.three.refs_2_.refs_7_ = bf16[96,832]{1,0:T(8,128)(2,1)S(1)} collective-permute-done((bf16[96,832]{1,0:T(8,128)(2,1)}, bf16[96,832]{1,0:T(8,128)(2,1)S(1)}, u32[]{:S(2)}, u32[]{:S(2)}) %collective-permute-start.7) | collective-permute-done | bytes 159776 | tf_op jit(solution)/shard_map/ppermute | solution.py:394
  80.5 3.9 collective-permute-start.22
  85.8 8.2 %collective-permute-done.21.refs_10_ = bf16[192,768]{1,0:T(8,128)(2,1)} collective-permute-done((bf16[192,768]{1,0:T(8,128)(2,1)}, bf16[192,768]{1,0:T(8,128)(2,1)}, u32[]{:S(2)}, u32[]{:S(2)}) %collective-permute-start.21) | collective-permute-done | bytes 294944 | tf_op jit(solution)/shard_map/ppermute | solution.py:394
  96.8 4.7 %collective-permute-done.10.refs_5_.refs_10_ = bf16[96,832]{1,0:T(8,128)(2,1)S(1)} collective-permute-done((bf16[96,832]{1,0:T(8,128)(2,1)}, bf16[96,832]{1,0:T(8,128)(2,1)S(1)}, u32[]{:S(2)}, u32[]{:S(2)}) %collective-permute-start.10) | collective-permute-done | bytes 159776 | tf_op jit(solution)/shard_map/ppermute | solution.py:390
  110.6 4.5 %vectors.1.refs_15_.refs_16_.bias = f32[8,768]{1,0:T(8,128)} custom-call(s32[29]{0:T(128)} %concatenate.6.at_ref.refs_0_.row_ref, bf16[96,832]{1,0:T(8,128)(2,1)} %get-tuple-element.57.one.refs_0_.refs_5_, bf16[96,832]{1,0:T(8,128)(2,1)} %copy-done.8, bf16[96,832]{1,0:T(8,128)(2,1)} %copy-done.9, bf16[96,832]{1,0:T(8,128)(2,1)} %copy-done.10, ...), custom_call_target="tpu_custom_call" | custom-call | tf_op jit(solution)/shard_map/vectors/pallas_call | solution.py:1029
  121.2 24.2 %attn.3 = (bf16[4,2,128,768]{3,2,1,0:T(8,128)(2,1)}, bf16[4,2,128,768]{3,2,1,0:T(8,128)(2,1)}, f32[768,576]{1,0:T(8,128)}, f32[192,768]{1,0:T(8,128)}, f32[8,768]{1,0:T(8,128)}) custom-call(s32[29]{0:T(128)} %concatenate.6.at_ref.refs_0_.row_ref, bf16[2,2,1,128,768]{4,3,2,1,0:T(8,128)(2,1)} %copy-done.7, ...), custom_call_target="tpu_custom_call" | custom-call | flops 24000000000 | bytes 15000000 | tf_op jit(solution)/shard_map/attn/pallas_call | solution.py:768
  147.3 38.4 %mlp.1 = (bf16[4,2,128,768]{3,2,1,0:T(8,128)(2,1)}, bf16[4,2,128,768]{3,2,1,0:T(8,128)(2,1)}, bf16[2,8,2,128,768]{4,3,2,1,0:T(8,128)(2,1)}, bf16[4,208,768]{2,1,...) custom-call(s32[29]{0:T(128)} %concatenate.6.at_ref.refs_0_.row_ref, bf16[2,2,1,128,768]{4,3,2,1,0:T(8,128)(2,1)} %copy-done.7, ...), custom_call_target="tpu_custom_call" | custom-call | flops 30000001024 | bytes 30000000 | tf_op jit(solution)/shard_map/mlp/pallas_call | solution.py:537
  185.7 25.2 %attn.4 = (bf16[4,2,128,768]{3,2,1,0:T(8,128)(2,1)}, bf16[4,2,128,768]{3,2,1,0:T(8,128)(2,1)}, f32[768,576]{1,0:T(8,128)}, f32[192,768]{1,0:T(8,128)}, f32[8,768]{1,0:T(8,128)}) custom-call(s32[29]{0:T(128)} %concatenate.6.at_ref.refs_0_.row_ref, bf16[2,2,2,128,768]{4,3,2,1,0:T(8,128)(2,1)} %copy-done.2, ...), custom_call_target="tpu_custom_call" | custom-call | flops 24000000000 | bytes 15000000 | tf_op jit(solution)/shard_map/attn/pallas_call | solution.py:768
  211.0 25.3 %attn.5 = (bf16[4,2,128,768]{3,2,1,0:T(8,128)(2,1)}, bf16[4,2,128,768]{3,2,1,0:T(8,128)(2,1)}, bf16[4,96,640]{2,1,0:T(8,128)(2,1)}, f32[4,96,640]{2,1,0:T(8,128)...) custom-call(s32[29]{0:T(128)} %concatenate.6.at_ref.refs_0_.row_ref, bf16[2,2,2,128,768]{4,3,2,1,0:T(8,128)(2,1)} %copy-done.2, ...), custom_call_target="tpu_custom_call" | custom-call | flops 24000000000 | bytes 15000000 | tf_op jit(solution)/shard_map/attn/pallas_call | solution.py:768
  237.8 4.5 %collective-permute-done.42 = bf16[96,768]{1,0:T(8,128)(2,1)S(1)} collective-permute-done((bf16[96,768]{1,0:T(8,128)(2,1)}, bf16[96,768]{1,0:T(8,128)(2,1)S(1)}, u32[]{:S(2)}, u32[]{:S(2)}) %collective-permute-start.42) | collective-permute-done | bytes 147488 | tf_op jit(solution)/shard_map/ppermute | solution.py:390
  250.5 33.9 %collective-permute-done.36 = bf16[4,96,640]{2,1,0:T(8,128)(2,1)S(1)} collective-permute-done((bf16[4,96,640]{2,1,0:T(8,128)(2,1)}, bf16[4,96,640]{2,1,0:T(8,128)(2,1)S(1)}, u32[]{:S(2)}, u32[]{:S(2)}) %collective-permute-start.36) | collective-permute-done | bytes 491552 | tf_op jit(solution)/shard_map/ppermute | solution.py:390
  284.5 5.0 %collective-permute-start.37 = (bf16[96,640]{1,0:T(8,128)(2,1)S(1)}, bf16[96,640]{1,0:T(8,128)(2,1)S(1)}, u32[]{:S(2)}, u32[]{:S(2)}) collective-permute-start(bf16[96,640]{1,0:T(8,128)(2,1)S(1)} %get-tuple-element.111), channel_id=1, source_target_pairs={{0,8},{8,16},{16,24},{24,0},{1,9},{9,17},{17,25},{25,1},{2,10},{10... | collective-permute-start | bytes 368648 | tf_op jit(solution)/shard_map/ppermute | solution.py:394
  291.9 3.2 collective-permute-done.37
  295.1 3.3 collective-permute-done.38
  299.1 3.4 collective-permute-start.46
  318.0 3.8 collective-permute-start.50
  331.8 11.4 %collective-permute-done.50 = bf16[208,768]{1,0:T(8,128)(2,1)S(1)} collective-permute-done((bf16[208,768]{1,0:T(8,128)(2,1)S(1)}, bf16[208,768]{1,0:T(8,128)(2,1)S(1)}, u32[]{:S(2)}, u32[]{:S(2)}) %collective-permute-start.50) | collective-permute-done | bytes 319520 | tf_op jit(solution)/shard_map/ppermute | solution.py:394
  347.2 30.4 %collective-permute-done.52 = bf16[2,24,768]{2,1,0:T(8,128)(2,1)S(1)} collective-permute-done((bf16[2,24,768]{2,1,0:T(8,128)(2,1)S(1)}, bf16[2,24,768]{2,1,0:T(8,128)(2,1)S(1)}, u32[]{:S(2)}, u32[]{:S(2)}) %collective-permute-start.52) | collective-permute-done | bytes 73760 | tf_op jit(solution)/shard_map/ppermute | solution.py:390
  395.6 4.7 %collective-permute-done.32.other_ref = bf16[2,128,768]{2,1,0:T(8,128)(2,1)S(1)} collective-permute-done((bf16[2,128,768]{2,1,0:T(8,128)(2,1)S(1)}, bf16[2,128,768]{2,1,0:T(8,128)(2,1)S(1)}, u32[]{:S(2)}, u32[]{:S(2)}) %collective-permute-start.32) | collective-permute-done | bytes 393248 | tf_op jit(solution)/shard_map/ppermute | solution.py:390
  404.0 4.3 %collective-permute-done.29.other_ref = bf16[2,128,768]{2,1,0:T(8,128)(2,1)S(1)} collective-permute-done((bf16[2,128,768]{2,1,0:T(8,128)(2,1)S(1)}, bf16[2,128,768]{2,1,0:T(8,128)(2,1)S(1)}, u32[]{:S(2)}, u32[]{:S(2)}) %collective-permute-start.29) | collective-permute-done | bytes 393248 | tf_op jit(solution)/shard_map/ppermute | solution.py:390
  (213 shorter events, 126.4 us)
Async XLA Ops:
  17.8 24.3 %collective-permute-start = (bf16[2,2,128,768]{3,2,1,0:T(8,128)(2,1)S(1)}, bf16[2,2,128,768]{3,2,1,0:T(8,128)(2,1)S(1)}, u32[]{:S(2)}, u32[]{:S(2)}) collective-permute-start(bf16[2,2,128,768]{3,2,1,0:T(8,128)(2,1)S(1)} %pad_maximum_fusion.1), channel_id=1, source_target_pairs={{0,4},{1,5},{2,6},{3,7},{4,0},{5,1},{6,2},{7,3},{8,12},{9,13},{10,... | collective-permute-start | bytes 2359304 | tf_op jit(solution)/shard_map/ppermute | solution.py:390
  27.9 56.6 %collective-permute-start.17 = (bf16[2,2,1,128,768]{4,3,2,1,0:T(8,128)(2,1)S(1)}, bf16[2,2,1,128,768]{4,3,2,1,0:T(8,128)(2,1)}, u32[]{:S(2)}, u32[]{:S(2)}) collective-permute-start(bf16[2,2,1,128,768]{4,3,2,1,0:T(8,128)(2,1)S(1)} %pad_maximum_fusion.2.refs_1_.refs_0_), channel_id=1, source_target_pairs={{0,2},{1,3},{2,0},{3,1},{4,6},{5,7},{6,4},{7,5},{8,10},{9,11},{10,... | collective-permute-start | bytes 2359304 | tf_op jit(solution)/shard_map/ppermute | solution.py:390
  42.3 78.4 %collective-permute-start.1 = (bf16[2,2,2,128,768]{4,3,2,1,0:T(8,128)(2,1)S(1)}, bf16[2,2,2,128,768]{4,3,2,1,0:T(8,128)(2,1)}, u32[]{:S(2)}, u32[]{:S(2)}) collective-permute-start(bf16[2,2,2,128,768]{4,3,2,1,0:T(8,128)(2,1)S(1)} %pad_maximum_fusion.refs_4_.refs_1_), channel_id=1, source_target_pairs={{0,2},{1,3},{2,0},{3,1},{4,6},{5,7},{6,4},{7,5},{8,10},{9,11},{10,... | collective-permute-start | bytes 4718600 | tf_op jit(solution)/shard_map/ppermute | solution.py:390
  49.2 20.8 %collective-permute-start.7 = (bf16[96,832]{1,0:T(8,128)(2,1)}, bf16[96,832]{1,0:T(8,128)(2,1)S(1)}, u32[]{:S(2)}, u32[]{:S(2)}) collective-permute-start(bf16[96,832]{1,0:T(8,128)(2,1)} %get-tuple-element.57.one.refs_0_.refs_5_), channel_id=1, source_target_pairs={{0,16},{8,24},{16,0},{24,8},{1,17},{9,25},{17,1},{25,9},{2,18},{10... | collective-permute-start | bytes 479240 | tf_op jit(solution)/shard_map/ppermute | solution.py:394
  51.8 32.6 %collective-permute-start.20 = (bf16[192,768]{1,0:T(8,128)(2,1)}, bf16[192,768]{1,0:T(8,128)(2,1)S(1)}, u32[]{:S(2)}, u32[]{:S(2)}) collective-permute-start(bf16[192,768]{1,0:T(8,128)(2,1)} %get-tuple-element.60.refs_8_), channel_id=1, source_target_pairs={{0,8},{8,16},{16,24},{24,0},{1,9},{9,17},{17,25},{25,1},{2,10},{10... | collective-permute-start | bytes 884744 | tf_op jit(solution)/shard_map/ppermute | solution.py:394
  84.4 35.8 %collective-permute-start.18 = (bf16[2,2,1,128,768]{4,3,2,1,0:T(8,128)(2,1)S(1)}, bf16[2,2,1,128,768]{4,3,2,1,0:T(8,128)(2,1)}, u32[]{:S(2)}, u32[]{:S(2)}) collective-permute-start(bf16[2,2,1,128,768]{4,3,2,1,0:T(8,128)(2,1)S(1)} %pad_maximum_fusion.2.refs_1_.refs_0_), channel_id=1, source_target_pairs={{0,1},{1,0},{2,3},{3,2},{4,5},{5,4},{6,7},{7,6},{8,9},{9,8},{10,11... | collective-permute-start | bytes 2359304 | tf_op jit(solution)/shard_map/ppermute | solution.py:390
  84.5 36.2 %collective-permute-start.19 = (bf16[2,2,1,128,768]{4,3,2,1,0:T(8,128)(2,1)}, bf16[2,2,1,128,768]{4,3,2,1,0:T(8,128)(2,1)}, u32[]{:S(2)}, u32[]{:S(2)}) collective-permute-start(bf16[2,2,1,128,768]{4,3,2,1,0:T(8,128)(2,1)} %collective-permute-done.17.refs_2_.refs_1_), channel_id=1, source_target_pairs={{0,1},{1,0},{2,3},{3,2},{4,5},{5,4},{6,7},{7,6},{8,9},{9,8},{10,11... | collective-permute-start | bytes 2359304 | tf_op jit(solution)/shard_map/ppermute | solution.py:390
  115.4 29.9 %collective-permute-start.24 = (bf16[192,768]{1,0:T(8,128)(2,1)S(1)}, bf16[192,768]{1,0:T(8,128)(2,1)S(1)}, u32[]{:S(2)}, u32[]{:S(2)}) collective-permute-start(bf16[192,768]{1,0:T(8,128)(2,1)S(1)} %collective-permute-done.20.refs_9_), channel_id=1, source_target_pairs={{0,4},{1,5},{2,6},{3,7},{4,0},{5,1},{6,2},{7,3},{8,12},{9,13},{10,... | collective-permute-start | bytes 884744 | tf_op jit(solution)/shard_map/ppermute | solution.py:390
  118.6 26.8 %collective-permute-start.25 = (bf16[192,768]{1,0:T(8,128)(2,1)}, bf16[192,768]{1,0:T(8,128)(2,1)S(1)}, u32[]{:S(2)}, u32[]{:S(2)}) collective-permute-start(bf16[192,768]{1,0:T(8,128)(2,1)} %collective-permute-done.21.refs_10_), channel_id=1, source_target_pairs={{0,4},{1,5},{2,6},{3,7},{4,0},{5,1},{6,2},{7,3},{8,12},{9,13},{10,... | collective-permute-start | bytes 884744 | tf_op jit(solution)/shard_map/ppermute | solution.py:390
  120.1 25.3 %collective-permute-start.26 = (bf16[192,768]{1,0:T(8,128)(2,1)}, bf16[192,768]{1,0:T(8,128)(2,1)S(1)}, u32[]{:S(2)}, u32[]{:S(2)}) collective-permute-start(bf16[192,768]{1,0:T(8,128)(2,1)} %copy-done.25), channel_id=1, source_target_pairs={{0,4},{1,5},{2,6},{3,7},{4,0},{5,1},{6,2},{7,3},{8,12},{9,13},{10,... | collective-permute-start | bytes 884744 | tf_op jit(solution)/shard_map/ppermute | solution.py:390
  120.6 24.8 %collective-permute-start.2 = (bf16[2,2,2,128,768]{4,3,2,1,0:T(8,128)(2,1)S(1)}, bf16[2,2,2,128,768]{4,3,2,1,0:T(8,128)(2,1)S(1)}, u32[]{:S(2)}, u32[]{:S(2)}) collective-permute-start(bf16[2,2,2,128,768]{4,3,2,1,0:T(8,128)(2,1)S(1)} %pad_maximum_fusion.refs_4_.refs_1_), channel_id=1, source_target_pairs={{0,1},{1,0},{2,3},{3,2},{4,5},{5,4},{6,7},{7,6},{8,9},{9,8},{10,11... | collective-permute-start | bytes 4718600 | tf_op jit(solution)/shard_map/ppermute | solution.py:390
  120.7 24.8 %collective-permute-start.3 = (bf16[2,2,2,128,768]{4,3,2,1,0:T(8,128)(2,1)}, bf16[2,2,2,128,768]{4,3,2,1,0:T(8,128)(2,1)S(1)}, u32[]{:S(2)}, u32[]{:S(2)}) collective-permute-start(bf16[2,2,2,128,768]{4,3,2,1,0:T(8,128)(2,1)} %collective-permute-done.1.refs_5_.refs_2_), channel_id=1, source_target_pairs={{0,1},{1,0},{2,3},{3,2},{4,5},{5,4},{6,7},{7,6},{8,9},{9,8},{10,11... | collective-permute-start | bytes 4718600 | tf_op jit(solution)/shard_map/ppermute | solution.py:390
  244.7 71.8 %collective-permute-start.48 = (bf16[4,208,768]{2,1,0:T(8,128)(2,1)}, bf16[4,208,768]{2,1,0:T(8,128)(2,1)}, u32[]{:S(2)}, u32[]{:S(2)}) collective-permute-start(bf16[4,208,768]{2,1,0:T(8,128)(2,1)} %get-tuple-element.95), channel_id=1, source_target_pairs={{0,4},{1,5},{2,6},{3,7},{4,0},{5,1},{6,2},{7,3},{8,12},{9,13},{10,... | collective-permute-start | bytes 3833864 | tf_op jit(solution)/shard_map/ppermute | solution.py:390
  246.2 38.1 %collective-permute-start.36 = (bf16[4,96,640]{2,1,0:T(8,128)(2,1)}, bf16[4,96,640]{2,1,0:T(8,128)(2,1)S(1)}, u32[]{:S(2)}, u32[]{:S(2)}) collective-permute-start(bf16[4,96,640]{2,1,0:T(8,128)(2,1)} %get-tuple-element.84), channel_id=1, source_target_pairs={{0,4},{1,5},{2,6},{3,7},{4,0},{5,1},{6,2},{7,3},{8,12},{9,13},{10,... | collective-permute-start | bytes 1474568 | tf_op jit(solution)/shard_map/ppermute | solution.py:390
  246.7 75.1 %collective-permute-start.33 = (bf16[4,2,128,768]{3,2,1,0:T(8,128)(2,1)}, bf16[4,2,128,768]{3,2,1,0:T(8,128)(2,1)}, u32[]{:S(2)}, u32[]{:S(2)}) collective-permute-start(bf16[4,2,128,768]{3,2,1,0:T(8,128)(2,1)} %get-tuple-element.76), channel_id=1, source_target_pairs={{0,1},{1,0},{2,3},{3,2},{4,5},{5,4},{6,7},{7,6},{8,9},{9,8},{10,11... | collective-permute-start | bytes 4718600 | tf_op jit(solution)/shard_map/ppermute | solution.py:390
  295.1 28.1 %collective-permute-start.30 = (bf16[4,2,128,768]{3,2,1,0:T(8,128)(2,1)}, bf16[4,2,128,768]{3,2,1,0:T(8,128)(2,1)}, u32[]{:S(2)}, u32[]{:S(2)}) collective-permute-start(bf16[4,2,128,768]{3,2,1,0:T(8,128)(2,1)} %get-tuple-element.74), channel_id=1, source_target_pairs={{0,1},{1,0},{2,3},{3,2},{4,5},{5,4},{6,7},{7,6},{8,9},{9,8},{10,11... | collective-permute-start | bytes 4718600 | tf_op jit(solution)/shard_map/ppermute | solution.py:390
  305.9 20.4 %collective-permute-start.27 = (bf16[4,2,128,768]{3,2,1,0:T(8,128)(2,1)}, bf16[4,2,128,768]{3,2,1,0:T(8,128)(2,1)}, u32[]{:S(2)}, u32[]{:S(2)}) collective-permute-start(bf16[4,2,128,768]{3,2,1,0:T(8,128)(2,1)} %get-tuple-element.72), channel_id=1, source_target_pairs={{0,1},{1,0},{2,3},{3,2},{4,5},{5,4},{6,7},{7,6},{8,9},{9,8},{10,11... | collective-permute-start | bytes 4718600 | tf_op jit(solution)/shard_map/ppermute | solution.py:390
  318.0 25.2 %collective-permute-start.50 = (bf16[208,768]{1,0:T(8,128)(2,1)S(1)}, bf16[208,768]{1,0:T(8,128)(2,1)S(1)}, u32[]{:S(2)}, u32[]{:S(2)}) collective-permute-start(bf16[208,768]{1,0:T(8,128)(2,1)S(1)} %get-tuple-element.106), channel_id=1, source_target_pairs={{0,16},{8,24},{16,0},{24,8},{1,17},{9,25},{17,1},{25,9},{2,18},{10... | collective-permute-start | bytes 958472 | tf_op jit(solution)/shard_map/ppermute | solution.py:394
  321.8 21.5 %collective-permute-start.51 = (bf16[208,768]{1,0:T(8,128)(2,1)S(1)}, bf16[208,768]{1,0:T(8,128)(2,1)S(1)}, u32[]{:S(2)}, u32[]{:S(2)}) collective-permute-start(bf16[208,768]{1,0:T(8,128)(2,1)S(1)} %get-tuple-element.105), channel_id=1, source_target_pairs={{0,24},{8,0},{16,8},{24,16},{1,25},{9,1},{17,9},{25,17},{2,26},{10... | collective-permute-start | bytes 958472 | tf_op jit(solution)/shard_map/ppermute | solution.py:394
  323.2 54.5 %collective-permute-start.34 = (bf16[2,2,128,768]{3,2,1,0:T(8,128)(2,1)S(1)}, bf16[2,2,128,768]{3,2,1,0:T(8,128)(2,1)S(1)}, u32[]{:S(2)}, u32[]{:S(2)}) collective-permute-start(bf16[2,2,128,768]{3,2,1,0:T(8,128)(2,1)S(1)} %add_convert_fusion), channel_id=1, source_target_pairs={{0,2},{1,3},{2,0},{3,1},{4,6},{5,7},{6,4},{7,5},{8,10},{9,11},{10,... | collective-permute-start | bytes 2359304 | tf_op jit(solution)/shard_map/ppermute | solution.py:390
  326.3 55.1 %collective-permute-start.31 = (bf16[2,2,128,768]{3,2,1,0:T(8,128)(2,1)S(1)}, bf16[2,2,128,768]{3,2,1,0:T(8,128)(2,1)S(1)}, u32[]{:S(2)}, u32[]{:S(2)}) collective-permute-start(bf16[2,2,128,768]{3,2,1,0:T(8,128)(2,1)S(1)} %add_convert_fusion.1), channel_id=1, source_target_pairs={{0,2},{1,3},{2,0},{3,1},{4,6},{5,7},{6,4},{7,5},{8,10},{9,11},{10,... | collective-permute-start | bytes 2359304 | tf_op jit(solution)/shard_map/ppermute | solution.py:390
  330.4 53.7 %collective-permute-start.28 = (bf16[2,2,128,768]{3,2,1,0:T(8,128)(2,1)S(1)}, bf16[2,2,128,768]{3,2,1,0:T(8,128)(2,1)S(1)}, u32[]{:S(2)}, u32[]{:S(2)}) collective-permute-start(bf16[2,2,128,768]{3,2,1,0:T(8,128)(2,1)S(1)} %add_convert_fusion.2), channel_id=1, source_target_pairs={{0,2},{1,3},{2,0},{3,1},{4,6},{5,7},{6,4},{7,5},{8,10},{9,11},{10,... | collective-permute-start | bytes 2359304 | tf_op jit(solution)/shard_map/ppermute | solution.py:390
  344.5 33.1 %collective-permute-start.52 = (bf16[2,24,768]{2,1,0:T(8,128)(2,1)S(1)}, bf16[2,24,768]{2,1,0:T(8,128)(2,1)S(1)}, u32[]{:S(2)}, u32[]{:S(2)}) collective-permute-start(bf16[2,24,768]{2,1,0:T(8,128)(2,1)S(1)} %get-tuple-element.120), channel_id=1, source_target_pairs={{0,2},{1,3},{2,0},{3,1},{4,6},{5,7},{6,4},{7,5},{8,10},{9,11},{10,... | collective-permute-start | bytes 221192 | tf_op jit(solution)/shard_map/ppermute | solution.py:390
  386.3 22.0 %collective-permute-start.29 = (bf16[2,128,768]{2,1,0:T(8,128)(2,1)S(1)}, bf16[2,128,768]{2,1,0:T(8,128)(2,1)S(1)}, u32[]{:S(2)}, u32[]{:S(2)}) collective-permute-start(bf16[2,128,768]{2,1,0:T(8,128)(2,1)S(1)} %get-tuple-element.102), channel_id=1, source_target_pairs={{0,4},{1,5},{2,6},{3,7},{4,0},{5,1},{6,2},{7,3},{8,12},{9,13},{10,... | collective-permute-start | bytes 1179656 | tf_op jit(solution)/shard_map/ppermute | solution.py:390
  (60 other events, 685.9 us)

commit v2 on v1

--- a/solution.py
+++ b/solution.py
@@ -428,142 +428,182 @@
 
 def mlp_kernel(chunks, row_ref, *refs):
     refs = list(refs)
-    parts = [[refs.pop(0) for _ in range(4)] for _ in chunks]
+    parts = [[refs.pop(0) for _ in range(8)] for _ in chunks]
     weights = [refs.pop(0) for _ in range(8)]
-    vecs, cot_ref, first_send, first_keep = [refs.pop(0) for _ in range(4)]
-    send_ref, keep_ref, rest_ref, gsend_ref, gkeep_ref, vec_ref = [refs.pop(0) for _ in range(6)]
-    w_in, w_down, x_s, c_s, h_s, act_s, dpre_s, part_s, g_in, g_down, seg_s = refs
+    vecs, cot_ref, first_send, first_keep, first_norm = [refs.pop(0) for _ in range(5)]
+    send_ref, keep_ref, rest_ref, norm_ref, gsend_ref, gkeep_ref, vec_ref = [refs.pop(0) for _ in range(7)]
+    w_in, w_down, h_s, c_s, act_s, dpre_s, x_n, first_s, part_s, g_in, g_down, seg_s, w_sem, x_sem, p_sem, o_sem = refs
     f32, bf16 = jnp.float32, jnp.bfloat16
-    step = pl.program_id(0)
     gain, shift, bias = vecs[2:3, :], vecs[3:4, :], vecs[6:7, :]
-
-    @pl.when(step == 0)
-    def _():
-        for at, source in enumerate(weights):
-            rows = pl.ds(pl.multiple_of(row_ref[at], 16), 96)
-            w_in[rows, :] = source[:96, :]
-            w_down[rows, :] = source[96:, :]
-        vec_ref[...] = jnp.zeros_like(vec_ref)
-
-    first = 0
-    for at, count in enumerate(chunks):
-        @pl.when((step >= first) & (step < first + count))
-        def _(at=at):
-            for piece in range(8):
-                source = parts[at][piece // 2]
-                rows = slice(piece * ROWS, (piece + 1) * ROWS)
-                x_s[rows, :] = source[piece % 2, 0, 0]
-                c_s[rows, :] = source[piece % 2, 1, 0]
-
-        first += count
-
-    vec_ref[3:4, :] += col_sum(cot_ref[0]) + col_sum(cot_ref[1])
-    for block in range(4):
-        rows = slice(block * 256, (block + 1) * 256)
-        normed, _ = normalize(x_s[rows, :].astype(f32))
-        hidden = (normed * gain + shift).astype(bf16)
-        h_s[rows, :] = hidden
-        pre = nn(hidden, w_in[...]) + bias
-        cdf = 0.5 * (1.0 + lax.erf(pre * 0.7071067811865476))
-        density = jnp.exp(-0.5 * pre * pre) * 0.3989422804014327
-        act = (pre * cdf).astype(bf16)
-        act_s[rows, :] = act
-        cot = c_s[rows, :]
-        d_pre = nt(cot, w_down[...]) * (cdf + pre * density)
-        d_low = d_pre.astype(bf16)
-        dpre_s[rows, :] = d_low
-        out = nn(act, w_down[...])
-        d_hidden = nt(d_low, w_in[...])
-        vec_ref[0:1, :] += col_sum(d_pre)
-        vec_ref[1:2, :] += col_sum(d_hidden * normed)
-        vec_ref[2:3, :] += col_sum(d_hidden)
-        for kind, value in ((0, out), (1, d_hidden * gain)):
-            for half in range(2):
-                part_s[block * 2 + half, kind] = value[half * ROWS : (half + 1) * ROWS].astype(bf16)
-
-    @pl.when(step == 0)
-    def _():
-        g_in[...] = tn(h_s[...], dpre_s[...])
-        g_down[...] = tn(act_s[...], c_s[...])
-        for target, source, first in ((keep_ref, first_keep, 0), (send_ref, first_send, 4)):
-            total = source[...].astype(f32) + part_s[first : first + 4].astype(f32)
-            target[...] = total.astype(bf16)
-
-    @pl.when(step > 0)
-    def _():
-        g_in[...] += tn(h_s[...], dpre_s[...])
-        g_down[...] += tn(act_s[...], c_s[...])
-        rest_ref[0] = part_s[...]
-
-    @pl.when(step == sum(chunks) - 1)
-    def _():
-        for at in range(8):
-            seg_s[at, :, :96] = jnp.broadcast_to(vec_ref[0:1, at * 96 : (at + 1) * 96], (16, 96))
-        for half, target in ((0, gkeep_ref), (1, gsend_ref)):
-            for zz in range(4):
-                at = zz * 2 + (row_ref[24] ^ half)
-                rows = pl.ds(pl.multiple_of(at * 96, 16), 96)
-                target[zz, :96, :] = g_in[rows, :].astype(target.dtype)
-                target[zz, 96:192, :] = g_down[rows, :].astype(target.dtype)
-                target[zz, 192:, :] = jnp.zeros((16, 768), target.dtype)
-                target[zz, 192:, :96] = seg_s[at, :, :96].astype(target.dtype)
+    where = [(at, inside) for at, count in enumerate(chunks) for inside in range(count)]
+    total = len(where)
+
+    weight_copies = []
+    for at, source in enumerate(weights):
+        rows = pl.ds(pl.multiple_of(row_ref[at], 16), 96)
+        for kind, target in ((0, w_in), (1, w_down)):
+            weight_copies.append(
+                pltpu.make_async_copy(
+                    source.at[pl.ds(kind * 96, 96)], target.at[rows], w_sem.at[at * 2 + kind]
+                )
+            )
+    part_copies = []
+    for seq, (at, inside) in enumerate(where):
+        for piece in range(8):
+            rows = pl.ds((seq * 8 + piece) * ROWS, ROWS)
+            sem = x_sem.at[(seq * 8 + piece) * 2]
+            if seq == 0:
+                source_rows = pl.ds(pl.multiple_of(row_ref[16 + piece], ROWS), ROWS)
+                part_copies.append(pltpu.make_async_copy(first_norm.at[source_rows], x_n.at[rows], sem))
+            else:
+                part_copies.append(
+                    pltpu.make_async_copy(parts[at][piece].at[0, inside], h_s.at[rows], sem)
+                )
+            part_copies.append(
+                pltpu.make_async_copy(
+                    parts[at][piece].at[1, inside], c_s.at[rows], x_sem.at[(seq * 8 + piece) * 2 + 1]
+                )
+            )
+    norm_copies = [
+        pltpu.make_async_copy(x_n.at[pl.ds(seq * 1024, 1024)], norm_ref.at[seq - 1], o_sem.at[total + seq])
+        for seq in range(1, total)
+    ]
+    first_copies = [
+        pltpu.make_async_copy(first_keep, first_s.at[pl.ds(0, 4)], p_sem.at[0]),
+        pltpu.make_async_copy(first_send, first_s.at[pl.ds(4, 4)], p_sem.at[1]),
+    ]
+    out_copies = [
+        pltpu.make_async_copy(part_s.at[0, pl.ds(0, 4)], keep_ref, o_sem.at[0]),
+        pltpu.make_async_copy(part_s.at[0, pl.ds(4, 4)], send_ref, o_sem.at[1]),
+    ] + [
+        pltpu.make_async_copy(part_s.at[seq % 2], rest_ref.at[seq - 1], o_sem.at[seq + 1])
+        for seq in range(1, total)
+    ]
+    for copy in part_copies[:16] + weight_copies + first_copies + part_copies[16:]:
+        copy.start()
+    vec_ref[...] = jnp.zeros_like(vec_ref)
+    for seq in range(2 * total):
+        vec_ref[3:4, :] += col_sum(cot_ref[seq])
+
+    def norm_rows(first):
+        for at in range(0, 256, 16):
+            rows = slice(first + at, first + at + 16)
+            normed, _ = normalize(h_s[rows, :].astype(f32))
+            x_n[rows, :] = normed
+            h_s[rows, :] = (normed * gain + shift).astype(bf16)
+
+    for seq in range(total):
+        rows = slice(seq * 1024, (seq + 1) * 1024)
+        if seq == 0:
+            for copy in part_copies[:16]:
+                copy.wait()
+            h_s[rows, :] = (x_n[rows, :] * gain + shift).astype(bf16)
+            for copy in weight_copies:
+                copy.wait()
+        for cols in (slice(0, 512), slice(512, 768)):
+            pre = nn(h_s[rows, :], w_in[:, cols]) + bias[:, cols]
+            d_act = nt(c_s[rows, :], w_down[cols, :])
+            cdf = 0.5 * (1.0 + lax.erf(pre * 0.7071067811865476))
+            density = jnp.exp(-0.5 * pre * pre) * 0.3989422804014327
+            act_s[rows, cols] = (pre * cdf).astype(bf16)
+            d_pre = d_act * (cdf + pre * density)
+            dpre_s[rows, cols] = d_pre.astype(bf16)
+            vec_ref[0:1, cols] += col_sum(d_pre)
+        if seq + 1 < total:
+            for copy in part_copies[seq * 16 + 16 : seq * 16 + 32]:
+                copy.wait()
+        if seq == 0:
+            for copy in first_copies:
+                copy.wait()
+        if seq == 2:
+            out_copies[0].wait()
+            out_copies[1].wait()
+        for block in range(4):
+            part_rows = slice(seq * 1024 + block * 256, seq * 1024 + (block + 1) * 256)
+            out = nn(act_s[part_rows, :], w_down[...])
+            d_hidden = nt(dpre_s[part_rows, :], w_in[...])
+            if seq + 1 < total:
+                norm_rows((seq + 1) * 1024 + block * 256)
+            vec_ref[1:2, :] += col_sum(d_hidden * x_n[part_rows, :])
+            vec_ref[2:3, :] += col_sum(d_hidden)
+            for kind, value in ((0, out), (1, d_hidden * gain)):
+                for half in range(2):
+                    piece = block * 2 + half
+                    part = value[half * ROWS : (half + 1) * ROWS]
+                    if seq == 0:
+                        part = part + first_s[piece, kind].astype(f32)
+                    part_s[seq % 2, piece, kind] = part.astype(bf16)
+        if seq + 1 < total:
+            norm_copies[seq].start()
+        if seq == 0:
+            out_copies[0].start()
+            out_copies[1].start()
+        else:
+            out_copies[seq + 1].start()
+
+    g_in[...] = tn(h_s[...], dpre_s[...])
+    g_down[...] = tn(act_s[...], c_s[...])
+    for at in range(8):
+        seg_s[at, :, :96] = jnp.broadcast_to(vec_ref[0:1, at * 96 : (at + 1) * 96], (16, 96))
+    for half, target in ((0, gkeep_ref), (1, gsend_ref)):
+        for zz in range(4):
+            at = zz * 2 + (row_ref[24] ^ half)
+            rows = pl.ds(pl.multiple_of(at * 96, 16), 96)
+            target[zz, :96, :] = g_in[rows, :].astype(target.dtype)
+            target[zz, 96:192, :] = g_down[rows, :].astype(target.dtype)
+            target[zz, 192:, :] = jnp.zeros((16, 768), target.dtype)
+            target[zz, 192:, :96] = seg_s[at, :, :96].astype(target.dtype)
+    for copy in out_copies[2:] + norm_copies:
+        copy.wait()
 
 
 def whole(shape):
     return pl.BlockSpec(shape, lambda *_: (0,) * len(shape))
 
 
-def mlp_call(row_offsets, parts, weights, vecs, cot, first_send, first_keep):
-    chunks = tuple(part[0].shape[2] for part in parts)
+def mlp_call(row_offsets, parts, weights, vecs, cot, first_send, first_keep, first_norm):
+    chunks = tuple(part[0].shape[1] for part in parts)
     total = sum(chunks)
     width = vecs.shape[-1]
     f32, bf16 = jnp.float32, jnp.bfloat16
 
-    def part_spec(first, count):
-        return pl.BlockSpec(
-            (2, 2, 1, ROWS, width),
-            lambda i, *_: (0, 0, jnp.clip(i - first, 0, count - 1), 0, 0),
-        )
-
-    specs, first = [], 0
-    for count in chunks:
-        specs += [part_spec(first, count)] * 4
-        first += count
-    rest_spec = pl.BlockSpec(
-        (1, 8, 2, ROWS, width), lambda i, *_: (jnp.maximum(i - 1, 0), 0, 0, 0, 0)
-    )
+    anywhere = pl.BlockSpec(memory_space=pl.ANY)
+    dma = pltpu.SemaphoreType.DMA
+    rows = total * 8 * ROWS
     half = (4, 2, ROWS, width)
     grads = (4, 208, width)
     return pl.pallas_call(
         functools.partial(mlp_kernel, chunks),
         grid_spec=pltpu.PrefetchScalarGridSpec(
             num_scalar_prefetch=1,
-            grid=(total,),
-            in_specs=specs
-            + [whole(a.shape) for a in weights]
-            + [whole(vecs.shape), pl.BlockSpec((2, ROWS, width), lambda i, *_: (i, 0, 0))]
-            + [whole(half), whole(half)],
-            out_specs=[whole(half), whole(half), rest_spec, whole(grads), whole(grads), whole((8, width))],
+            grid=(1,),
+            in_specs=[anywhere] * (8 * len(parts) + 8)
+            + [whole(vecs.shape), whole(cot.shape)]
+            + [anywhere] * 3,
+            out_specs=[anywhere] * 4 + [whole(grads), whole(grads), whole((8, width))],
             scratch_shapes=[pltpu.VMEM((width, width), bf16)] * 2
-            + [pltpu.VMEM((8 * ROWS, width), bf16)] * 5
-            + [pltpu.VMEM((8, 2, ROWS, width), bf16)]
+            + [pltpu.VMEM((rows, width), bf16)] * 4
+            + [pltpu.VMEM((rows, width), f32)]
+            + [pltpu.VMEM((8, 2, ROWS, width), bf16), pltpu.VMEM((2, 8, 2, ROWS, width), bf16)]
             + [pltpu.VMEM((width, width), f32)] * 2
-            + [pltpu.VMEM((8, 16, 128), f32)],
+            + [pltpu.VMEM((8, 16, 128), f32)]
+            + [dma((16,)), dma((total * 16,)), dma((2,)), dma((2 * total,))],
         ),
         out_shape=[
             jax.ShapeDtypeStruct(half, bf16),
             jax.ShapeDtypeStruct(half, bf16),
             jax.ShapeDtypeStruct((total - 1, 8, 2, ROWS, width), bf16),
+            jax.ShapeDtypeStruct((total - 1, 8 * ROWS, width), f32),
             jax.ShapeDtypeStruct(grads, bf16),
             jax.ShapeDtypeStruct(grads, f32),
             jax.ShapeDtypeStruct((8, width), f32),
         ],
-        compiler_params=pltpu.CompilerParams(vmem_limit_bytes=56 << 20),
+        compiler_params=pltpu.CompilerParams(vmem_limit_bytes=58 << 20),
         cost_estimate=pl.CostEstimate(
             flops=30_000_000_000, transcendentals=0, bytes_accessed=30_000_000
         ),
         name="mlp",
-    )(row_offsets, *[a for part in parts for a in part], *weights, vecs, cot, first_send, first_keep)
+    )(row_offsets, *[a for part in parts for a in part], *weights, vecs, cot, first_send, first_keep, first_norm)
 
 
 def rotary_tables():
@@ -581,26 +621,81 @@
     return cos_fine, sin_fine, cos_coarse, sin_coarse, first, second
 
 
-def attn_kernel(has_prev, last, *refs):
+def attn_kernel(has_prev, last, at_seq, inside, row_ref, *refs):
     refs = list(refs)
-    row_ref = refs.pop(0)
-    parts = [refs.pop(0) for _ in range(4)]
+    parts = [refs.pop(0) for _ in range(8)]
     weights = [refs.pop(0) for _ in range(8)]
-    o_own, o_other = [refs.pop(0) for _ in range(2)]
-    vecs = refs.pop(0)
+    o_own, o_other, vecs = [refs.pop(0) for _ in range(3)]
     if has_prev:
-        partial = refs.pop(0)
-        pq_ref, po_ref, pv_ref = [refs.pop(0) for _ in range(3)]
+        partial, norm_ref, pq_ref, po_ref, pv_ref = [refs.pop(0) for _ in range(5)]
     if last:
         mv_ref, at_ref, col_ref = [refs.pop(0) for _ in range(3)]
         send_ref, keep_ref, qsend_ref, qkeep_ref, osend_ref, okeep_ref = [refs.pop(0) for _ in range(6)]
     else:
         send_ref, keep_ref, gq_ref, go_ref, vec_ref = [refs.pop(0) for _ in range(5)]
-    wq, wo, x_n, h_s, c_s, q_s, k_s, v_s, kt_s, vt_s, ga_s, gat_s, dk_s, dv_s, at_s, att_s, dp_s, out_s, s_s, tab = refs[:20]
+    if not has_prev:
+        norm_out_ref = refs.pop(0)
+    wq, wo, x_s, c_s, x_n, h_s = [refs.pop(0) for _ in range(6)]
+    q_s, k_s, v_s, g_s, kt_s, vt_s, gt_s = [refs.pop(0) for _ in range(7)]
+    dq_s, dk_s, dv_s, at_s, att_s, dp_s, res_s, tab = [refs.pop(0) for _ in range(8)]
+    w_sem, x_sem, r_sem = [refs.pop(0) for _ in range(3)]
+    if has_prev:
+        pp_s, pq_s, po_s, p_sem = [refs.pop(0) for _ in range(4)]
     f32, bf16 = jnp.float32, jnp.bfloat16
     seq = 8 * ROWS
-    gain, shift, bias = vecs[0:1, :], vecs[1:2, :], vecs[5:6, :576]
-
+    blocks = seq // BLOCK
+    gain, shift, bias = vecs[0:1, :], vecs[1:2, :], vecs[5:6, :640]
+
+    def place(piece):
+        return pl.ds(pl.multiple_of(row_ref[16 + piece], ROWS), ROWS)
+
+    weight_copies = [
+        pltpu.make_async_copy(
+            source.at[:, pl.ds(0, 640)],
+            wq.at[pl.ds(pl.multiple_of(row_ref[at], 16), 96)],
+            w_sem.at[at],
+        )
+        for at, source in enumerate(weights)
+    ]
+    out_weight_copies = [
+        pltpu.make_async_copy(
+            source, wo.at[pl.ds(pl.multiple_of(row_ref[8 + at], 16), 96)], w_sem.at[8 + at]
+        )
+        for at, source in enumerate((o_own, o_other))
+    ]
+    part_copies = [
+        [
+            pltpu.make_async_copy(
+                parts[piece].at[kind, inside], target.at[place(piece)], x_sem.at[kind * 8 + piece]
+            )
+            for piece in range(8)
+        ]
+        for kind, target in (((1, c_s),) if has_prev else ((0, x_s), (1, c_s)))
+    ]
+    if has_prev:
+        norm_part_copies = [
+            pltpu.make_async_copy(
+                norm_ref.at[at_seq - 1, pl.ds(piece * ROWS, ROWS)], x_n.at[place(piece)], x_sem.at[piece]
+            )
+            for piece in range(8)
+        ]
+        part_copies.insert(0, norm_part_copies)
+    for copy in part_copies[0] + weight_copies + part_copies[1] + out_weight_copies:
+        copy.start()
+    if has_prev:
+        prev_copies = [
+            pltpu.make_async_copy(
+                partial.at[at_seq - 1, piece, kind], pp_s.at[kind, place(piece)], p_sem.at[kind * 8 + piece]
+            )
+            for piece in range(8)
+            for kind in range(2)
+        ]
+        prev_copies.append(pltpu.make_async_copy(pq_ref, pq_s, p_sem.at[16]))
+        prev_copies.append(pltpu.make_async_copy(po_ref, po_s, p_sem.at[17]))
+        for copy in prev_copies:
+            copy.start()
+
+    wo[192:, :] = jnp.zeros((64, 768), bf16)
     cos_f, sin_f, cos_c, sin_c, first, second = rotary_tables()
     for at in range(seq // 32):
         rows = slice(at * 32, (at + 1) * 32)
@@ -610,119 +705,181 @@
         tab[1, rows, :] = jnp.where(first, -sine, 0.0)
         tab[2, rows, :] = jnp.where(second, sine, 0.0)
 
-    for at, source in enumerate(weights):
-        rows = pl.ds(pl.multiple_of(row_ref[at], 16), 96)
-        wq[rows, :] = source[:, :576]
-    for other, source in ((0, o_own), (1, o_other)):
-        rows = pl.ds(pl.multiple_of(row_ref[8 + other], 16), 96)
-        wo[rows, :] = source[...]
-
-    for piece in range(8):
-        source = parts[piece // 2]
-        rows = pl.ds(pl.multiple_of(row_ref[16 + piece], ROWS), ROWS)
-        normed, _ = normalize(source[piece % 2, 0, 0].astype(f32))
-        x_n[rows, :] = normed
-        h_s[rows, :] = (normed * gain + shift).astype(bf16)
-        c_s[rows, :] = source[piece % 2, 1, 0]
-
-    for block in range(4):
+    lane = lax.broadcasted_iota(jnp.int32, (256, 128), 1)
+    left = lane < 64
+
+    def heads_of(block, project, grad):
         rows = slice(block * 256, (block + 1) * 256)
-        project = nn(h_s[rows, :], wq[...]) + bias
         cosine, low, high = tab[0, rows, :], tab[1, rows, :], tab[2, rows, :]
-        grad_t = nt(wo[...], c_s[rows, :])
         for head in range(3):
             pair = project[:, head * 128 : (head + 1) * 128]
             pair = pair * cosine + pltpu.roll(pair, 120, 1) * low + pltpu.roll(pair, 8, 1) * high
-            q_s[head, rows, :] = pair[:, :64].astype(bf16)
-            key = pltpu.roll(pair, 64, 1)[:, :64]
-            k_s[head, rows, :] = key.astype(bf16)
-            kt_s[head, :, rows] = jnp.transpose(key).astype(bf16)
-            value = project[:, 384 + head * 64 : 384 + (head + 1) * 64]
-            v_s[head, rows, :] = value.astype(bf16)
-            vt_s[head, :, rows] = jnp.transpose(value).astype(bf16)
-            part = grad_t[head * 64 : (head + 1) * 64]
-            gat_s[head, :, rows] = part.astype(bf16)
-            ga_s[head, rows, :] = jnp.transpose(part).astype(bf16)
-
-    key_at = lax.broadcasted_iota(jnp.int32, (BLOCK, BLOCK), 0)
-    query_at = lax.broadcasted_iota(jnp.int32, (BLOCK, BLOCK), 1)
-    allowed = key_at <= query_at
+            k_s[head, rows, :] = jnp.where(left, 0.0, pair).astype(bf16)
+            q_s[head, rows, :] = jnp.where(left, 0.0, pltpu.roll(pair, 64, 1)).astype(bf16)
+            kt_s[head, :, rows] = jnp.transpose(pair)[64:].astype(bf16)
+        v_pair, v_last = project[:, 384:512], jnp.where(left, project[:, 512:640], 0.0)
+        vt_s[:128, rows] = jnp.transpose(v_pair).astype(bf16)
+        vt_s[128:, rows] = jnp.transpose(v_last)[:64].astype(bf16)
+        for target, pair_value, last_value in ((v_s, v_pair, v_last), (g_s, grad[:, :128], grad[:, 128:])):
+            target[0, rows, :] = jnp.where(left, pair_value, 0.0).astype(bf16)
+            target[1, rows, :] = jnp.where(left, 0.0, pair_value).astype(bf16)
+            target[2, rows, :] = last_value.astype(bf16)
+
+    for copy in part_copies[0] + weight_copies + part_copies[1] + out_weight_copies:
+        copy.wait()
+    for block in (1, 3):
+        wide = slice((block - 1) * 256, (block + 1) * 256)
+        if has_prev:
+            h_s[wide, :] = (x_n[wide, :] * gain + shift).astype(bf16)
+        else:
+            for part in range(32):
+                rows = slice((block - 1) * 256 + part * 16, (block - 1) * 256 + (part + 1) * 16)
+                normed, _ = normalize(x_s[rows, :].astype(f32))
+                x_n[rows, :] = normed
+                h_s[rows, :] = (normed * gain + shift).astype(bf16)
+        project_wide = nn(h_s[wide, :], wq[...]) + bias
+        grad_wide = nt(c_s[wide, :], wo[...])
+        gt_s[:, wide] = nt(wo[:192, :], c_s[wide, :]).astype(bf16)
+        for half in range(2):
+            heads_of(block - 1 + half, project_wide[half * 256 : half * 256 + 256], grad_wide[half * 256 : half * 256 + 256])
+
+    allowed = lax.broadcasted_iota(jnp.int32, (BLOCK, BLOCK), 0) <= lax.broadcasted_iota(
+        jnp.int32, (BLOCK, BLOCK), 1
+    )
+
+    def rows_of(block):
+        return slice(block * BLOCK, (block + 1) * BLOCK)
+
+    def scores_of(head, block):
+        query, grad = q_s[head, rows_of(block), :], g_s[head, rows_of(block), :]
+        upto = (block + 1) * BLOCK
+        scores = nt(k_s[head, :upto, :], query)
+        scores = [scores[rows_of(at)] for at in range(block + 1)]
+        scores[block] = jnp.where(allowed, scores[block], -1e30)
+        d_prob = nt(v_s[head, :upto, :], grad)
+        return scores, [d_prob[rows_of(at)] for at in range(block + 1)]
+
+    def softmax_of(scores):
+        top = jnp.max(scores[0], axis=0, keepdims=True)
+        for part in scores[1:]:
+            top = jnp.maximum(top, jnp.max(part, axis=0, keepdims=True))
+        probs = [jnp.exp(part - top) for part in scores]
+        total = col_sum(probs[0])
+        for part in probs[1:]:
+            total = total + col_sum(part)
+        scale = 1.0 / total
+        probs = [part * scale for part in probs]
+        return probs, [part.astype(bf16) for part in probs]
+
+    def values_of(head, block, probs, lows, d_prob):
+        rows, upto = rows_of(block), (block + 1) * BLOCK
+        low = jnp.concatenate(lows, axis=0) if block else lows[0]
+        att_t = nn(vt_s[head * 64 : (head + 1) * 64, :upto], low)
+        att_low = att_t.astype(bf16)
+        att_s[head * 64 : (head + 1) * 64, rows] = att_low
+        d_value = nn(low, g_s[head, rows, :])
+        into = head // 2
+        keep = slice(0, upto if head == 1 else upto - BLOCK)
+        if keep.stop:
+            dv_s[into, keep, :] += d_value[keep]
+        if head != 1:
+            dv_s[into, rows, :] = d_value[upto - BLOCK :]
+        delta = col_sum(gt_s[head * 64 : (head + 1) * 64, rows].astype(f32) * att_low.astype(f32))
+        return [(p * (d - delta)).astype(bf16) for p, d in zip(probs, d_prob)]
+
+    def grads_of(head, block, d_scores):
+        rows, upto = rows_of(block), (block + 1) * BLOCK
+        d_score = jnp.concatenate(d_scores, axis=0) if block else d_scores[0]
+        d_key = nn(d_score, q_s[head, rows, :])
+        if block:
+            dk_s[head, : upto - BLOCK, :] += d_key[: upto - BLOCK]
+        dk_s[head, rows, :] = d_key[upto - BLOCK :]
+        dq_s[head, rows, :64] = jnp.transpose(nn(kt_s[head, :, :upto], d_score))
+
+    order = [(head, block) for block in range(blocks) for head in range(3)]
+    ahead = scores_of(*order[0])
+    waiting = None
+    for at, (head, block) in enumerate(order):
+        scores, d_prob = ahead
+        if at + 1 < len(order):
+            ahead = scores_of(*order[at + 1])
+        probs, lows = softmax_of(scores)
+        if waiting is not None:
+            grads_of(*waiting)
+        waiting = (head, block, values_of(head, block, probs, lows, d_prob))
+    grads_of(*waiting)
+
+    project_sums = []
     for head in range(3):
-        for block in range(seq // BLOCK):
-            rows = slice(block * BLOCK, (block + 1) * BLOCK)
-            upto = (block + 1) * BLOCK
-            query = q_s[head, rows, :]
-            grad = ga_s[head, rows, :]
-            diag = jnp.where(allowed, nt(k_s[head, rows, :], query), -1e30)
-            if block:
-                scores = jnp.concatenate([nt(k_s[head, : upto - BLOCK, :], query), diag], axis=0)
-            else:
-                scores = diag
-            top = jnp.max(scores, axis=0, keepdims=True)
-            prob = jnp.exp(scores - top)
-            prob = prob * (1.0 / jnp.sum(prob, axis=0, keepdims=True))
-            low_prob = prob.astype(bf16)
-            att_t = nn(vt_s[head, :, :upto], low_prob)
-            att_low = att_t.astype(bf16)
-            att_s[head * 64 : (head + 1) * 64, rows] = att_low
-            at_s[rows, head * 64 : (head + 1) * 64] = jnp.transpose(att_t).astype(bf16)
-            delta = jnp.sum(
-                gat_s[head, :, rows].astype(f32) * att_low.astype(f32), axis=0, keepdims=True
-            )
-            d_prob = nt(v_s[head, :upto, :], grad)
-            d_score = (prob * (d_prob - delta)).astype(bf16)
-            d_value = nn(low_prob, grad)
-            d_key = nn(d_score, query)
-            if block:
-                keep = slice(0, upto - BLOCK)
-                dv_s[keep, :] += d_value[: upto - BLOCK]
-                dk_s[keep, :] += d_key[: upto - BLOCK]
-            dv_s[rows, :] = d_value[upto - BLOCK :]
-            dk_s[rows, :] = d_key[upto - BLOCK :]
-            d_query = jnp.transpose(nn(kt_s[head, :, :upto], d_score))
-            dp_s[rows, head * 128 : head * 128 + 64] = d_query
+        total = jnp.zeros((1, 128), f32)
         for block in range(4):
             rows = slice(block * 256, (block + 1) * 256)
-            pair = jnp.concatenate(
-                [dp_s[rows, head * 128 : head * 128 + 64], dk_s[rows, :]], axis=1
-            )
+            pair = jnp.concatenate([dq_s[head, rows, :64], dk_s[head, rows, 64:]], axis=1)
             cosine, low, high = tab[0, rows, :], tab[1, rows, :], tab[2, rows, :]
             pair = pair * cosine - pltpu.roll(pair, 120, 1) * low - pltpu.roll(pair, 8, 1) * high
-            dp_s[rows, head * 128 : (head + 1) * 128] = pair
-            dp_s[rows, 384 + head * 64 : 384 + (head + 1) * 64] = dv_s[rows, :]
-
-    project = dp_s[...]
-    project_low = project.astype(bf16)
-    g_query = tn(h_s[...], project_low)
-    g_out = nn(att_s[...], c_s[...])
-    sums = [col_sum(project), jnp.zeros((1, 768), f32), jnp.zeros((1, 768), f32)]
+            total = total + col_sum(pair)
+            dp_s[rows, head * 128 : (head + 1) * 128] = pair.astype(bf16)
+        project_sums.append(total)
+    for into in range(2):
+        dp_s[:, 384 + into * 128 : 512 + into * 128] = dv_s[into].astype(bf16)
+        project_sums.append(col_sum(dv_s[into]))
+    if has_prev:
+        for copy in prev_copies:
+            copy.wait()
     for block in range(4):
         rows = slice(block * 256, (block + 1) * 256)
-        d_hidden = nt(project_low[rows], wq[...])
-        out_s[rows, :] = nn(at_s[rows, :], wo[...])
-        s_s[rows, :] = d_hidden * gain
-        sums[1] += col_sum(d_hidden * x_n[rows, :])
-        sums[2] += col_sum(d_hidden)
+        at_s[rows, :128] = jnp.transpose(att_s[:128, rows].astype(f32)).astype(bf16)
+        at_s[rows, 128:] = jnp.concatenate(
+            [jnp.transpose(att_s[128:, rows].astype(f32)), jnp.zeros((256, 64), f32)], axis=1
+        ).astype(bf16)
+    out = nn(at_s[...], wo[...])
+    d_hidden = nt(dp_s[...], wq[...])
+    s = d_hidden * gain
     if has_prev:
-        g_query = g_query + pq_ref[...]
-        g_out = g_out + po_ref[...]
-        sums = [sums[0] + pv_ref[0:1, :576], sums[1] + pv_ref[1:2, :], sums[2] + pv_ref[2:3, :]]
+        out = out + pp_s[0].astype(f32)
+        s = s + pp_s[1].astype(f32)
+    res_s[0] = out.astype(bf16)
+    res_s[1] = s.astype(bf16)
+    sums = [
+        jnp.concatenate(project_sums, axis=1),
+        col_sum(d_hidden * x_n[...]),
+        col_sum(d_hidden),
+    ]
+    result_copies = [
+        pltpu.make_async_copy(
+            res_s.at[kind, place(piece)],
+            (keep_ref if piece < 4 else send_ref).at[piece % 4, kind],
+            r_sem.at[piece * 2 + kind],
+        )
+        for piece in (4, 5, 6, 7, 0, 1, 2, 3)
+        for kind in range(2)
+    ]
+    if not has_prev:
+        result_copies.append(pltpu.make_async_copy(x_n, norm_out_ref, r_sem.at[16]))
+    for copy in result_copies:
+        copy.start()
+    g_query = tn(h_s[...], dp_s[...])
+    g_out = nn(att_s[...], c_s[...])
+    if has_prev:
+        g_query = g_query + pq_s[...]
+        g_out = g_out + po_s[...]
+        sums = [sums[0] + pv_ref[0:1, :640], sums[1] + pv_ref[1:2, :], sums[2] + pv_ref[2:3, :]]
     if last:
-        gq_s, go_s, tr_s = refs[20:]
-        gq_s[:, :576] = g_query
+        gq_s, go_s, tr_s = refs
+        gq_s[...] = g_query
         go_s[...] = g_out
         tr_s[...] = jnp.zeros_like(tr_s)
         tr_s[64:65, :] = sums[1]
         tr_s[65:66, :] = sums[2]
         tr_s[66:69, :] = mv_ref[1:4, :]
         columns = jnp.transpose(tr_s[...])
-        lane = lax.broadcasted_iota(jnp.int32, (768, 128), 1)
+        lanes = lax.broadcasted_iota(jnp.int32, (768, 128), 1)
         target_at = col_ref[0:1, :576] + row_ref[25] * 192
         for third in range(3):
             hit = at_ref[:, third : third + 1] == target_at
-            column = jnp.sum(jnp.where(hit, sums[0], 0.0), axis=1, keepdims=True)
-            columns = jnp.where(lane == 69 + third, column, columns)
-        gq_s[:, 512:640] = jnp.where(lane < 64, gq_s[:, 512:640], columns)
+            column = jnp.sum(jnp.where(hit, sums[0][:, :576], 0.0), axis=1, keepdims=True)
+            columns = jnp.where(lanes == 69 + third, column, columns)
+        gq_s[:, 512:640] = jnp.where(lanes < 64, gq_s[:, 512:640], columns)
         for half, target in ((0, qkeep_ref), (1, qsend_ref)):
             for zz in range(4):
                 at = zz * 2 + (row_ref[24] ^ half)
@@ -735,81 +892,86 @@
         gq_ref[...] = g_query
         go_ref[...] = g_out
         vec_ref[...] = jnp.zeros_like(vec_ref)
-        vec_ref[0:1, :576] = sums[0]
+        vec_ref[0:1, :640] = sums[0]
         vec_ref[1:2, :] = sums[1]
         vec_ref[2:3, :] = sums[2]
-    for piece in range(8):
-        rows = pl.ds(pl.multiple_of(row_ref[16 + piece], ROWS), ROWS)
-        target = keep_ref if piece < 4 else send_ref
-        for kind, source in ((0, out_s), (1, s_s)):
-            total = source[rows, :]
-            if has_prev:
-                total = total + partial[0, piece, kind].astype(f32)
-            target[piece % 4, kind] = total.astype(bf16)
-
-
-def attn_call(row_offsets, parts, at, weights, o_own, o_other, vecs, partial, seq, prev, tail):
+    for copy in result_copies:
+        copy.wait()
+
+
+def attn_call(row_offsets, parts, inside, weights, o_own, o_other, vecs, partial, seq, prev, tail):
     width = vecs.shape[-1]
     f32, bf16 = jnp.float32, jnp.bfloat16
-    part_spec = pl.BlockSpec((2, 2, 1, ROWS, width), lambda i, *_: (0, 0, at, 0, 0))
-    partial_spec = pl.BlockSpec((1, 8, 2, ROWS, width), lambda i, *_: (seq - 1, 0, 0, 0, 0))
-    extra = list(prev) if prev is not None else []
-    partials = [partial] if prev is not None else []
-    last = tail is not None
-    after = list(tail) if last else []
+    anywhere = pl.BlockSpec(memory_space=pl.ANY)
+    dma = pltpu.SemaphoreType.DMA
+    has_prev, last = prev is not None, tail is not None
     rows = 8 * ROWS
     half = (4, 2, ROWS, width)
     shapes = [(half, bf16), (half, bf16)]
     if last:
         shapes += [((4, 96, 640), bf16), ((4, 96, 640), f32), ((96, width), bf16), ((96, width), f32)]
     else:
-        shapes += [((width, 576), f32), ((192, width), f32), ((8, width), f32)]
-    outs = [jax.ShapeDtypeStruct(shape, kind) for shape, kind in shapes]
+        shapes += [((width, 640), f32), ((192, width), f32), ((8, width), f32)]
+    out_specs = [anywhere] * 2 + [whole(shape) for shape, _ in shapes[2:]]
+    if not has_prev:
+        shapes.append(((rows, width), f32))
+        out_specs.append(anywhere)
+    operands = [*parts, *weights, o_own, o_other, vecs]
+    in_specs = [anywhere] * 18 + [whole(vecs.shape)]
+    scratch = [
+        pltpu.VMEM((width, 640), bf16),
+        pltpu.VMEM((256, width), bf16),
+        pltpu.VMEM((rows, width), bf16),
+        pltpu.VMEM((rows, width), bf16),
+        pltpu.VMEM((rows, width), f32),
+        pltpu.VMEM((rows, width), bf16),
+    ]
+    scratch += [pltpu.VMEM((3, rows, 128), bf16)] * 4
+    scratch += [
+        pltpu.VMEM((3, 64, rows), bf16),
+        pltpu.VMEM((192, rows), bf16),
+        pltpu.VMEM((192, rows), bf16),
+        pltpu.VMEM((3, rows, 128), f32),
+        pltpu.VMEM((3, rows, 128), f32),
+        pltpu.VMEM((2, rows, 128), f32),
+        pltpu.VMEM((rows, 256), bf16),
+        pltpu.VMEM((192, rows), bf16),
+        pltpu.VMEM((rows, 640), bf16),
+        pltpu.VMEM((2, rows, width), bf16),
+        pltpu.VMEM((3, rows, 128), f32),
+        dma((10,)),
+        dma((16,)),
+        dma((17,)),
+    ]
+    if has_prev:
+        operands += [*partial, *prev]
+        in_specs += [anywhere] * 4 + [whole(prev[2].shape)]
+        scratch += [
+            pltpu.VMEM((2, rows, width), bf16),
+            pltpu.VMEM((width, 640), f32),
+            pltpu.VMEM((192, width), f32),
+            dma((18,)),
+        ]
+    if last:
+        operands += list(tail)
+        in_specs += [whole(a.shape) for a in tail]
+        scratch += [pltpu.VMEM((width, 640), f32), pltpu.VMEM((192, width), f32), pltpu.VMEM((128, width), f32)]
     return pl.pallas_call(
-        functools.partial(attn_kernel, prev is not None, last),
+        functools.partial(attn_kernel, has_prev, last, seq, inside),
         grid_spec=pltpu.PrefetchScalarGridSpec(
             num_scalar_prefetch=1,
             grid=(1,),
-            in_specs=[part_spec] * 4
-            + [whole(a.shape) for a in (*weights, o_own, o_other, vecs)]
-            + [partial_spec] * len(partials)
-            + [whole(a.shape) for a in extra + after],
-            out_specs=[whole(a.shape) for a in outs],
-            scratch_shapes=[
-                pltpu.VMEM((width, 576), bf16),
-                pltpu.VMEM((192, width), bf16),
-                pltpu.VMEM((rows, width), f32),
-                pltpu.VMEM((rows, width), bf16),
-                pltpu.VMEM((rows, width), bf16),
-                pltpu.VMEM((3, rows, 64), bf16),
-                pltpu.VMEM((3, rows, 64), bf16),
-                pltpu.VMEM((3, rows, 64), bf16),
-                pltpu.VMEM((3, 64, rows), bf16),
-                pltpu.VMEM((3, 64, rows), bf16),
-                pltpu.VMEM((3, rows, 64), bf16),
-                pltpu.VMEM((3, 64, rows), bf16),
-                pltpu.VMEM((rows, 64), f32),
-                pltpu.VMEM((rows, 64), f32),
-                pltpu.VMEM((rows, 192), bf16),
-                pltpu.VMEM((192, rows), bf16),
-                pltpu.VMEM((rows, 576), f32),
-                pltpu.VMEM((rows, width), f32),
-                pltpu.VMEM((rows, width), f32),
-                pltpu.VMEM((3, rows, 128), f32),
-            ]
-            + (
-                [pltpu.VMEM((width, 640), f32), pltpu.VMEM((192, width), f32), pltpu.VMEM((128, width), f32)]
-                if last
-                else []
-            ),
+            in_specs=in_specs,
+            out_specs=out_specs,
+            scratch_shapes=scratch,
         ),
-        out_shape=outs,
-        compiler_params=pltpu.CompilerParams(vmem_limit_bytes=56 << 20),
+        out_shape=[jax.ShapeDtypeStruct(shape, kind) for shape, kind in shapes],
+        compiler_params=pltpu.CompilerParams(vmem_limit_bytes=58 << 20),
         cost_estimate=pl.CostEstimate(
             flops=24_000_000_000, transcendentals=0, bytes_accessed=15_000_000
         ),
         name="attn",
-    )(row_offsets, *parts, *weights, o_own, o_other, vecs, *partials, *extra, *after)
+    )(row_offsets, *operands)
 
 
 def finish_kernel(half_ref, x_ref, c_ref, own_ref, other_ref, bias, *refs):
@@ -1142,9 +1304,10 @@
     first = 0
     for count in CHUNKS:
         got = swap(rows_of(1 - y, first, count), 4)
-        two = jnp.stack([rows_of(y, first, count), got])
-        side = swap(two, 2)
-        parts.append((two, side, swap(two, 1), swap(side, 1)))
+        own = rows_of(y, first, count)
+        side, side_got = swap(own, 2), swap(got, 2)
+        near = (own, got, side, side_got)
+        parts.append(near + tuple(swap(a, 1) for a in near))
         first += count
 
     pack_got = swap(pack_send, 2)
@@ -1178,7 +1341,8 @@
                 value = value + pick(block, at).astype(f32)
             return value
 
-        sent = [shift_z(total((z + k) % 4).astype(bf16), k) for k in (1, 2, 3)]
+        low = [total((z + k) % 4).astype(bf16) for k in (1, 2, 3)]
+        sent = [shift_z(part, k + 1) for k, part in enumerate(low)]
         result = total(z)
         for part in sent:
             result = result + part.astype(f32)
@@ -1193,21 +1357,21 @@
         far = (keep[1].astype(f32) + got[1].astype(f32) + side[1].astype(f32)).astype(bf16)
         return finish_call(half, seq, inputs, cotangent, mine, swap(far, 4), vecs, done)
 
-    first_send, first_keep, g_q, g_o, vec = attention(0, None, None)
+    first_send, first_keep, g_q, g_o, vec, first_norm = attention(0, None, None)
     prev = (g_q, g_o, vec)
-    send, keep, rest_part, g_send, g_keep, mlp_vec = mlp_call(
-        row_offsets, parts, mlp_all, vecs, cotangent, first_send, first_keep
+    send, keep, rest_part, rest_norm, g_send, g_keep, mlp_vec = mlp_call(
+        row_offsets, parts, mlp_all, vecs, cotangent, first_send, first_keep, first_norm
     )
     g_got = swap(g_send, 4)
     done = scatter(0, send, keep, None)
-    send, keep, g_q, g_o, vec = attention(1, rest_part, prev)
+    send, keep, g_q, g_o, vec = attention(1, (rest_part, rest_norm), prev)
     done = scatter(1, send, keep, done)
     mlp_grad = reduce_z((g_keep, g_got))
     grad_w_mlp = mlp_grad[96:192]
     grad_b_in = mlp_grad[192, :96]
     grad_w_in = spread_in_call(exchange_four(mlp_grad[:96].astype(bf16).reshape(4, 24, 768), x, c))
     send, keep, q_send, q_keep, o_send, o_keep = attention(
-        2, rest_part, (g_q, g_o, vec), (mlp_vec, at_rows, at_cols)
+        2, (rest_part, rest_norm), (g_q, g_o, vec), (mlp_vec, at_rows, at_cols)
     )
     done = scatter(2, send, keep, done)
     q_grad = reduce_z((q_keep, swap(q_send, 4)))

time: 416 us -> 393 us (0.945)
  Pallas kernels: 140 us -> 128 us
  waiting for transfers between devices: 170 us -> 163 us
  local copies, waits for them, and re-layouts: 19 us -> 12.7 us
    ppermute x15, waiting for transfers between devices: 49.3 us -> 37.9 us  [shift_z(): return lax.ppermute(value, 'fsdp', [(i, (i + step) % 4) for i in range(4)])]
    pallas_call x3, Pallas kernels: 74.7 us -> 64.5 us  [attn_call(): pl.pallas_call(functools.partial(attn_kernel, has_prev, last, seq, inside...]
    concatenate x1, local copies, waits for them, and re-layouts: 5.53 us -> 0.09 us  [fast_body(): jnp.concatenate([ln1_gain, ln1_bias, ln2_gain, ln2_bias, b_out, b_mlp_out...]
    ppermute x39 -> x45, waiting for transfers between devices: 120 us -> 125 us  [swap(): return lax.ppermute(value, 'ctx', [(i, i ^ bit) for i in range(8)])]
    ppermute x39 -> x45, starting transfers between devices: 35.6 us -> 37.4 us  [swap(): return lax.ppermute(value, 'ctx', [(i, i ^ bit) for i in range(8)])]
  transfers between devices with their start and end apart: 54 -> 60, of which waited for: 28 -> 31; matrix products, arithmetic and copies ran while one was open for 6% -> 6% of each run, Pallas kernels for 11% -> 11%
where the time goes in v2:
time: 393 us; the launch traced here: 390 us
  waiting for transfers between devices  163 us (41%)
  Pallas kernels  128 us (33%)
  starting transfers between devices  66.2 us (17%)
  other arithmetic  17.6 us (4%)
  local copies, waits for them, and re-layouts  12.7 us (3%)
    ppermute x45, waiting for transfers between devices, swap(): return lax.ppermute(value, 'ctx', [(i, i ^ bit) for i in range(8)])  125 us
    pallas_call x3, Pallas kernels, attn_call(): pl.pallas_call(functools.partial(attn_kernel, has_prev, last, seq, inside...  64.5 us
    ppermute x15, waiting for transfers between devices, shift_z(): return lax.ppermute(value, 'fsdp', [(i, (i + step) % 4) for i in range(4)])  37.9 us
    ppermute x45, starting transfers between devices, swap(): return lax.ppermute(value, 'ctx', [(i, i ^ bit) for i in range(8)])  37.4 us
    pallas_call x1, Pallas kernels, mlp_call(): pl.pallas_call(functools.partial(mlp_kernel, chunks), grid_spec=pltpu.Pre...  36.7 us
    ppermute x15, starting transfers between devices, shift_z(): return lax.ppermute(value, 'fsdp', [(i, (i + step) % 4) for i in range(4)])  28.8 us
    pallas_call x3, Pallas kernels, finish_call(): pl.pallas_call(finish_kernel, grid_spec=pltpu.PrefetchScalarGridSpec(num_...  8.85 us
  transfers between devices with their start and end apart: 60, of which 31 were waited for; matrix products, arithmetic and copies ran while one was open for 6% of the time, Pallas kernels for 11%

profile of v2, /device:TPU:0, one launch (start us, length us, event | category | flops | bytes accessed | tf_op | source)
XLA Modules:
  0.0 389.7 jit_solution(2890544444016754307)
XLA Ops:
  2.9 3.0 collective-permute-start.20
  13.1 4.9 %collective-permute-done.7.got_ref = bf16[2,24,1408]{2,1,0:T(8,128)(2,1)S(1)} collective-permute-done((bf16[2,24,1408]{2,1,0:T(8,128)(2,1)}, bf16[2,24,1408]{2,1,0:T(8,128)(2,1)S(1)}, u32[]{:S(2)}, u32[]{:S(2)}) %collective-permute-start.7) | collective-permute-done | bytes 135200 | tf_op jit(solution)/shard_map/ppermute | solution.py:390
  34.2 5.5 %collective-permute-done.10.three.refs_2_.refs_10_ = bf16[96,832]{1,0:T(8,128)(2,1)S(1)} collective-permute-done((bf16[96,832]{1,0:T(8,128)(2,1)}, bf16[96,832]{1,0:T(8,128)(2,1)S(1)}, u32[]{:S(2)}, u32[]{:S(2)}) %collective-permute-start.10) | collective-permute-done | bytes 159776 | tf_op jit(solution)/shard_map/ppermute | solution.py:394
  42.1 3.3 collective-permute-start.27
  59.6 4.8 %collective-permute-done.27.refs_18_ = bf16[192,768]{1,0:T(8,128)(2,1)} collective-permute-done((bf16[192,768]{1,0:T(8,128)(2,1)S(1)}, bf16[192,768]{1,0:T(8,128)(2,1)}, u32[]{:S(2)}, u32[]{:S(2)}) %collective-permute-start.27) | collective-permute-done | bytes 294944 | tf_op jit(solution)/shard_map/ppermute | solution.py:394
  86.5 4.5 %vectors.1.refs_18_.refs_24_.bias = f32[8,768]{1,0:T(8,128)} custom-call(s32[29]{0:T(128)} %concatenate.6.at_ref.row_ref, bf16[96,832]{1,0:T(8,128)(2,1)} %get-tuple-element.59.one.refs_0_.refs_8_, bf16[96,832]{1,0:T(8,128)(2,1)} %copy-done.8, bf16[96,832]{1,0:T(8,128)(2,1)} %copy-done.9, bf16[96,832]{1,0:T(8,128)(2,1)} %copy-done.10, ...), custom_call_target="tpu_custom_call" | custom-call | tf_op jit(solution)/shard_map/vectors/pallas_call | solution.py:1191
  91.0 5.0 %collective-permute-done.1.refs_10_.refs_2_ = bf16[2,2,128,768]{3,2,1,0:T(8,128)(2,1)S(1)} collective-permute-done((bf16[2,2,128,768]{3,2,1,0:T(8,128)(2,1)S(1)}, bf16[2,2,128,768]{3,2,1,0:T(8,128)(2,1)S(1)}, u32[]{:S(2)}, u32[]{:S(2)}) %collective-permute-start.1) | collective-permute-done | bytes 786464 | tf_op jit(solution)/shard_map/ppermute | solution.py:390
  98.5 11.4 %collective-permute-done.2.refs_11_.refs_3_ = bf16[2,2,128,768]{3,2,1,0:T(8,128)(2,1)S(1)} collective-permute-done((bf16[2,2,128,768]{3,2,1,0:T(8,128)(2,1)}, bf16[2,2,128,768]{3,2,1,0:T(8,128)(2,1)S(1)}, u32[]{:S(2)}, u32[]{:S(2)}) %collective-permute-start.2) | collective-permute-done | bytes 786464 | tf_op jit(solution)/shard_map/ppermute | solution.py:390
  109.9 20.2 %attn.3 = (bf16[4,2,128,768]{3,2,1,0:T(8,128)(2,1)}, bf16[4,2,128,768]{3,2,1,0:T(8,128)(2,1)}, f32[768,640]{1,0:T(8,128)}, f32[192,768]{1,0:T(8,128)}, f32[8,768]{1,0:T(8,128)}, /*index=5*/f32[1024,768]{1,0:T(8,128)}) custom-call(s32[29]{0:T(128)} %concatenate.6.at_ref.row_ref, bf16[2,1,128,768]{3,2,1,0:T(8,128)(2,1)} %pad_maximum_fusion.2.refs_0_, ...), custom_call_target="tpu_custom_call" | custom-call | flops 24000000000 | bytes 15000000 | tf_op jit(solution)/shard_map/attn/pallas_call | solution.py:959
  131.7 36.7 %mlp.1 = (bf16[4,2,128,768]{3,2,1,0:T(8,128)(2,1)}, bf16[4,2,128,768]{3,2,1,0:T(8,128)(2,1)}, bf16[2,8,2,128,768]{4,3,2,1,0:T(8,128)(2,1)}, f32[2,1024,768]{2,1,...) custom-call(s32[29]{0:T(128)} %concatenate.6.at_ref.row_ref, ...), custom_call_target="tpu_custom_call" | custom-call | flops 30000001024 | bytes 30000000 | tf_op jit(solution)/shard_map/mlp/pallas_call | solution.py:575
  168.4 21.2 %attn.4 = (bf16[4,2,128,768]{3,2,1,0:T(8,128)(2,1)}, bf16[4,2,128,768]{3,2,1,0:T(8,128)(2,1)}, f32[768,640]{1,0:T(8,128)}, f32[192,768]{1,0:T(8,128)}, f32[8,768]{1,0:T(8,128)}) custom-call(s32[29]{0:T(128)} %concatenate.6.at_ref.row_ref, bf16[2,2,128,768]{3,2,1,0:T(8,128)(2,1)} %copy-done.6, bf16[2,2,128,768]{3,2,1,0:T(8,128)(2,1)} %collective-permute-done.refs_9_.refs_1_, ...), custom_call_target="tpu_custom_call" | custom-call | flops 24000000000 | bytes 15000000 | tf_op jit(solution)/shard_map/attn/pallas_call | solution.py:959
  189.6 23.1 %attn.5 = (bf16[4,2,128,768]{3,2,1,0:T(8,128)(2,1)}, bf16[4,2,128,768]{3,2,1,0:T(8,128)(2,1)}, bf16[4,96,640]{2,1,0:T(8,128)(2,1)}, f32[4,96,640]{2,1,0:T(8,128)...) custom-call(s32[29]{0:T(128)} %concatenate.6.at_ref.row_ref, bf16[2,2,128,768]{3,2,1,0:T(8,128)(2,1)} %copy-done.6, ...), custom_call_target="tpu_custom_call" | custom-call | flops 24000000000 | bytes 15000000 | tf_op jit(solution)/shard_map/attn/pallas_call | solution.py:959
  214.3 4.9 %collective-permute-done.48 = bf16[96,768]{1,0:T(8,128)(2,1)S(1)} collective-permute-done((bf16[96,768]{1,0:T(8,128)(2,1)}, bf16[96,768]{1,0:T(8,128)(2,1)S(1)}, u32[]{:S(2)}, u32[]{:S(2)}) %collective-permute-start.48) | collective-permute-done | bytes 147488 | tf_op jit(solution)/shard_map/ppermute | solution.py:390
  227.6 34.3 %collective-permute-done.42 = bf16[4,96,640]{2,1,0:T(8,128)(2,1)S(1)} collective-permute-done((bf16[4,96,640]{2,1,0:T(8,128)(2,1)}, bf16[4,96,640]{2,1,0:T(8,128)(2,1)S(1)}, u32[]{:S(2)}, u32[]{:S(2)}) %collective-permute-start.42) | collective-permute-done | bytes 491552 | tf_op jit(solution)/shard_map/ppermute | solution.py:390
  262.0 4.2 %collective-permute-start.43 = (bf16[96,640]{1,0:T(8,128)(2,1)S(1)}, bf16[96,640]{1,0:T(8,128)(2,1)S(1)}, u32[]{:S(2)}, u32[]{:S(2)}) collective-permute-start(bf16[96,640]{1,0:T(8,128)(2,1)S(1)} %get-tuple-element.115), channel_id=1, source_target_pairs={{0,8},{8,16},{16,24},{24,0},{1,9},{9,17},{17,25},{25,1},{2,10},{10... | collective-permute-start | bytes 368648 | tf_op jit(solution)/shard_map/ppermute | solution.py:394
  268.8 3.0 collective-permute-done.43
  271.8 3.4 collective-permute-done.44
  276.0 3.4 collective-permute-start.52
  286.5 3.0 collective-permute-done.46
  295.0 3.7 collective-permute-start.56
  307.8 12.4 %collective-permute-done.56 = bf16[208,768]{1,0:T(8,128)(2,1)S(1)} collective-permute-done((bf16[208,768]{1,0:T(8,128)(2,1)S(1)}, bf16[208,768]{1,0:T(8,128)(2,1)S(1)}, u32[]{:S(2)}, u32[]{:S(2)}) %collective-permute-start.56) | collective-permute-done | bytes 319520 | tf_op jit(solution)/shard_map/ppermute | solution.py:394
  323.3 31.3 %collective-permute-done.58 = bf16[2,24,768]{2,1,0:T(8,128)(2,1)S(1)} collective-permute-done((bf16[2,24,768]{2,1,0:T(8,128)(2,1)S(1)}, bf16[2,24,768]{2,1,0:T(8,128)(2,1)S(1)}, u32[]{:S(2)}, u32[]{:S(2)}) %collective-permute-start.58) | collective-permute-done | bytes 73760 | tf_op jit(solution)/shard_map/ppermute | solution.py:390
  372.5 4.7 %collective-permute-done.38.other_ref = bf16[2,128,768]{2,1,0:T(8,128)(2,1)S(1)} collective-permute-done((bf16[2,128,768]{2,1,0:T(8,128)(2,1)S(1)}, bf16[2,128,768]{2,1,0:T(8,128)(2,1)S(1)}, u32[]{:S(2)}, u32[]{:S(2)}) %collective-permute-start.38) | collective-permute-done | bytes 393248 | tf_op jit(solution)/shard_map/ppermute | solution.py:390
  381.0 4.2 %collective-permute-done.35.other_ref = bf16[2,128,768]{2,1,0:T(8,128)(2,1)S(1)} collective-permute-done((bf16[2,128,768]{2,1,0:T(8,128)(2,1)S(1)}, bf16[2,128,768]{2,1,0:T(8,128)(2,1)S(1)}, u32[]{:S(2)}, u32[]{:S(2)}) %collective-permute-start.35) | collective-permute-done | bytes 393248 | tf_op jit(solution)/shard_map/ppermute | solution.py:390
  (245 shorter events, 132.1 us)
Async XLA Ops:
  2.9 26.0 %collective-permute-start.20 = (bf16[2,1,128,768]{3,2,1,0:T(8,128)(2,1)}, bf16[2,1,128,768]{3,2,1,0:T(8,128)(2,1)}, u32[]{:S(2)}, u32[]{:S(2)}) collective-permute-start(bf16[2,1,128,768]{3,2,1,0:T(8,128)(2,1)} %pad_maximum_fusion.2.refs_0_), channel_id=1, source_target_pairs={{0,2},{1,3},{2,0},{3,1},{4,6},{5,7},{6,4},{7,5},{8,10},{9,11},{10,... | collective-permute-start | bytes 1179656 | tf_op jit(solution)/shard_map/ppermute | solution.py:390
  5.8 42.1 %collective-permute-start.22 = (bf16[2,1,128,768]{3,2,1,0:T(8,128)(2,1)}, bf16[2,1,128,768]{3,2,1,0:T(8,128)(2,1)}, u32[]{:S(2)}, u32[]{:S(2)}) collective-permute-start(bf16[2,1,128,768]{3,2,1,0:T(8,128)(2,1)} %pad_maximum_fusion.2.refs_0_), channel_id=1, source_target_pairs={{0,1},{1,0},{2,3},{3,2},{4,5},{5,4},{6,7},{7,6},{8,9},{9,8},{10,11... | collective-permute-start | bytes 1179656 | tf_op jit(solution)/shard_map/ppermute | solution.py:390
  28.9 52.5 %collective-permute-start = (bf16[2,2,128,768]{3,2,1,0:T(8,128)(2,1)S(1)}, bf16[2,2,128,768]{3,2,1,0:T(8,128)(2,1)}, u32[]{:S(2)}, u32[]{:S(2)}) collective-permute-start(bf16[2,2,128,768]{3,2,1,0:T(8,128)(2,1)S(1)} %pad_maximum_fusion.1), channel_id=1, source_target_pairs={{0,4},{1,5},{2,6},{3,7},{4,0},{5,1},{6,2},{7,3},{8,12},{9,13},{10,... | collective-permute-start | bytes 2359304 | tf_op jit(solution)/shard_map/ppermute | solution.py:390
  42.1 22.3 %collective-permute-start.27 = (bf16[192,768]{1,0:T(8,128)(2,1)S(1)}, bf16[192,768]{1,0:T(8,128)(2,1)}, u32[]{:S(2)}, u32[]{:S(2)}) collective-permute-start(bf16[192,768]{1,0:T(8,128)(2,1)S(1)} %copy-done.35), channel_id=1, source_target_pairs={{0,16},{8,24},{16,0},{24,8},{1,17},{9,25},{17,1},{25,9},{2,18},{10... | collective-permute-start | bytes 884744 | tf_op jit(solution)/shard_map/ppermute | solution.py:394
  58.1 24.9 %collective-permute-start.21 = (bf16[2,1,128,768]{3,2,1,0:T(8,128)(2,1)}, bf16[2,1,128,768]{3,2,1,0:T(8,128)(2,1)}, u32[]{:S(2)}, u32[]{:S(2)}) collective-permute-start(bf16[2,1,128,768]{3,2,1,0:T(8,128)(2,1)} %collective-permute-done.19.refs_1_), channel_id=1, source_target_pairs={{0,2},{1,3},{2,0},{3,1},{4,6},{5,7},{6,4},{7,5},{8,10},{9,11},{10,... | collective-permute-start | bytes 1179656 | tf_op jit(solution)/shard_map/ppermute | solution.py:390
  75.6 20.4 %collective-permute-start.1 = (bf16[2,2,128,768]{3,2,1,0:T(8,128)(2,1)S(1)}, bf16[2,2,128,768]{3,2,1,0:T(8,128)(2,1)S(1)}, u32[]{:S(2)}, u32[]{:S(2)}) collective-permute-start(bf16[2,2,128,768]{3,2,1,0:T(8,128)(2,1)S(1)} %pad_maximum_fusion.refs_8_.refs_0_), channel_id=1, source_target_pairs={{0,2},{1,3},{2,0},{3,1},{4,6},{5,7},{6,4},{7,5},{8,10},{9,11},{10,... | collective-permute-start | bytes 2359304 | tf_op jit(solution)/shard_map/ppermute | solution.py:390
  81.4 28.5 %collective-permute-start.2 = (bf16[2,2,128,768]{3,2,1,0:T(8,128)(2,1)}, bf16[2,2,128,768]{3,2,1,0:T(8,128)(2,1)S(1)}, u32[]{:S(2)}, u32[]{:S(2)}) collective-permute-start(bf16[2,2,128,768]{3,2,1,0:T(8,128)(2,1)} %collective-permute-done.refs_9_.refs_1_), channel_id=1, source_target_pairs={{0,2},{1,3},{2,0},{3,1},{4,6},{5,7},{6,4},{7,5},{8,10},{9,11},{10,... | collective-permute-start | bytes 2359304 | tf_op jit(solution)/shard_map/ppermute | solution.py:390
  96.0 34.2 %collective-permute-start.31 = (bf16[192,768]{1,0:T(8,128)(2,1)}, bf16[192,768]{1,0:T(8,128)(2,1)S(1)}, u32[]{:S(2)}, u32[]{:S(2)}) collective-permute-start(bf16[192,768]{1,0:T(8,128)(2,1)} %collective-permute-done.27.refs_18_), channel_id=1, source_target_pairs={{0,4},{1,5},{2,6},{3,7},{4,0},{5,1},{6,2},{7,3},{8,12},{9,13},{10,... | collective-permute-start | bytes 884744 | tf_op jit(solution)/shard_map/ppermute | solution.py:390
  97.5 32.7 %collective-permute-start.32 = (bf16[192,768]{1,0:T(8,128)(2,1)}, bf16[192,768]{1,0:T(8,128)(2,1)S(1)}, u32[]{:S(2)}, u32[]{:S(2)}) collective-permute-start(bf16[192,768]{1,0:T(8,128)(2,1)} %collective-permute-done.28.refs_19_), channel_id=1, source_target_pairs={{0,4},{1,5},{2,6},{3,7},{4,0},{5,1},{6,2},{7,3},{8,12},{9,13},{10,... | collective-permute-start | bytes 884744 | tf_op jit(solution)/shard_map/ppermute | solution.py:390
  98.0 32.2 %collective-permute-start.4 = (bf16[2,2,128,768]{3,2,1,0:T(8,128)(2,1)}, bf16[2,2,128,768]{3,2,1,0:T(8,128)(2,1)S(1)}, u32[]{:S(2)}, u32[]{:S(2)}) collective-permute-start(bf16[2,2,128,768]{3,2,1,0:T(8,128)(2,1)} %collective-permute-done.refs_9_.refs_1_), channel_id=1, source_target_pairs={{0,1},{1,0},{2,3},{3,2},{4,5},{5,4},{6,7},{7,6},{8,9},{9,8},{10,11... | collective-permute-start | bytes 2359304 | tf_op jit(solution)/shard_map/ppermute | solution.py:390
  98.0 32.2 %collective-permute-start.5 = (bf16[2,2,128,768]{3,2,1,0:T(8,128)(2,1)S(1)}, bf16[2,2,128,768]{3,2,1,0:T(8,128)(2,1)S(1)}, u32[]{:S(2)}, u32[]{:S(2)}) collective-permute-start(bf16[2,2,128,768]{3,2,1,0:T(8,128)(2,1)S(1)} %collective-permute-done.1.refs_10_.refs_2_), channel_id=1, source_target_pairs={{0,1},{1,0},{2,3},{3,2},{4,5},{5,4},{6,7},{7,6},{8,9},{9,8},{10,11... | collective-permute-start | bytes 2359304 | tf_op jit(solution)/shard_map/ppermute | solution.py:390
  109.9 20.3 %collective-permute-start.6 = (bf16[2,2,128,768]{3,2,1,0:T(8,128)(2,1)S(1)}, bf16[2,2,128,768]{3,2,1,0:T(8,128)(2,1)S(1)}, u32[]{:S(2)}, u32[]{:S(2)}) collective-permute-start(bf16[2,2,128,768]{3,2,1,0:T(8,128)(2,1)S(1)} %collective-permute-done.2.refs_11_.refs_3_), channel_id=1, source_target_pairs={{0,1},{1,0},{2,3},{3,2},{4,5},{5,4},{6,7},{7,6},{8,9},{9,8},{10,11... | collective-permute-start | bytes 2359304 | tf_op jit(solution)/shard_map/ppermute | solution.py:390
  221.8 71.5 %collective-permute-start.54 = (bf16[4,208,768]{2,1,0:T(8,128)(2,1)}, bf16[4,208,768]{2,1,0:T(8,128)(2,1)}, u32[]{:S(2)}, u32[]{:S(2)}) collective-permute-start(bf16[4,208,768]{2,1,0:T(8,128)(2,1)} %get-tuple-element.99), channel_id=1, source_target_pairs={{0,4},{1,5},{2,6},{3,7},{4,0},{5,1},{6,2},{7,3},{8,12},{9,13},{10,... | collective-permute-start | bytes 3833864 | tf_op jit(solution)/shard_map/ppermute | solution.py:390
  223.3 38.6 %collective-permute-start.42 = (bf16[4,96,640]{2,1,0:T(8,128)(2,1)}, bf16[4,96,640]{2,1,0:T(8,128)(2,1)S(1)}, u32[]{:S(2)}, u32[]{:S(2)}) collective-permute-start(bf16[4,96,640]{2,1,0:T(8,128)(2,1)} %get-tuple-element.88), channel_id=1, source_target_pairs={{0,4},{1,5},{2,6},{3,7},{4,0},{5,1},{6,2},{7,3},{8,12},{9,13},{10,... | collective-permute-start | bytes 1474568 | tf_op jit(solution)/shard_map/ppermute | solution.py:390
  223.8 74.8 %collective-permute-start.39 = (bf16[4,2,128,768]{3,2,1,0:T(8,128)(2,1)}, bf16[4,2,128,768]{3,2,1,0:T(8,128)(2,1)}, u32[]{:S(2)}, u32[]{:S(2)}) collective-permute-start(bf16[4,2,128,768]{3,2,1,0:T(8,128)(2,1)} %get-tuple-element.80), channel_id=1, source_target_pairs={{0,1},{1,0},{2,3},{3,2},{4,5},{5,4},{6,7},{7,6},{8,9},{9,8},{10,11... | collective-permute-start | bytes 4718600 | tf_op jit(solution)/shard_map/ppermute | solution.py:390
  271.8 28.4 %collective-permute-start.36 = (bf16[4,2,128,768]{3,2,1,0:T(8,128)(2,1)}, bf16[4,2,128,768]{3,2,1,0:T(8,128)(2,1)}, u32[]{:S(2)}, u32[]{:S(2)}) collective-permute-start(bf16[4,2,128,768]{3,2,1,0:T(8,128)(2,1)} %get-tuple-element.78), channel_id=1, source_target_pairs={{0,1},{1,0},{2,3},{3,2},{4,5},{5,4},{6,7},{7,6},{8,9},{9,8},{10,11... | collective-permute-start | bytes 4718600 | tf_op jit(solution)/shard_map/ppermute | solution.py:390
  282.8 19.3 %collective-permute-start.33 = (bf16[4,2,128,768]{3,2,1,0:T(8,128)(2,1)}, bf16[4,2,128,768]{3,2,1,0:T(8,128)(2,1)}, u32[]{:S(2)}, u32[]{:S(2)}) collective-permute-start(bf16[4,2,128,768]{3,2,1,0:T(8,128)(2,1)} %get-tuple-element.76), channel_id=1, source_target_pairs={{0,1},{1,0},{2,3},{3,2},{4,5},{5,4},{6,7},{7,6},{8,9},{9,8},{10,11... | collective-permute-start | bytes 4718600 | tf_op jit(solution)/shard_map/ppermute | solution.py:390
  295.0 25.2 %collective-permute-start.56 = (bf16[208,768]{1,0:T(8,128)(2,1)S(1)}, bf16[208,768]{1,0:T(8,128)(2,1)S(1)}, u32[]{:S(2)}, u32[]{:S(2)}) collective-permute-start(bf16[208,768]{1,0:T(8,128)(2,1)S(1)} %get-tuple-element.110), channel_id=1, source_target_pairs={{0,16},{8,24},{16,0},{24,8},{1,17},{9,25},{17,1},{25,9},{2,18},{10... | collective-permute-start | bytes 958472 | tf_op jit(solution)/shard_map/ppermute | solution.py:394
  298.7 21.5 %collective-permute-start.57 = (bf16[208,768]{1,0:T(8,128)(2,1)S(1)}, bf16[208,768]{1,0:T(8,128)(2,1)S(1)}, u32[]{:S(2)}, u32[]{:S(2)}) collective-permute-start(bf16[208,768]{1,0:T(8,128)(2,1)S(1)} %get-tuple-element.109), channel_id=1, source_target_pairs={{0,24},{8,0},{16,8},{24,16},{1,25},{9,1},{17,9},{25,17},{2,26},{10... | collective-permute-start | bytes 958472 | tf_op jit(solution)/shard_map/ppermute | solution.py:394
  300.1 54.5 %collective-permute-start.40 = (bf16[2,2,128,768]{3,2,1,0:T(8,128)(2,1)S(1)}, bf16[2,2,128,768]{3,2,1,0:T(8,128)(2,1)S(1)}, u32[]{:S(2)}, u32[]{:S(2)}) collective-permute-start(bf16[2,2,128,768]{3,2,1,0:T(8,128)(2,1)S(1)} %add_convert_fusion), channel_id=1, source_target_pairs={{0,2},{1,3},{2,0},{3,1},{4,6},{5,7},{6,4},{7,5},{8,10},{9,11},{10,... | collective-permute-start | bytes 2359304 | tf_op jit(solution)/shard_map/ppermute | solution.py:390
  302.1 55.9 %collective-permute-start.37 = (bf16[2,2,128,768]{3,2,1,0:T(8,128)(2,1)S(1)}, bf16[2,2,128,768]{3,2,1,0:T(8,128)(2,1)S(1)}, u32[]{:S(2)}, u32[]{:S(2)}) collective-permute-start(bf16[2,2,128,768]{3,2,1,0:T(8,128)(2,1)S(1)} %add_convert_fusion.1), channel_id=1, source_target_pairs={{0,2},{1,3},{2,0},{3,1},{4,6},{5,7},{6,4},{7,5},{8,10},{9,11},{10,... | collective-permute-start | bytes 2359304 | tf_op jit(solution)/shard_map/ppermute | solution.py:390
  307.3 53.7 %collective-permute-start.34 = (bf16[2,2,128,768]{3,2,1,0:T(8,128)(2,1)S(1)}, bf16[2,2,128,768]{3,2,1,0:T(8,128)(2,1)S(1)}, u32[]{:S(2)}, u32[]{:S(2)}) collective-permute-start(bf16[2,2,128,768]{3,2,1,0:T(8,128)(2,1)S(1)} %add_convert_fusion.2), channel_id=1, source_target_pairs={{0,2},{1,3},{2,0},{3,1},{4,6},{5,7},{6,4},{7,5},{8,10},{9,11},{10,... | collective-permute-start | bytes 2359304 | tf_op jit(solution)/shard_map/ppermute | solution.py:390
  321.4 33.1 %collective-permute-start.58 = (bf16[2,24,768]{2,1,0:T(8,128)(2,1)S(1)}, bf16[2,24,768]{2,1,0:T(8,128)(2,1)S(1)}, u32[]{:S(2)}, u32[]{:S(2)}) collective-permute-start(bf16[2,24,768]{2,1,0:T(8,128)(2,1)S(1)} %get-tuple-element.124), channel_id=1, source_target_pairs={{0,2},{1,3},{2,0},{3,1},{4,6},{5,7},{6,4},{7,5},{8,10},{9,11},{10,... | collective-permute-start | bytes 221192 | tf_op jit(solution)/shard_map/ppermute | solution.py:390
  363.2 22.0 %collective-permute-start.35 = (bf16[2,128,768]{2,1,0:T(8,128)(2,1)S(1)}, bf16[2,128,768]{2,1,0:T(8,128)(2,1)S(1)}, u32[]{:S(2)}, u32[]{:S(2)}) collective-permute-start(bf16[2,128,768]{2,1,0:T(8,128)(2,1)S(1)} %get-tuple-element.106), channel_id=1, source_target_pairs={{0,4},{1,5},{2,6},{3,7},{4,0},{5,1},{6,2},{7,3},{8,12},{9,13},{10,... | collective-permute-start | bytes 1179656 | tf_op jit(solution)/shard_map/ppermute | solution.py:390
  (77 other events, 774.9 us)

commit v3 on v2

--- a/solution.py
+++ b/solution.py
@@ -651,7 +651,7 @@
 
     weight_copies = [
         pltpu.make_async_copy(
-            source.at[:, pl.ds(0, 640)],
+            source,
             wq.at[pl.ds(pl.multiple_of(row_ref[at], 16), 96)],
             w_sem.at[at],
         )
@@ -974,48 +974,56 @@
     )(row_offsets, *operands)
 
 
-def finish_kernel(half_ref, x_ref, c_ref, own_ref, other_ref, bias, *refs):
+def finish_kernel(seqs, half_ref, x_ref, c_ref, *refs):
+    refs = list(refs)
+    terms = [[refs.pop(0) for _ in range(4)] for _ in seqs]
+    bias = refs.pop(0)
     out_ref, grad_ref = refs[-2:]
     f32 = jnp.float32
 
-    def write(source):
+    def write(sources):
+        total = [source[0].astype(f32) for source in sources]
+        total = sum(total[1:], total[0])
         x = x_ref[0].astype(f32)
         normed, inverse = normalize(x)
-        out_ref[0] = x + bias[4:5, :] + source[0].astype(f32)
-        s = source[1].astype(f32)
+        out_ref[0] = x + bias[4:5, :] + total[0]
+        s = total[1]
         mean_s = jnp.mean(s, axis=-1, keepdims=True)
         mean_sn = jnp.mean(s * normed, axis=-1, keepdims=True)
         grad_ref[0] = c_ref[0] + inverse * (s - mean_s - normed * mean_sn)
 
-    @pl.when(pl.program_id(0) == 0)
-    def _():
-        write(own_ref)
-
-    @pl.when(pl.program_id(0) == 1)
-    def _():
-        write(other_ref)
-
-
-def finish_call(half, seq, x, cot, own, other, bias, done):
+    for at in range(len(seqs)):
+        for other in range(2):
+            @pl.when(pl.program_id(0) == at * 2 + other)
+            def _(at=at, other=other):
+                write(terms[at][3:] if other else terms[at][:3])
+
+
+def finish_call(half, seqs, x, cot, terms, bias, done):
     _, rows, width = x.shape
     f32 = jnp.float32
     seq_spec = pl.BlockSpec(
-        (1, rows, width), lambda i, at: (jnp.where(i == 0, at[0], 1 - at[0]) * 3 + seq, 0, 0)
-    )
+        (1, rows, width),
+        lambda i, at: (jnp.where(i % 2 == 0, at[0], 1 - at[0]) * 3 + seqs[0] + i // 2, 0, 0),
+    )
+    part_spec = pl.BlockSpec((1, 2, rows, width), lambda i, at: (0, 0, 0, 0))
     before = list(done) if done is not None else []
+    operands = [x, cot, *[a for parts in terms for a in parts], bias]
     return pl.pallas_call(
-        finish_kernel,
+        functools.partial(finish_kernel, seqs),
         grid_spec=pltpu.PrefetchScalarGridSpec(
             num_scalar_prefetch=1,
-            grid=(2,),
-            in_specs=[seq_spec, seq_spec, whole(own.shape), whole(other.shape), whole(bias.shape)]
+            grid=(2 * len(seqs),),
+            in_specs=[seq_spec, seq_spec]
+            + [part_spec] * (4 * len(seqs))
+            + [whole(bias.shape)]
             + [pl.BlockSpec(memory_space=pl.ANY)] * len(before),
             out_specs=[seq_spec, seq_spec],
         ),
         out_shape=[jax.ShapeDtypeStruct(x.shape, f32)] * 2,
-        input_output_aliases={6: 0, 7: 1} if before else {},
+        input_output_aliases={len(operands) + 1: 0, len(operands) + 2: 1} if before else {},
         name="finish",
-    )(half, x, cot, own, other, bias, *before)
+    )(half, *operands, *before)
 
 
 def pick(value, index, axis=0):
@@ -1057,7 +1065,7 @@
     )(row_offsets, w_in, w_qkv, small)
 
 
-def join_kernel(at_ref, own_ref, got_ref, far_ref, down_ref, out_ref, attn_ref, mlp_ref, four, rows_s, cols_s):
+def join_kernel(at_ref, own_ref, got_ref, far_ref, down_ref, attn_ref, mlp_ref, four, rows_s):
     f32, bf16 = jnp.float32, jnp.bfloat16
     x, c = at_ref[26], at_ref[27]
     four[0] = own_ref[c].astype(f32)
@@ -1067,53 +1075,49 @@
     for source in range(4):
         near = ((source & 1) ^ c) * 2 + ((source >> 1) ^ x)
         rows_s[source * 24 : (source + 1) * 24, :] = four[near]
-        cols_s[source * 24 : (source + 1) * 24, :] = out_ref[:, source * 192 : (source + 1) * 192].astype(f32)
     mlp_ref[:96, :] = rows_s[:, :768].astype(bf16)
     mlp_ref[96:, :] = down_ref[...]
-    attn_ref[:, :640] = rows_s[:, 768:].astype(bf16)
-    attn_ref[:, 640:] = cols_s[...].astype(bf16)
-
-
-def join_call(row_offsets, own, got, far, w_down, w_out):
+    attn_ref[...] = rows_s[:, 768:].astype(bf16)
+
+
+def join_call(row_offsets, own, got, far, w_down):
     f32, bf16 = jnp.float32, jnp.bfloat16
-    outs = [jax.ShapeDtypeStruct((96, 832), bf16), jax.ShapeDtypeStruct((192, 768), bf16)]
+    outs = [jax.ShapeDtypeStruct((96, 640), bf16), jax.ShapeDtypeStruct((192, 768), bf16)]
     return pl.pallas_call(
         join_kernel,
         grid_spec=pltpu.PrefetchScalarGridSpec(
             num_scalar_prefetch=1,
             grid=(1,),
-            in_specs=[whole(a.shape) for a in (own, got, far, w_down, w_out)],
+            in_specs=[whole(a.shape) for a in (own, got, far, w_down)],
             out_specs=[whole(a.shape) for a in outs],
-            scratch_shapes=[
-                pltpu.VMEM((4, 24, 1408), f32), pltpu.VMEM((96, 1408), f32), pltpu.VMEM((96, 192), f32)
-            ],
+            scratch_shapes=[pltpu.VMEM((4, 24, 1408), f32), pltpu.VMEM((96, 1408), f32)],
         ),
         out_shape=outs,
         name="join",
-    )(row_offsets, own, got, far, w_down, w_out)
+    )(row_offsets, own, got, far, w_down)
 
 
 def pick_out_kernel(at_ref, one, two, three, four, own_ref, send_ref, all_s):
     for at, source in enumerate((one, two, three, four)):
-        all_s[at] = source[:, 640:]
+        all_s[at] = source[...]
     for core in range(2):
         own_ref[core] = all_s[(at_ref[28] - at_ref[26] * 2 - core + 4) % 4]
         send_ref[core] = all_s[(at_ref[28] - (1 - at_ref[26]) * 2 - core + 4) % 4]
 
 
 def pick_out_call(row_offsets, pieces):
-    half = jax.ShapeDtypeStruct((2, 96, 192), jnp.bfloat16)
+    half = jax.ShapeDtypeStruct((2, 24, 768), jnp.bfloat16)
     return pl.pallas_call(
         pick_out_kernel,
         grid_spec=pltpu.PrefetchScalarGridSpec(
             num_scalar_prefetch=1,
             grid=(1,),
-            in_specs=[whole((96, 832))] * 4,
+            in_specs=[whole((24, 768))] * 4,
             out_specs=[whole(half.shape)] * 2,
-            scratch_shapes=[pltpu.VMEM((4, 96, 192), jnp.bfloat16)],
+            scratch_shapes=[pltpu.VMEM((4, 24, 768), jnp.bfloat16)],
         ),
         out_shape=[half, half],
-        name="pick_out",
+        name="out_pick",
     )(row_offsets, *pieces)
 
 
@@ -1126,10 +1130,7 @@
     four[3] = far_ref[1].astype(f32)
     for source in range(4):
         near = ((source & 1) ^ c) * 2 + ((source >> 1) ^ x)
-        for group in range(4):
-            rows_s[source * 24 : (source + 1) * 24, group * 192 : (group + 1) * 192] = four[
-                near, group * 24 : (group + 1) * 24, :
-            ]
+        rows_s[source * 24 : (source + 1) * 24, :] = four[near]
     out_ref[...] = rows_s[...].astype(bf16)
 
 
@@ -1142,7 +1143,7 @@
             grid=(1,),
             in_specs=[whole(a.shape) for a in (own, got, far)],
             out_specs=whole((96, 768)),
-            scratch_shapes=[pltpu.VMEM((4, 96, 192), f32), pltpu.VMEM((96, 768), f32)],
+            scratch_shapes=[pltpu.VMEM((4, 24, 768), f32), pltpu.VMEM((96, 768), f32)],
         ),
         out_shape=jax.ShapeDtypeStruct((96, 768), bf16),
         name="join_out",
@@ -1203,11 +1204,22 @@
     )(row_offsets, *pieces, rows, cols)
 
 
-def spread_q_kernel(blocks_ref, q_ref, *out_refs):
+def spread_kernel(at_ref, q_mine, q_far, in_mine, in_far, q_ref, in_ref, *refs):
     f32 = jnp.float32
+    out_refs, (q_four, in_four) = refs[:6], refs[6:]
+    x, c = at_ref[26], at_ref[27]
+    for four, near, far in ((q_four, q_mine, q_far), (in_four, in_mine, in_far)):
+        for side in range(2):
+            four[side] = near[side]
+            four[2 + side] = far[side]
     total = None
     for h in range(4):
-        block = blocks_ref[h].astype(f32)
+        near = ((h & 1) ^ c) * 2 + ((h >> 1) ^ x)
+        block = in_four[near].astype(f32)
+        for zy in range(8):
+            first = zy * 384 + h * 96
+            in_ref[:, first : first + 96] = block[:, zy * 96 : (zy + 1) * 96]
+        block = q_four[near].astype(f32)
         for head in range(3):
             for kind in range(2):
                 first = kind * 768 + h * 192 + head * 64
@@ -1224,30 +1236,22 @@
     out_refs[5][...] = jnp.concatenate(rows[5:], axis=1)
 
 
-def spread_q_call(blocks):
-    f32 = jnp.float32
-    shapes = [(24, 2304)] + [(1, 24)] * 5 + [(1, 72)]
+def spread_call(row_offsets, q_pair, in_pair):
+    f32, bf16 = jnp.float32, jnp.bfloat16
+    shapes = [(24, 2304), (24, 3072)] + [(1, 24)] * 5 + [(1, 72)]
+    operands = [*q_pair, *in_pair]
     return pl.pallas_call(
-        spread_q_kernel,
+        spread_kernel,
+        grid_spec=pltpu.PrefetchScalarGridSpec(
+            num_scalar_prefetch=1,
+            grid=(1,),
+            in_specs=[whole(a.shape) for a in operands],
+            out_specs=[whole(shape) for shape in shapes],
+            scratch_shapes=[pltpu.VMEM((4, 24, 640), bf16), pltpu.VMEM((4, 24, 768), bf16)],
+        ),
         out_shape=[jax.ShapeDtypeStruct(shape, f32) for shape in shapes],
-        name="spread_q",
-    )(blocks)
-
-
-def spread_in_kernel(blocks_ref, in_ref):
-    for h in range(4):
-        block = blocks_ref[h].astype(jnp.float32)
-        for zy in range(8):
-            first = zy * 384 + h * 96
-            in_ref[:, first : first + 96] = block[:, zy * 96 : (zy + 1) * 96]
-
-
-def spread_in_call(blocks):
-    return pl.pallas_call(
-        spread_in_kernel,
-        out_shape=jax.ShapeDtypeStruct((24, 3072), jnp.float32),
-        name="spread_in",
-    )(blocks)
+        name="spread",
+    )(row_offsets, *operands)
 
 
 def exchange_four(blocks, x, c):
@@ -1256,13 +1260,8 @@
     got = swap(pick(blocks, 1 - x), 2)
     both = jnp.stack([own, got])
     mine = pick(both, c, 1)
-    theirs = swap(pick(both, 1 - c, 1), 1)
-    mine = jnp.where(x == 0, mine, mine[::-1])
-    theirs = jnp.where(x == 0, theirs, theirs[::-1])
-    pairs = jnp.where(
-        c == 0, jnp.stack([mine, theirs], axis=1), jnp.stack([theirs, mine], axis=1)
-    )
-    return pairs.reshape((4,) + pairs.shape[2:])
+    send = pick(both, 1 - c, 1)
+    return mine, swap(send, 1)
 
 
 def fast(*args):
@@ -1312,12 +1311,13 @@
 
     pack_got = swap(pack_send, 2)
     pack_far = swap(jnp.stack([pick(pack_own, 1 - c), pick(pack_got, 1 - c)]), 1)
-    attn_w, mlp_w = join_call(row_offsets, pack_own, pack_got, pack_far, w_mlp_out, w_out)
+    out_all = [w_out] + [shift_z(w_out, k) for k in (1, 2, 3)]
+    attn_w, mlp_w = join_call(row_offsets, pack_own, pack_got, pack_far, w_mlp_out)
     attn_own = [attn_w] + [shift_z(attn_w, k) for k in (1, 2, 3)]
     mlp_own = [mlp_w] + [shift_z(mlp_w, k) for k in (1, 2, 3)]
     attn_all = attn_own + [swap(part, 4) for part in attn_own]
     mlp_all = mlp_own + [swap(part, 4) for part in mlp_own]
-    out_mine, out_send = pick_out_call(row_offsets, attn_own)
+    out_mine, out_send = pick_out_call(row_offsets, out_all)
     out_got = swap(out_send, 2)
     out_far = swap(jnp.stack([pick(out_mine, 1 - c), pick(out_got, 1 - c)]), 1)
     out_own = join_out_call(row_offsets, out_mine, out_got, out_far)
@@ -1334,8 +1334,9 @@
             vecs, partial, seq, prev, tail,
         )
 
-    def reduce_z(blocks):
+    def reduce_z(blocks, place=lambda at: at):
         def total(at):
+            at = place(at)
             value = pick(blocks[0], at).astype(f32)
             for block in blocks[1:]:
                 value = value + pick(block, at).astype(f32)
@@ -1350,12 +1351,14 @@
 
     half = jnp.reshape(y, (1,)).astype(jnp.int32)
 
-    def scatter(seq, send, keep, done):
+    def scatter(send, keep):
         got = swap(send, 1)
         side = swap((keep[2:].astype(f32) + got[2:].astype(f32)).astype(bf16), 2)
-        mine = (keep[0].astype(f32) + got[0].astype(f32) + side[0].astype(f32)).astype(bf16)
-        far = (keep[1].astype(f32) + got[1].astype(f32) + side[1].astype(f32)).astype(bf16)
-        return finish_call(half, seq, inputs, cotangent, mine, swap(far, 4), vecs, done)
+        far = (keep[1:2].astype(f32) + got[1:2].astype(f32) + side[1:2].astype(f32)).astype(bf16)
+        return keep, got, side, swap(far, 4)
+
+    def finish(seqs, terms, done):
+        return finish_call(half, seqs, inputs, cotangent, terms, vecs, done)
 
     first_send, first_keep, g_q, g_o, vec, first_norm = attention(0, None, None)
     prev = (g_q, g_o, vec)
@@ -1363,25 +1366,30 @@
         row_offsets, parts, mlp_all, vecs, cotangent, first_send, first_keep, first_norm
     )
     g_got = swap(g_send, 4)
-    done = scatter(0, send, keep, None)
+    terms = [scatter(send, keep)]
     send, keep, g_q, g_o, vec = attention(1, (rest_part, rest_norm), prev)
-    done = scatter(1, send, keep, done)
+    terms.append(scatter(send, keep))
     mlp_grad = reduce_z((g_keep, g_got))
     grad_w_mlp = mlp_grad[96:192]
     grad_b_in = mlp_grad[192, :96]
-    grad_w_in = spread_in_call(exchange_four(mlp_grad[:96].astype(bf16).reshape(4, 24, 768), x, c))
+    in_pair = exchange_four(mlp_grad[:96].astype(bf16).reshape(4, 24, 768), x, c)
     send, keep, q_send, q_keep, o_send, o_keep = attention(
         2, (rest_part, rest_norm), (g_q, g_o, vec), (mlp_vec, at_rows, at_cols)
     )
-    done = scatter(2, send, keep, done)
+    terms.append(scatter(send, keep))
+    done = None
+    for seq in range(3):
+        done = finish((seq,), terms[seq : seq + 1], done)
     q_grad = reduce_z((q_keep, swap(q_send, 4)))
-    spread = spread_q_call(exchange_four(q_grad.astype(bf16).reshape(4, 24, 640), x, c))
-    grad_w_qkv = spread[0]
-    one_gain, one_bias, two_gain, two_bias, grad_bias, grad_bq = [v.reshape(-1) for v in spread[1:]]
+    q_low = q_grad.astype(bf16).reshape(4, 24, 640)
+    q_pair = exchange_four(q_low, x, c)
+    grad_w_qkv, grad_w_in, *spread = spread_call(row_offsets, q_pair, in_pair)
+    one_gain, one_bias, two_gain, two_bias, grad_bias, grad_bq = [v.reshape(-1) for v in spread]
 
     o_parts = o_keep + swap(o_send, 4).astype(f32)
-    o_blocks = exchange_four(o_parts.astype(bf16).reshape(4, 24, 768), x, c)
-    grad_w_out = reduce_z((o_blocks,))
+    o_low = o_parts.astype(bf16).reshape(4, 24, 768)
+    o_blocks = jnp.concatenate(exchange_four(o_low, x, c))
+    grad_w_out = reduce_z((o_blocks,), lambda at: ((at & 1) ^ c) * 2 + ((at >> 1) ^ x))
 
     outputs, grad_inputs = done
     return (

time: 393 us -> 371 us (0.944)
  waiting for transfers between devices: 163 us -> 137 us
    ppermute x45, waiting for transfers between devices: 125 us -> 85.2 us  [swap(): return lax.ppermute(value, 'ctx', [(i, i ^ bit) for i in range(8)])]
    ppermute x15 -> x18, waiting for transfers between devices: 37.9 us -> 52 us  [shift_z(): return lax.ppermute(value, 'fsdp', [(i, (i + step) % 4) for i in range(4)])]
    ppermute x15 -> x18, starting transfers between devices: 28.8 us -> 24.5 us  [shift_z(): return lax.ppermute(value, 'fsdp', [(i, (i + step) % 4) for i in range(4)])]
    unnamed x83 -> x113, local copies, waits for them, and re-layouts: 5.25 us -> 8.37 us
    pallas_call x5 -> x4, Pallas kernels: 12.4 us -> 12.5 us  [the longest x3 9.82 us: finish_call(): pl.pallas_call(functools.partial(finish_kernel, seqs), grid_spec=pltpu.Pr...]
  transfers between devices with their start and end apart: 60 -> 63, of which waited for: 31 -> 24; matrix products, arithmetic and copies ran while one was open for 6% -> 7% of each run, Pallas kernels for 11% -> 12%
where the time goes in v3:
time: 371 us; the launch traced here: 367 us
  waiting for transfers between devices  137 us (37%)
  Pallas kernels  128 us (35%)
  starting transfers between devices  65.6 us (18%)
  other arithmetic  18.2 us (5%)
  local copies, waits for them, and re-layouts  16.3 us (4%)
    ppermute x45, waiting for transfers between devices, swap(): return lax.ppermute(value, 'ctx', [(i, i ^ bit) for i in range(8)])  85.2 us
    pallas_call x3, Pallas kernels, attn_call(): pl.pallas_call(functools.partial(attn_kernel, has_prev, last, seq, inside...  64.5 us
    ppermute x18, waiting for transfers between devices, shift_z(): return lax.ppermute(value, 'fsdp', [(i, (i + step) % 4) for i in range(4)])  52 us
    ppermute x45, starting transfers between devices, swap(): return lax.ppermute(value, 'ctx', [(i, i ^ bit) for i in range(8)])  41 us
    pallas_call x1, Pallas kernels, mlp_call(): pl.pallas_call(functools.partial(mlp_kernel, chunks), grid_spec=pltpu.Pre...  36.6 us
    ppermute x18, starting transfers between devices, shift_z(): return lax.ppermute(value, 'fsdp', [(i, (i + step) % 4) for i in range(4)])  24.5 us
    pallas_call x3, Pallas kernels, finish_call(): pl.pallas_call(functools.partial(finish_kernel, seqs), grid_spec=pltpu.Pr...  9.82 us
    unnamed x113, local copies, waits for them, and re-layouts  8.37 us
  transfers between devices with their start and end apart: 63, of which 24 were waited for; matrix products, arithmetic and copies ran while one was open for 7% of the time, Pallas kernels for 12%

profile of v3, /device:TPU:0, one launch (start us, length us, event | category | flops | bytes accessed | tf_op | source)
XLA Modules:
  0.0 366.6 jit_solution(5325397519861791797)
XLA Ops:
  36.0 3.4 collective-permute-done.21.refs_17_
  42.5 5.3 %collective-permute-done.10.refs_2_.refs_10_ = bf16[96,640]{1,0:T(8,128)(2,1)S(1)} collective-permute-done((bf16[96,640]{1,0:T(8,128)(2,1)S(1)}, bf16[96,640]{1,0:T(8,128)(2,1)S(1)}, u32[]{:S(2)}, u32[]{:S(2)}) %collective-permute-start.10) | collective-permute-done | bytes 122912 | tf_op jit(solution)/shard_map/ppermute | solution.py:394
  49.8 19.2 %collective-permute-done.12.refs_4_.refs_12_ = bf16[96,640]{1,0:T(8,128)(2,1)S(1)} collective-permute-done((bf16[96,640]{1,0:T(8,128)(2,1)S(1)}, bf16[96,640]{1,0:T(8,128)(2,1)S(1)}, u32[]{:S(2)}, u32[]{:S(2)}) %collective-permute-start.12) | collective-permute-done | bytes 122912 | tf_op jit(solution)/shard_map/ppermute | solution.py:390
  75.3 3.2 collective-permute-start.30
  83.7 7.2 %collective-permute-done.30.refs_18_ = bf16[192,768]{1,0:T(8,128)(2,1)S(1)} collective-permute-done((bf16[192,768]{1,0:T(8,128)(2,1)S(1)}, bf16[192,768]{1,0:T(8,128)(2,1)S(1)}, u32[]{:S(2)}, u32[]{:S(2)}) %collective-permute-start.30) | collective-permute-done | bytes 294944 | tf_op jit(solution)/shard_map/ppermute | solution.py:394
  97.5 4.5 %vectors.1.refs_18_.refs_24_.refs_4_ = f32[8,768]{1,0:T(8,128)} custom-call(s32[29]{0:T(128)} %concatenate.9.at_ref.row_ref, bf16[96,640]{1,0:T(8,128)(2,1)} %get-tuple-element.60.refs_0_.refs_8_, bf16[96,640]{1,0:T(8,128)(2,1)} %copy-done.17, bf16[96,640]{1,0:T(8,128)(2,1)} %copy-done.18, bf16[96,640]{1,0:T(8,128)(2,1)} %copy-done.19, ...), custom_call_target="tpu_custom_call" | custom-call | tf_op jit(solution)/shard_map/vectors/pallas_call | solution.py:1192
  102.0 9.4 %collective-permute-done.1.refs_10_.refs_2_ = bf16[2,2,128,768]{3,2,1,0:T(8,128)(2,1)} collective-permute-done((bf16[2,2,128,768]{3,2,1,0:T(8,128)(2,1)S(1)}, bf16[2,2,128,768]{3,2,1,0:T(8,128)(2,1)}, u32[]{:S(2)}, u32[]{:S(2)}) %collective-permute-start.1) | collective-permute-done | bytes 786464 | tf_op jit(solution)/shard_map/ppermute | solution.py:390
  114.0 13.2 %collective-permute-done.2.refs_11_.refs_3_ = bf16[2,2,128,768]{3,2,1,0:T(8,128)(2,1)S(1)} collective-permute-done((bf16[2,2,128,768]{3,2,1,0:T(8,128)(2,1)}, bf16[2,2,128,768]{3,2,1,0:T(8,128)(2,1)S(1)}, u32[]{:S(2)}, u32[]{:S(2)}) %collective-permute-start.2) | collective-permute-done | bytes 786464 | tf_op jit(solution)/shard_map/ppermute | solution.py:390
  127.1 20.2 %attn.3 = (bf16[4,2,128,768]{3,2,1,0:T(8,128)(2,1)}, bf16[4,2,128,768]{3,2,1,0:T(8,128)(2,1)}, f32[768,640]{1,0:T(8,128)}, f32[192,768]{1,0:T(8,128)}, f32[8,768]{1,0:T(8,128)}, /*index=5*/f32[1024,768]{1,0:T(8,128)}) custom-call(s32[29]{0:T(128)} %concatenate.9.at_ref.row_ref, bf16[2,1,128,768]{3,2,1,0:T(8,128)(2,1)} %copy-done.12, ...), custom_call_target="tpu_custom_call" | custom-call | flops 24000000000 | bytes 15000000 | tf_op jit(solution)/shard_map/attn/pallas_call | solution.py:959
  148.9 36.6 %mlp.1 = (bf16[4,2,128,768]{3,2,1,0:T(8,128)(2,1)}, bf16[4,2,128,768]{3,2,1,0:T(8,128)(2,1)}, bf16[2,8,2,128,768]{4,3,2,1,0:T(8,128)(2,1)}, f32[2,1024,768]{2,1,...) custom-call(s32[29]{0:T(128)} %concatenate.9.at_ref.row_ref, ...), custom_call_target="tpu_custom_call" | custom-call | flops 30000001024 | bytes 30000000 | tf_op jit(solution)/shard_map/mlp/pallas_call | solution.py:575
  185.6 21.2 %attn.4 = (bf16[4,2,128,768]{3,2,1,0:T(8,128)(2,1)}, bf16[4,2,128,768]{3,2,1,0:T(8,128)(2,1)}, f32[768,640]{1,0:T(8,128)}, f32[192,768]{1,0:T(8,128)}, f32[8,768]{1,0:T(8,128)}) custom-call(s32[29]{0:T(128)} %concatenate.9.at_ref.row_ref, bf16[2,2,128,768]{3,2,1,0:T(8,128)(2,1)} %copy-done.8, bf16[2,2,128,768]{3,2,1,0:T(8,128)(2,1)} %collective-permute-done.refs_9_.refs_1_, ...), custom_call_target="tpu_custom_call" | custom-call | flops 24000000000 | bytes 15000000 | tf_op jit(solution)/shard_map/attn/pallas_call | solution.py:959
  206.8 23.1 %attn.5 = (bf16[4,2,128,768]{3,2,1,0:T(8,128)(2,1)}, bf16[4,2,128,768]{3,2,1,0:T(8,128)(2,1)}, bf16[4,96,640]{2,1,0:T(8,128)(2,1)}, f32[4,96,640]{2,1,0:T(8,128)...) custom-call(s32[29]{0:T(128)} %concatenate.9.at_ref.row_ref, bf16[2,2,128,768]{3,2,1,0:T(8,128)(2,1)} %copy-done.8, ...), custom_call_target="tpu_custom_call" | custom-call | flops 24000000000 | bytes 15000000 | tf_op jit(solution)/shard_map/attn/pallas_call | solution.py:959
  232.0 4.9 %collective-permute-done.57 = bf16[96,768]{1,0:T(8,128)(2,1)S(1)} collective-permute-done((bf16[96,768]{1,0:T(8,128)(2,1)}, bf16[96,768]{1,0:T(8,128)(2,1)S(1)}, u32[]{:S(2)}, u32[]{:S(2)}) %collective-permute-start.57) | collective-permute-done | bytes 147488 | tf_op jit(solution)/shard_map/ppermute | solution.py:390
  249.9 4.8 %collective-permute-done.60 = bf16[24,768]{1,0:T(8,128)(2,1)S(1)} collective-permute-done((bf16[24,768]{1,0:T(8,128)(2,1)S(1)}, bf16[24,768]{1,0:T(8,128)(2,1)S(1)}, u32[]{:S(2)}, u32[]{:S(2)}) %collective-permute-start.60) | collective-permute-done | bytes 36896 | tf_op jit(solution)/shard_map/ppermute | solution.py:394
  254.9 4.9 %collective-permute-done.61 = bf16[24,768]{1,0:T(8,128)(2,1)} collective-permute-done((bf16[24,768]{1,0:T(8,128)(2,1)}, bf16[24,768]{1,0:T(8,128)(2,1)}, u32[]{:S(2)}, u32[]{:S(2)}) %collective-permute-start.61) | collective-permute-done | bytes 36896 | tf_op jit(solution)/shard_map/ppermute | solution.py:394
  264.0 7.2 %collective-permute-done.46 = bf16[96,640]{1,0:T(8,128)(2,1)} collective-permute-done((bf16[96,640]{1,0:T(8,128)(2,1)S(1)}, bf16[96,640]{1,0:T(8,128)(2,1)}, u32[]{:S(2)}, u32[]{:S(2)}) %collective-permute-start.46) | collective-permute-done | bytes 122912 | tf_op jit(solution)/shard_map/ppermute | solution.py:394
  271.2 7.0 %collective-permute-done.47 = bf16[96,640]{1,0:T(8,128)(2,1)} collective-permute-done((bf16[96,640]{1,0:T(8,128)(2,1)}, bf16[96,640]{1,0:T(8,128)(2,1)}, u32[]{:S(2)}, u32[]{:S(2)}) %collective-permute-start.47) | collective-permute-done | bytes 122912 | tf_op jit(solution)/shard_map/ppermute | solution.py:394
  286.4 4.4 %collective-permute-start.53 = (bf16[208,768]{1,0:T(8,128)(2,1)S(1)}, bf16[208,768]{1,0:T(8,128)(2,1)S(1)}, u32[]{:S(2)}, u32[]{:S(2)}) collective-permute-start(bf16[208,768]{1,0:T(8,128)(2,1)S(1)} %get-tuple-element.106), channel_id=1, source_target_pairs={{0,16},{8,24},{16,0},{24,8},{1,17},{9,25},{17,1},{25,9},{2,18},{10... | collective-permute-start | bytes 958472 | tf_op jit(solution)/shard_map/ppermute | solution.py:394
  300.3 9.9 %collective-permute-done.53 = bf16[208,768]{1,0:T(8,128)(2,1)S(1)} collective-permute-done((bf16[208,768]{1,0:T(8,128)(2,1)S(1)}, bf16[208,768]{1,0:T(8,128)(2,1)S(1)}, u32[]{:S(2)}, u32[]{:S(2)}) %collective-permute-start.53) | collective-permute-done | bytes 319520 | tf_op jit(solution)/shard_map/ppermute | solution.py:394
  315.5 12.9 %collective-permute-done.40.refs_2_ = bf16[2,2,128,768]{3,2,1,0:T(8,128)(2,1)S(1)} collective-permute-done((bf16[2,2,128,768]{3,2,1,0:T(8,128)(2,1)S(1)}, bf16[2,2,128,768]{3,2,1,0:T(8,128)(2,1)S(1)}, u32[]{:S(2)}, u32[]{:S(2)}) %collective-permute-start.40) | collective-permute-done | bytes 786464 | tf_op jit(solution)/shard_map/ppermute | solution.py:390
  331.5 12.7 %collective-permute-done.37.refs_2_ = bf16[2,2,128,768]{3,2,1,0:T(8,128)(2,1)S(1)} collective-permute-done((bf16[2,2,128,768]{3,2,1,0:T(8,128)(2,1)S(1)}, bf16[2,2,128,768]{3,2,1,0:T(8,128)(2,1)S(1)}, u32[]{:S(2)}, u32[]{:S(2)}) %collective-permute-start.37) | collective-permute-done | bytes 786464 | tf_op jit(solution)/shard_map/ppermute | solution.py:390
  354.5 3.3 finish.3
  358.5 3.3 finish.4
  362.6 3.3 finish.5
  (270 shorter events, 120.0 us)
Async XLA Ops:
  2.1 68.5 %collective-permute-start.23 = (bf16[2,1,128,768]{3,2,1,0:T(8,128)(2,1)S(1)}, bf16[2,1,128,768]{3,2,1,0:T(8,128)(2,1)S(1)}, u32[]{:S(2)}, u32[]{:S(2)}) collective-permute-start(bf16[2,1,128,768]{3,2,1,0:T(8,128)(2,1)S(1)} %pad_maximum_fusion.2.refs_0_), channel_id=1, source_target_pairs={{0,2},{1,3},{2,0},{3,1},{4,6},{5,7},{6,4},{7,5},{8,10},{9,11},{10,... | collective-permute-start | bytes 1179656 | tf_op jit(solution)/shard_map/ppermute | solution.py:390
  5.2 66.0 %collective-permute-start.25 = (bf16[2,1,128,768]{3,2,1,0:T(8,128)(2,1)S(1)}, bf16[2,1,128,768]{3,2,1,0:T(8,128)(2,1)}, u32[]{:S(2)}, u32[]{:S(2)}) collective-permute-start(bf16[2,1,128,768]{3,2,1,0:T(8,128)(2,1)S(1)} %pad_maximum_fusion.2.refs_0_), channel_id=1, source_target_pairs={{0,1},{1,0},{2,3},{3,2},{4,5},{5,4},{6,7},{7,6},{8,9},{9,8},{10,11... | collective-permute-start | bytes 1179656 | tf_op jit(solution)/shard_map/ppermute | solution.py:390
  25.1 43.9 %collective-permute-start.22 = (bf16[2,1,128,768]{3,2,1,0:T(8,128)(2,1)S(1)}, bf16[2,1,128,768]{3,2,1,0:T(8,128)(2,1)}, u32[]{:S(2)}, u32[]{:S(2)}) collective-permute-start(bf16[2,1,128,768]{3,2,1,0:T(8,128)(2,1)S(1)} %pad_maximum_fusion.3), channel_id=1, source_target_pairs={{0,4},{1,5},{2,6},{3,7},{4,0},{5,1},{6,2},{7,3},{8,12},{9,13},{10,... | collective-permute-start | bytes 1179656 | tf_op jit(solution)/shard_map/ppermute | solution.py:390
  47.8 45.1 %collective-permute-start = (bf16[2,2,128,768]{3,2,1,0:T(8,128)(2,1)S(1)}, bf16[2,2,128,768]{3,2,1,0:T(8,128)(2,1)}, u32[]{:S(2)}, u32[]{:S(2)}) collective-permute-start(bf16[2,2,128,768]{3,2,1,0:T(8,128)(2,1)S(1)} %pad_maximum_fusion.1), channel_id=1, source_target_pairs={{0,4},{1,5},{2,6},{3,7},{4,0},{5,1},{6,2},{7,3},{8,12},{9,13},{10,... | collective-permute-start | bytes 2359304 | tf_op jit(solution)/shard_map/ppermute | solution.py:390
  92.4 20.5 %collective-permute-start.3 = (bf16[2,2,128,768]{3,2,1,0:T(8,128)(2,1)S(1)}, bf16[2,2,128,768]{3,2,1,0:T(8,128)(2,1)}, u32[]{:S(2)}, u32[]{:S(2)}) collective-permute-start(bf16[2,2,128,768]{3,2,1,0:T(8,128)(2,1)S(1)} %pad_maximum_fusion.refs_8_.refs_0_), channel_id=1, source_target_pairs={{0,1},{1,0},{2,3},{3,2},{4,5},{5,4},{6,7},{7,6},{8,9},{9,8},{10,11... | collective-permute-start | bytes 2359304 | tf_op jit(solution)/shard_map/ppermute | solution.py:390
  92.9 34.2 %collective-permute-start.2 = (bf16[2,2,128,768]{3,2,1,0:T(8,128)(2,1)}, bf16[2,2,128,768]{3,2,1,0:T(8,128)(2,1)S(1)}, u32[]{:S(2)}, u32[]{:S(2)}) collective-permute-start(bf16[2,2,128,768]{3,2,1,0:T(8,128)(2,1)} %collective-permute-done.refs_9_.refs_1_), channel_id=1, source_target_pairs={{0,2},{1,3},{2,0},{3,1},{4,6},{5,7},{6,4},{7,5},{8,10},{9,11},{10,... | collective-permute-start | bytes 2359304 | tf_op jit(solution)/shard_map/ppermute | solution.py:390
  111.4 36.0 %collective-permute-start.34 = (bf16[192,768]{1,0:T(8,128)(2,1)}, bf16[192,768]{1,0:T(8,128)(2,1)S(1)}, u32[]{:S(2)}, u32[]{:S(2)}) collective-permute-start(bf16[192,768]{1,0:T(8,128)(2,1)} %copy-done.49), channel_id=1, source_target_pairs={{0,4},{1,5},{2,6},{3,7},{4,0},{5,1},{6,2},{7,3},{8,12},{9,13},{10,... | collective-permute-start | bytes 884744 | tf_op jit(solution)/shard_map/ppermute | solution.py:390
  112.9 34.4 %collective-permute-start.35 = (bf16[192,768]{1,0:T(8,128)(2,1)}, bf16[192,768]{1,0:T(8,128)(2,1)S(1)}, u32[]{:S(2)}, u32[]{:S(2)}) collective-permute-start(bf16[192,768]{1,0:T(8,128)(2,1)} %copy-done.50), channel_id=1, source_target_pairs={{0,4},{1,5},{2,6},{3,7},{4,0},{5,1},{6,2},{7,3},{8,12},{9,13},{10,... | collective-permute-start | bytes 884744 | tf_op jit(solution)/shard_map/ppermute | solution.py:390
  113.5 34.0 %collective-permute-start.4 = (bf16[2,2,128,768]{3,2,1,0:T(8,128)(2,1)}, bf16[2,2,128,768]{3,2,1,0:T(8,128)(2,1)S(1)}, u32[]{:S(2)}, u32[]{:S(2)}) collective-permute-start(bf16[2,2,128,768]{3,2,1,0:T(8,128)(2,1)} %collective-permute-done.refs_9_.refs_1_), channel_id=1, source_target_pairs={{0,1},{1,0},{2,3},{3,2},{4,5},{5,4},{6,7},{7,6},{8,9},{9,8},{10,11... | collective-permute-start | bytes 2359304 | tf_op jit(solution)/shard_map/ppermute | solution.py:390
  113.5 34.0 %collective-permute-start.5 = (bf16[2,2,128,768]{3,2,1,0:T(8,128)(2,1)}, bf16[2,2,128,768]{3,2,1,0:T(8,128)(2,1)S(1)}, u32[]{:S(2)}, u32[]{:S(2)}) collective-permute-start(bf16[2,2,128,768]{3,2,1,0:T(8,128)(2,1)} %collective-permute-done.1.refs_10_.refs_2_), channel_id=1, source_target_pairs={{0,1},{1,0},{2,3},{3,2},{4,5},{5,4},{6,7},{7,6},{8,9},{9,8},{10,11... | collective-permute-start | bytes 2359304 | tf_op jit(solution)/shard_map/ppermute | solution.py:390
  231.5 28.3 %collective-permute-start.45 = (bf16[4,96,640]{2,1,0:T(8,128)(2,1)}, bf16[4,96,640]{2,1,0:T(8,128)(2,1)S(1)}, u32[]{:S(2)}, u32[]{:S(2)}) collective-permute-start(bf16[4,96,640]{2,1,0:T(8,128)(2,1)} %get-tuple-element.89), channel_id=1, source_target_pairs={{0,4},{1,5},{2,6},{3,7},{4,0},{5,1},{6,2},{7,3},{8,12},{9,13},{10,... | collective-permute-start | bytes 1474568 | tf_op jit(solution)/shard_map/ppermute | solution.py:390
  232.0 58.8 %collective-permute-start.42 = (bf16[4,2,128,768]{3,2,1,0:T(8,128)(2,1)}, bf16[4,2,128,768]{3,2,1,0:T(8,128)(2,1)S(1)}, u32[]{:S(2)}, u32[]{:S(2)}) collective-permute-start(bf16[4,2,128,768]{3,2,1,0:T(8,128)(2,1)} %get-tuple-element.81), channel_id=1, source_target_pairs={{0,1},{1,0},{2,3},{3,2},{4,5},{5,4},{6,7},{7,6},{8,9},{9,8},{10,11... | collective-permute-start | bytes 4718600 | tf_op jit(solution)/shard_map/ppermute | solution.py:390
  240.0 44.4 %collective-permute-start.51 = (bf16[4,208,768]{2,1,0:T(8,128)(2,1)}, bf16[4,208,768]{2,1,0:T(8,128)(2,1)S(1)}, u32[]{:S(2)}, u32[]{:S(2)}) collective-permute-start(bf16[4,208,768]{2,1,0:T(8,128)(2,1)} %get-tuple-element.91), channel_id=1, source_target_pairs={{0,4},{1,5},{2,6},{3,7},{4,0},{5,1},{6,2},{7,3},{8,12},{9,13},{10,... | collective-permute-start | bytes 3833864 | tf_op jit(solution)/shard_map/ppermute | solution.py:390
  245.2 45.9 %collective-permute-start.39 = (bf16[4,2,128,768]{3,2,1,0:T(8,128)(2,1)}, bf16[4,2,128,768]{3,2,1,0:T(8,128)(2,1)}, u32[]{:S(2)}, u32[]{:S(2)}) collective-permute-start(bf16[4,2,128,768]{3,2,1,0:T(8,128)(2,1)} %get-tuple-element.79), channel_id=1, source_target_pairs={{0,1},{1,0},{2,3},{3,2},{4,5},{5,4},{6,7},{7,6},{8,9},{9,8},{10,11... | collective-permute-start | bytes 4718600 | tf_op jit(solution)/shard_map/ppermute | solution.py:390
  259.8 34.2 %collective-permute-start.36 = (bf16[4,2,128,768]{3,2,1,0:T(8,128)(2,1)}, bf16[4,2,128,768]{3,2,1,0:T(8,128)(2,1)}, u32[]{:S(2)}, u32[]{:S(2)}) collective-permute-start(bf16[4,2,128,768]{3,2,1,0:T(8,128)(2,1)} %get-tuple-element.77), channel_id=1, source_target_pairs={{0,1},{1,0},{2,3},{3,2},{4,5},{5,4},{6,7},{7,6},{8,9},{9,8},{10,11... | collective-permute-start | bytes 4718600 | tf_op jit(solution)/shard_map/ppermute | solution.py:390
  286.4 23.8 %collective-permute-start.53 = (bf16[208,768]{1,0:T(8,128)(2,1)S(1)}, bf16[208,768]{1,0:T(8,128)(2,1)S(1)}, u32[]{:S(2)}, u32[]{:S(2)}) collective-permute-start(bf16[208,768]{1,0:T(8,128)(2,1)S(1)} %get-tuple-element.106), channel_id=1, source_target_pairs={{0,16},{8,24},{16,0},{24,8},{1,17},{9,25},{17,1},{25,9},{2,18},{10... | collective-permute-start | bytes 958472 | tf_op jit(solution)/shard_map/ppermute | solution.py:394
  290.8 20.9 %collective-permute-start.54 = (bf16[208,768]{1,0:T(8,128)(2,1)S(1)}, bf16[208,768]{1,0:T(8,128)(2,1)S(1)}, u32[]{:S(2)}, u32[]{:S(2)}) collective-permute-start(bf16[208,768]{1,0:T(8,128)(2,1)S(1)} %get-tuple-element.105), channel_id=1, source_target_pairs={{0,24},{8,0},{16,8},{24,16},{1,25},{9,1},{17,9},{25,17},{2,26},{10... | collective-permute-start | bytes 958472 | tf_op jit(solution)/shard_map/ppermute | solution.py:394
  291.1 22.5 %collective-permute-start.43 = (bf16[2,2,128,768]{3,2,1,0:T(8,128)(2,1)S(1)}, bf16[2,2,128,768]{3,2,1,0:T(8,128)(2,1)S(1)}, u32[]{:S(2)}, u32[]{:S(2)}) collective-permute-start(bf16[2,2,128,768]{3,2,1,0:T(8,128)(2,1)S(1)} %add_convert_fusion), channel_id=1, source_target_pairs={{0,2},{1,3},{2,0},{3,1},{4,6},{5,7},{6,4},{7,5},{8,10},{9,11},{10,... | collective-permute-start | bytes 2359304 | tf_op jit(solution)/shard_map/ppermute | solution.py:390
  294.0 34.4 %collective-permute-start.40 = (bf16[2,2,128,768]{3,2,1,0:T(8,128)(2,1)S(1)}, bf16[2,2,128,768]{3,2,1,0:T(8,128)(2,1)S(1)}, u32[]{:S(2)}, u32[]{:S(2)}) collective-permute-start(bf16[2,2,128,768]{3,2,1,0:T(8,128)(2,1)S(1)} %add_convert_fusion.1), channel_id=1, source_target_pairs={{0,2},{1,3},{2,0},{3,1},{4,6},{5,7},{6,4},{7,5},{8,10},{9,11},{10,... | collective-permute-start | bytes 2359304 | tf_op jit(solution)/shard_map/ppermute | solution.py:390
  298.7 48.6 %collective-permute-start.49 = (bf16[2,24,640]{2,1,0:T(8,128)(2,1)S(1)}, bf16[2,24,640]{2,1,0:T(8,128)(2,1)S(1)}, u32[]{:S(2)}, u32[]{:S(2)}) collective-permute-start(bf16[2,24,640]{2,1,0:T(8,128)(2,1)S(1)} %get-tuple-element.131), channel_id=1, source_target_pairs={{0,2},{1,3},{2,0},{3,1},{4,6},{5,7},{6,4},{7,5},{8,10},{9,11},{10,... | collective-permute-start | bytes 184328 | tf_op jit(solution)/shard_map/ppermute | solution.py:390
  310.2 34.1 %collective-permute-start.37 = (bf16[2,2,128,768]{3,2,1,0:T(8,128)(2,1)S(1)}, bf16[2,2,128,768]{3,2,1,0:T(8,128)(2,1)S(1)}, u32[]{:S(2)}, u32[]{:S(2)}) collective-permute-start(bf16[2,2,128,768]{3,2,1,0:T(8,128)(2,1)S(1)} %add_convert_fusion.2), channel_id=1, source_target_pairs={{0,2},{1,3},{2,0},{3,1},{4,6},{5,7},{6,4},{7,5},{8,10},{9,11},{10,... | collective-permute-start | bytes 2359304 | tf_op jit(solution)/shard_map/ppermute | solution.py:390
  313.1 35.0 %collective-permute-start.55 = (bf16[2,24,768]{2,1,0:T(8,128)(2,1)S(1)}, bf16[2,24,768]{2,1,0:T(8,128)(2,1)S(1)}, u32[]{:S(2)}, u32[]{:S(2)}) collective-permute-start(bf16[2,24,768]{2,1,0:T(8,128)(2,1)S(1)} %get-tuple-element.127), channel_id=1, source_target_pairs={{0,2},{1,3},{2,0},{3,1},{4,6},{5,7},{6,4},{7,5},{8,10},{9,11},{10,... | collective-permute-start | bytes 221192 | tf_op jit(solution)/shard_map/ppermute | solution.py:390
  313.8 40.0 %collective-permute-start.44 = (bf16[1,2,128,768]{3,2,1,0:T(8,128)(2,1)S(1)}, bf16[1,2,128,768]{3,2,1,0:T(8,128)(2,1)S(1)}, u32[]{:S(2)}, u32[]{:S(2)}) collective-permute-start(bf16[1,2,128,768]{3,2,1,0:T(8,128)(2,1)S(1)} %add_convert_fusion.3), channel_id=1, source_target_pairs={{0,4},{1,5},{2,6},{3,7},{4,0},{5,1},{6,2},{7,3},{8,12},{9,13},{10,... | collective-permute-start | bytes 1179656 | tf_op jit(solution)/shard_map/ppermute | solution.py:390
  329.8 27.9 %collective-permute-start.41 = (bf16[1,2,128,768]{3,2,1,0:T(8,128)(2,1)S(1)}, bf16[1,2,128,768]{3,2,1,0:T(8,128)(2,1)S(1)}, u32[]{:S(2)}, u32[]{:S(2)}) collective-permute-start(bf16[1,2,128,768]{3,2,1,0:T(8,128)(2,1)S(1)} %add_convert_fusion.4), channel_id=1, source_target_pairs={{0,4},{1,5},{2,6},{3,7},{4,0},{5,1},{6,2},{7,3},{8,12},{9,13},{10,... | collective-permute-start | bytes 1179656 | tf_op jit(solution)/shard_map/ppermute | solution.py:390
  (95 other events, 1100.6 us)

commit v4 on v3

--- a/solution.py
+++ b/solution.py
@@ -630,7 +630,7 @@
         partial, norm_ref, pq_ref, po_ref, pv_ref = [refs.pop(0) for _ in range(5)]
     if last:
         mv_ref, at_ref, col_ref = [refs.pop(0) for _ in range(3)]
-        send_ref, keep_ref, qsend_ref, qkeep_ref, osend_ref, okeep_ref = [refs.pop(0) for _ in range(6)]
+        send_ref, keep_ref, qsend_ref, qkeep_ref = [refs.pop(0) for _ in range(4)]
     else:
         send_ref, keep_ref, gq_ref, go_ref, vec_ref = [refs.pop(0) for _ in range(5)]
     if not has_prev:
@@ -884,10 +884,10 @@
             for zz in range(4):
                 at = zz * 2 + (row_ref[24] ^ half)
                 rows = pl.ds(pl.multiple_of(at * 96, 16), 96)
-                target[zz] = gq_s[rows, :].astype(target.dtype)
-        for half, target in ((0, okeep_ref), (1, osend_ref)):
+                target[zz, :, :640] = gq_s[rows, :].astype(target.dtype)
+                target[zz, :, 640:] = jnp.zeros((96, 128), target.dtype)
             rows = pl.ds(pl.multiple_of((row_ref[24] ^ half) * 96, 16), 96)
-            target[...] = go_s[rows, :].astype(target.dtype)
+            target[4] = go_s[rows, :].astype(target.dtype)
     else:
         gq_ref[...] = g_query
         go_ref[...] = g_out
@@ -909,7 +909,7 @@
     half = (4, 2, ROWS, width)
     shapes = [(half, bf16), (half, bf16)]
     if last:
-        shapes += [((4, 96, 640), bf16), ((4, 96, 640), f32), ((96, width), bf16), ((96, width), f32)]
+        shapes += [((5, 96, width), bf16), ((5, 96, width), f32)]
     else:
         shapes += [((width, 640), f32), ((192, width), f32), ((8, width), f32)]
     out_specs = [anywhere] * 2 + [whole(shape) for shape, _ in shapes[2:]]
@@ -1204,22 +1204,20 @@
     )(row_offsets, *pieces, rows, cols)
 
 
-def spread_kernel(at_ref, q_mine, q_far, in_mine, in_far, q_ref, in_ref, *refs):
+def spread_kernel(at_ref, mine, far, q_ref, in_ref, o_ref, *refs):
     f32 = jnp.float32
-    out_refs, (q_four, in_four) = refs[:6], refs[6:]
-    x, c = at_ref[26], at_ref[27]
-    for four, near, far in ((q_four, q_mine, q_far), (in_four, in_mine, in_far)):
-        for side in range(2):
-            four[side] = near[side]
-            four[2 + side] = far[side]
+    out_refs, four = refs[:6], refs[6]
+    x, c, z = at_ref[26], at_ref[27], at_ref[28]
+    for side in range(2):
+        four[side] = mine[side]
+        four[2 + side] = far[side]
+    o_ref[...] = four[((z & 1) ^ c) * 2 + ((z >> 1) ^ x), :, 1408:].astype(f32)
     total = None
     for h in range(4):
-        near = ((h & 1) ^ c) * 2 + ((h >> 1) ^ x)
-        block = in_four[near].astype(f32)
+        block = four[((h & 1) ^ c) * 2 + ((h >> 1) ^ x)][:, :1408].astype(f32)
         for zy in range(8):
             first = zy * 384 + h * 96
-            in_ref[:, first : first + 96] = block[:, zy * 96 : (zy + 1) * 96]
-        block = q_four[near].astype(f32)
+            in_ref[:, first : first + 96] = block[:, 640 + zy * 96 : 640 + (zy + 1) * 96]
         for head in range(3):
             for kind in range(2):
                 first = kind * 768 + h * 192 + head * 64
@@ -1236,22 +1234,21 @@
     out_refs[5][...] = jnp.concatenate(rows[5:], axis=1)
 
 
-def spread_call(row_offsets, q_pair, in_pair):
+def spread_call(row_offsets, mine, far):
     f32, bf16 = jnp.float32, jnp.bfloat16
-    shapes = [(24, 2304), (24, 3072)] + [(1, 24)] * 5 + [(1, 72)]
-    operands = [*q_pair, *in_pair]
+    shapes = [(24, 2304), (24, 3072), (24, 768)] + [(1, 24)] * 5 + [(1, 72)]
     return pl.pallas_call(
         spread_kernel,
         grid_spec=pltpu.PrefetchScalarGridSpec(
             num_scalar_prefetch=1,
             grid=(1,),
-            in_specs=[whole(a.shape) for a in operands],
+            in_specs=[whole(mine.shape), whole(far.shape)],
             out_specs=[whole(shape) for shape in shapes],
-            scratch_shapes=[pltpu.VMEM((4, 24, 640), bf16), pltpu.VMEM((4, 24, 768), bf16)],
+            scratch_shapes=[pltpu.VMEM((4, 24, 2176), bf16)],
         ),
         out_shape=[jax.ShapeDtypeStruct(shape, f32) for shape in shapes],
         name="spread",
-    )(row_offsets, *operands)
+    )(row_offsets, mine, far)
 
 
 def exchange_four(blocks, x, c):
@@ -1334,20 +1331,33 @@
             vecs, partial, seq, prev, tail,
         )
 
-    def reduce_z(blocks, place=lambda at: at):
+    def reduce_z(blocks, cols):
         def total(at):
-            at = place(at)
-            value = pick(blocks[0], at).astype(f32)
+            value = pick(blocks[0], at)[:, :cols].astype(f32)
             for block in blocks[1:]:
-                value = value + pick(block, at).astype(f32)
+                value = value + pick(block, at)[:, :cols].astype(f32)
             return value
 
         low = [total((z + k) % 4).astype(bf16) for k in (1, 2, 3)]
         sent = [shift_z(part, k + 1) for k, part in enumerate(low)]
-        result = total(z)
-        for part in sent:
-            result = result + part.astype(f32)
-        return result
+
+        def rows_of_sum(first, count):
+            result = total(z)[first : first + count]
+            for part in sent:
+                result = result + part[first : first + count].astype(f32)
+            return result
+
+        return rows_of_sum
+
+    def to_owner_z(value):
+        total = value
+        low = value.astype(bf16)
+        for k in (1, 2, 3):
+            pairs = [
+                (zz * 8 + i, (zz + k) % 4 * 8 + i) for zz in range(4) for i in range(8) if (zz + k) % 4 == i % 4
+            ]
+            total = total + lax.ppermute(low, ("fsdp", "ctx"), pairs).astype(f32)
+        return total
 
     half = jnp.reshape(y, (1,)).astype(jnp.int32)
 
@@ -1369,27 +1379,24 @@
     terms = [scatter(send, keep)]
     send, keep, g_q, g_o, vec = attention(1, (rest_part, rest_norm), prev)
     terms.append(scatter(send, keep))
-    mlp_grad = reduce_z((g_keep, g_got))
-    grad_w_mlp = mlp_grad[96:192]
-    grad_b_in = mlp_grad[192, :96]
-    in_pair = exchange_four(mlp_grad[:96].astype(bf16).reshape(4, 24, 768), x, c)
-    send, keep, q_send, q_keep, o_send, o_keep = attention(
+    mlp_rows = reduce_z((g_keep, g_got), 768)
+    grad_w_mlp = mlp_rows(96, 96)
+    grad_b_in = mlp_rows(192, 1)[0, :96]
+    send, keep, q_send, q_keep = attention(
         2, (rest_part, rest_norm), (g_q, g_o, vec), (mlp_vec, at_rows, at_cols)
     )
     terms.append(scatter(send, keep))
     done = None
     for seq in range(3):
         done = finish((seq,), terms[seq : seq + 1], done)
-    q_grad = reduce_z((q_keep, swap(q_send, 4)))
-    q_low = q_grad.astype(bf16).reshape(4, 24, 640)
-    q_pair = exchange_four(q_low, x, c)
-    grad_w_qkv, grad_w_in, *spread = spread_call(row_offsets, q_pair, in_pair)
+    q_got = swap(q_send, 4)
+    q_rows = reduce_z((q_keep, q_got), 640)
+    o_sum = q_keep[4] + q_got[4].astype(f32)
+    o_grad = to_owner_z(o_sum)
+    low = [part.astype(bf16) for part in (q_rows(0, 96), mlp_rows(0, 96), o_grad)]
+    blocks = jnp.concatenate(low, axis=1).reshape(4, 24, 2176)
+    grad_w_qkv, grad_w_in, grad_w_out, *spread = spread_call(row_offsets, *exchange_four(blocks, x, c))
     one_gain, one_bias, two_gain, two_bias, grad_bias, grad_bq = [v.reshape(-1) for v in spread]
-
-    o_parts = o_keep + swap(o_send, 4).astype(f32)
-    o_low = o_parts.astype(bf16).reshape(4, 24, 768)
-    o_blocks = jnp.concatenate(exchange_four(o_low, x, c))
-    grad_w_out = reduce_z((o_blocks,), lambda at: ((at & 1) ^ c) * 2 + ((at >> 1) ^ x))
 
     outputs, grad_inputs = done
     return (

time: 371 us -> 375 us (1.011)
  waiting for transfers between devices: 137 us -> 146 us
  other arithmetic: 18.2 us -> 14.4 us
    ppermute x18 -> x15, waiting for transfers between devices: 52 us -> 31 us  [shift_z(): return lax.ppermute(value, 'fsdp', [(i, (i + step) % 4) for i in range(4)])]
    ppermute x45 -> x40, waiting for transfers between devices: 85.2 us -> 102 us  [swap(): return lax.ppermute(value, 'ctx', [(i, i ^ bit) for i in range(8)])]
    ppermute x0 -> x3, waiting for transfers between devices: none -> 13.2 us  [to_owner_z(): total = total + lax.ppermute(low, ('fsdp', 'ctx'), pairs).astype(f32)]
    ppermute x45 -> x40, starting transfers between devices: 41 us -> 34.6 us  [swap(): return lax.ppermute(value, 'ctx', [(i, i ^ bit) for i in range(8)])]
    ppermute x0 -> x3, starting transfers between devices: none -> 3.84 us  [to_owner_z(): total = total + lax.ppermute(low, ('fsdp', 'ctx'), pairs).astype(f32)]
    ppermute x18 -> x15, starting transfers between devices: 24.5 us -> 25.7 us  [shift_z(): return lax.ppermute(value, 'fsdp', [(i, (i + step) % 4) for i in range(4)])]
    unnamed x113 -> x115, local copies, waits for them, and re-layouts: 8.37 us -> 9.13 us
  transfers between devices with their start and end apart: 63 -> 58, of which waited for: 24 -> 22; matrix products, arithmetic and copies ran while one was open for 7% -> 5% of each run, Pallas kernels for 12% -> 12%
where the time goes in v4:
time: 375 us; the launch traced here: 371 us
  waiting for transfers between devices  146 us (39%)
  Pallas kernels  128 us (34%)
  starting transfers between devices  64.2 us (17%)
  local copies, waits for them, and re-layouts  16.3 us (4%)
  other arithmetic  14.4 us (4%)
    ppermute x40, waiting for transfers between devices, swap(): return lax.ppermute(value, 'ctx', [(i, i ^ bit) for i in range(8)])  102 us
    pallas_call x3, Pallas kernels, attn_call(): pl.pallas_call(functools.partial(attn_kernel, has_prev, last, seq, inside...  64.6 us
    pallas_call x1, Pallas kernels, mlp_call(): pl.pallas_call(functools.partial(mlp_kernel, chunks), grid_spec=pltpu.Pre...  36.6 us
    ppermute x40, starting transfers between devices, swap(): return lax.ppermute(value, 'ctx', [(i, i ^ bit) for i in range(8)])  34.6 us
    ppermute x15, waiting for transfers between devices, shift_z(): return lax.ppermute(value, 'fsdp', [(i, (i + step) % 4) for i in range(4)])  31 us
    ppermute x15, starting transfers between devices, shift_z(): return lax.ppermute(value, 'fsdp', [(i, (i + step) % 4) for i in range(4)])  25.7 us
    ppermute x3, waiting for transfers between devices, to_owner_z(): total = total + lax.ppermute(low, ('fsdp', 'ctx'), pairs).astype(f32)  13.2 us
    pallas_call x3, Pallas kernels, finish_call(): pl.pallas_call(functools.partial(finish_kernel, seqs), grid_spec=pltpu.Pr...  9.82 us
  transfers between devices with their start and end apart: 58, of which 22 were waited for; matrix products, arithmetic and copies ran while one was open for 5% of the time, Pallas kernels for 12%

profile of v4, /device:TPU:0, one launch (start us, length us, event | category | flops | bytes accessed | tf_op | source)
XLA Modules:
  0.0 370.6 jit_solution(537908747714225247)
XLA Ops:
  36.0 3.4 collective-permute-done.21.refs_17_
  42.5 5.3 %collective-permute-done.10.refs_2_.refs_10_ = bf16[96,640]{1,0:T(8,128)(2,1)S(1)} collective-permute-done((bf16[96,640]{1,0:T(8,128)(2,1)S(1)}, bf16[96,640]{1,0:T(8,128)(2,1)S(1)}, u32[]{:S(2)}, u32[]{:S(2)}) %collective-permute-start.10) | collective-permute-done | bytes 122912 | tf_op jit(solution)/shard_map/ppermute | solution.py:394
  49.9 19.2 %collective-permute-done.12.refs_4_.refs_12_ = bf16[96,640]{1,0:T(8,128)(2,1)S(1)} collective-permute-done((bf16[96,640]{1,0:T(8,128)(2,1)S(1)}, bf16[96,640]{1,0:T(8,128)(2,1)S(1)}, u32[]{:S(2)}, u32[]{:S(2)}) %collective-permute-start.12) | collective-permute-done | bytes 122912 | tf_op jit(solution)/shard_map/ppermute | solution.py:390
  83.7 7.2 %collective-permute-done.30.refs_18_ = bf16[192,768]{1,0:T(8,128)(2,1)S(1)} collective-permute-done((bf16[192,768]{1,0:T(8,128)(2,1)S(1)}, bf16[192,768]{1,0:T(8,128)(2,1)S(1)}, u32[]{:S(2)}, u32[]{:S(2)}) %collective-permute-start.30) | collective-permute-done | bytes 294944 | tf_op jit(solution)/shard_map/ppermute | solution.py:394
  97.6 4.5 %vectors.1.refs_18_.refs_24_.refs_4_ = f32[8,768]{1,0:T(8,128)} custom-call(s32[29]{0:T(128)} %concatenate.9.at_ref.row_ref, bf16[96,640]{1,0:T(8,128)(2,1)} %get-tuple-element.59.refs_0_.refs_8_, bf16[96,640]{1,0:T(8,128)(2,1)} %copy-done.22, bf16[96,640]{1,0:T(8,128)(2,1)} %copy-done.23, bf16[96,640]{1,0:T(8,128)(2,1)} %copy-done.24, ...), custom_call_target="tpu_custom_call" | custom-call | tf_op jit(solution)/shard_map/vectors/pallas_call | solution.py:1192
  102.0 9.4 %collective-permute-done.1.refs_10_.refs_2_ = bf16[2,2,128,768]{3,2,1,0:T(8,128)(2,1)} collective-permute-done((bf16[2,2,128,768]{3,2,1,0:T(8,128)(2,1)S(1)}, bf16[2,2,128,768]{3,2,1,0:T(8,128)(2,1)}, u32[]{:S(2)}, u32[]{:S(2)}) %collective-permute-start.1) | collective-permute-done | bytes 786464 | tf_op jit(solution)/shard_map/ppermute | solution.py:390
  114.0 13.2 %collective-permute-done.2.refs_11_.refs_3_ = bf16[2,2,128,768]{3,2,1,0:T(8,128)(2,1)S(1)} collective-permute-done((bf16[2,2,128,768]{3,2,1,0:T(8,128)(2,1)}, bf16[2,2,128,768]{3,2,1,0:T(8,128)(2,1)S(1)}, u32[]{:S(2)}, u32[]{:S(2)}) %collective-permute-start.2) | collective-permute-done | bytes 786464 | tf_op jit(solution)/shard_map/ppermute | solution.py:390
  127.2 20.2 %attn.3 = (bf16[4,2,128,768]{3,2,1,0:T(8,128)(2,1)}, bf16[4,2,128,768]{3,2,1,0:T(8,128)(2,1)}, f32[768,640]{1,0:T(8,128)}, f32[192,768]{1,0:T(8,128)}, f32[8,768]{1,0:T(8,128)}, /*index=5*/f32[1024,768]{1,0:T(8,128)}) custom-call(s32[29]{0:T(128)} %concatenate.9.at_ref.row_ref, bf16[2,1,128,768]{3,2,1,0:T(8,128)(2,1)} %copy-done.12, ...), custom_call_target="tpu_custom_call" | custom-call | flops 24000000000 | bytes 15000000 | tf_op jit(solution)/shard_map/attn/pallas_call | solution.py:959
  149.0 36.6 %mlp.1 = (bf16[4,2,128,768]{3,2,1,0:T(8,128)(2,1)}, bf16[4,2,128,768]{3,2,1,0:T(8,128)(2,1)}, bf16[2,8,2,128,768]{4,3,2,1,0:T(8,128)(2,1)}, f32[2,1024,768]{2,1,...) custom-call(s32[29]{0:T(128)} %concatenate.9.at_ref.row_ref, ...), custom_call_target="tpu_custom_call" | custom-call | flops 30000001024 | bytes 30000000 | tf_op jit(solution)/shard_map/mlp/pallas_call | solution.py:575
  185.6 21.2 %attn.4 = (bf16[4,2,128,768]{3,2,1,0:T(8,128)(2,1)}, bf16[4,2,128,768]{3,2,1,0:T(8,128)(2,1)}, f32[768,640]{1,0:T(8,128)}, f32[192,768]{1,0:T(8,128)}, f32[8,768]{1,0:T(8,128)}) custom-call(s32[29]{0:T(128)} %concatenate.9.at_ref.row_ref, bf16[2,2,128,768]{3,2,1,0:T(8,128)(2,1)} %copy-done.8, bf16[2,2,128,768]{3,2,1,0:T(8,128)(2,1)} %collective-permute-done.refs_9_.refs_1_, ...), custom_call_target="tpu_custom_call" | custom-call | flops 24000000000 | bytes 15000000 | tf_op jit(solution)/shard_map/attn/pallas_call | solution.py:959
  206.8 23.2 %attn.5 = (bf16[4,2,128,768]{3,2,1,0:T(8,128)(2,1)}, bf16[4,2,128,768]{3,2,1,0:T(8,128)(2,1)}, bf16[5,96,768]{2,1,0:T(8,128)(2,1)}, f32[5,96,768]{2,1,0:T(8,128)}) custom-call(s32[29]{0:T(128)} %concatenate.9.at_ref.row_ref, bf16[2,2,128,768]{3,2,1,0:T(8,128)(2,1)} %copy-done.8, bf16[2,2,128,768]{3,2,1,0:T(8,128)(2,1)} %collective-permute-done.refs_9_.refs_1_, ...), custom_call_target="tpu_custom_call" | custom-call | flops 24000000000 | bytes 15000000 | tf_op jit(solution)/shard_map/attn/pallas_call | solution.py:959
  232.6 17.1 %collective-permute-done.45 = bf16[5,96,768]{2,1,0:T(8,128)(2,1)} collective-permute-done((bf16[5,96,768]{2,1,0:T(8,128)(2,1)}, bf16[5,96,768]{2,1,0:T(8,128)(2,1)}, u32[]{:S(2)}, u32[]{:S(2)}) %collective-permute-start.45) | collective-permute-done | bytes 737312 | tf_op jit(solution)/shard_map/ppermute | solution.py:390
  255.1 3.4 collective-permute-start.47
  258.5 3.4 collective-permute-done.46
  268.4 4.2 %collective-permute-done.48 = bf16[96,640]{1,0:T(8,128)(2,1)S(1)} collective-permute-done((bf16[96,640]{1,0:T(8,128)(2,1)S(1)}, bf16[96,640]{1,0:T(8,128)(2,1)S(1)}, u32[]{:S(2)}, u32[]{:S(2)}) %collective-permute-start.48) | collective-permute-done | bytes 122912 | tf_op jit(solution)/shard_map/ppermute | solution.py:394
  274.6 6.0 %collective-permute-done.54 = bf16[96,768]{1,0:T(8,128)(2,1)} collective-permute-done((bf16[96,768]{1,0:T(8,128)(2,1)S(1)}, bf16[96,768]{1,0:T(8,128)(2,1)}, u32[]{:S(2)}, u32[]{:S(2)}) %collective-permute-start.54) | collective-permute-done | bytes 147488 | tf_op jit(solution)/shard_map/ppermute | solution.py:1359
  283.0 7.2 %collective-permute-done.55 = bf16[96,768]{1,0:T(8,128)(2,1)S(1)} collective-permute-done((bf16[96,768]{1,0:T(8,128)(2,1)S(1)}, bf16[96,768]{1,0:T(8,128)(2,1)S(1)}, u32[]{:S(2)}, u32[]{:S(2)}) %collective-permute-start.55) | collective-permute-done | bytes 147488 | tf_op jit(solution)/shard_map/ppermute | solution.py:1359
  293.8 3.8 %collective-permute-start.52 = (bf16[208,768]{1,0:T(8,128)(2,1)S(1)}, bf16[208,768]{1,0:T(8,128)(2,1)S(1)}, u32[]{:S(2)}, u32[]{:S(2)}) collective-permute-start(bf16[208,768]{1,0:T(8,128)(2,1)S(1)} %get-tuple-element.103), channel_id=1, source_target_pairs={{0,24},{8,0},{16,8},{24,16},{1,25},{9,1},{17,9},{25,17},{2,26},{10... | collective-permute-start | bytes 958472 | tf_op jit(solution)/shard_map/ppermute | solution.py:394
  302.8 7.6 %collective-permute-done.51 = bf16[208,768]{1,0:T(8,128)(2,1)S(1)} collective-permute-done((bf16[208,768]{1,0:T(8,128)(2,1)S(1)}, bf16[208,768]{1,0:T(8,128)(2,1)S(1)}, u32[]{:S(2)}, u32[]{:S(2)}) %collective-permute-start.51) | collective-permute-done | bytes 319520 | tf_op jit(solution)/shard_map/ppermute | solution.py:394
  312.4 5.9 %collective-permute-done.43.refs_2_ = bf16[2,2,128,768]{3,2,1,0:T(8,128)(2,1)S(1)} collective-permute-done((bf16[2,2,128,768]{3,2,1,0:T(8,128)(2,1)S(1)}, bf16[2,2,128,768]{3,2,1,0:T(8,128)(2,1)S(1)}, u32[]{:S(2)}, u32[]{:S(2)}) %collective-permute-start.43) | collective-permute-done | bytes 786464 | tf_op jit(solution)/shard_map/ppermute | solution.py:390
  320.1 15.0 %collective-permute-done.40.refs_2_ = bf16[2,2,128,768]{3,2,1,0:T(8,128)(2,1)S(1)} collective-permute-done((bf16[2,2,128,768]{3,2,1,0:T(8,128)(2,1)S(1)}, bf16[2,2,128,768]{3,2,1,0:T(8,128)(2,1)S(1)}, u32[]{:S(2)}, u32[]{:S(2)}) %collective-permute-start.40) | collective-permute-done | bytes 786464 | tf_op jit(solution)/shard_map/ppermute | solution.py:390
  338.2 10.9 %collective-permute-done.37.refs_2_ = bf16[2,2,128,768]{3,2,1,0:T(8,128)(2,1)S(1)} collective-permute-done((bf16[2,2,128,768]{3,2,1,0:T(8,128)(2,1)S(1)}, bf16[2,2,128,768]{3,2,1,0:T(8,128)(2,1)S(1)}, u32[]{:S(2)}, u32[]{:S(2)}) %collective-permute-start.37) | collective-permute-done | bytes 786464 | tf_op jit(solution)/shard_map/ppermute | solution.py:390
  362.6 3.3 finish.4
  366.6 3.3 finish.5
  (263 shorter events, 114.6 us)
Async XLA Ops:
  2.1 68.5 %collective-permute-start.23 = (bf16[2,1,128,768]{3,2,1,0:T(8,128)(2,1)S(1)}, bf16[2,1,128,768]{3,2,1,0:T(8,128)(2,1)S(1)}, u32[]{:S(2)}, u32[]{:S(2)}) collective-permute-start(bf16[2,1,128,768]{3,2,1,0:T(8,128)(2,1)S(1)} %pad_maximum_fusion.3.refs_0_), channel_id=1, source_target_pairs={{0,2},{1,3},{2,0},{3,1},{4,6},{5,7},{6,4},{7,5},{8,10},{9,11},{10,... | collective-permute-start | bytes 1179656 | tf_op jit(solution)/shard_map/ppermute | solution.py:390
  5.2 66.0 %collective-permute-start.25 = (bf16[2,1,128,768]{3,2,1,0:T(8,128)(2,1)S(1)}, bf16[2,1,128,768]{3,2,1,0:T(8,128)(2,1)}, u32[]{:S(2)}, u32[]{:S(2)}) collective-permute-start(bf16[2,1,128,768]{3,2,1,0:T(8,128)(2,1)S(1)} %pad_maximum_fusion.3.refs_0_), channel_id=1, source_target_pairs={{0,1},{1,0},{2,3},{3,2},{4,5},{5,4},{6,7},{7,6},{8,9},{9,8},{10,11... | collective-permute-start | bytes 1179656 | tf_op jit(solution)/shard_map/ppermute | solution.py:390
  25.1 43.9 %collective-permute-start.22 = (bf16[2,1,128,768]{3,2,1,0:T(8,128)(2,1)S(1)}, bf16[2,1,128,768]{3,2,1,0:T(8,128)(2,1)}, u32[]{:S(2)}, u32[]{:S(2)}) collective-permute-start(bf16[2,1,128,768]{3,2,1,0:T(8,128)(2,1)S(1)} %pad_maximum_fusion.4), channel_id=1, source_target_pairs={{0,4},{1,5},{2,6},{3,7},{4,0},{5,1},{6,2},{7,3},{8,12},{9,13},{10,... | collective-permute-start | bytes 1179656 | tf_op jit(solution)/shard_map/ppermute | solution.py:390
  47.8 45.1 %collective-permute-start = (bf16[2,2,128,768]{3,2,1,0:T(8,128)(2,1)S(1)}, bf16[2,2,128,768]{3,2,1,0:T(8,128)(2,1)}, u32[]{:S(2)}, u32[]{:S(2)}) collective-permute-start(bf16[2,2,128,768]{3,2,1,0:T(8,128)(2,1)S(1)} %pad_maximum_fusion.1), channel_id=1, source_target_pairs={{0,4},{1,5},{2,6},{3,7},{4,0},{5,1},{6,2},{7,3},{8,12},{9,13},{10,... | collective-permute-start | bytes 2359304 | tf_op jit(solution)/shard_map/ppermute | solution.py:390
  49.3 19.7 %collective-permute-start.12 = (bf16[96,640]{1,0:T(8,128)(2,1)S(1)}, bf16[96,640]{1,0:T(8,128)(2,1)S(1)}, u32[]{:S(2)}, u32[]{:S(2)}) collective-permute-start(bf16[96,640]{1,0:T(8,128)(2,1)S(1)} %copy-done.21), channel_id=1, source_target_pairs={{0,4},{1,5},{2,6},{3,7},{4,0},{5,1},{6,2},{7,3},{8,12},{9,13},{10,... | collective-permute-start | bytes 368648 | tf_op jit(solution)/shard_map/ppermute | solution.py:390
  90.9 20.5 %collective-permute-start.1 = (bf16[2,2,128,768]{3,2,1,0:T(8,128)(2,1)S(1)}, bf16[2,2,128,768]{3,2,1,0:T(8,128)(2,1)}, u32[]{:S(2)}, u32[]{:S(2)}) collective-permute-start(bf16[2,2,128,768]{3,2,1,0:T(8,128)(2,1)S(1)} %pad_maximum_fusion.refs_8_.refs_0_), channel_id=1, source_target_pairs={{0,2},{1,3},{2,0},{3,1},{4,6},{5,7},{6,4},{7,5},{8,10},{9,11},{10,... | collective-permute-start | bytes 2359304 | tf_op jit(solution)/shard_map/ppermute | solution.py:390
  92.4 20.6 %collective-permute-start.3 = (bf16[2,2,128,768]{3,2,1,0:T(8,128)(2,1)S(1)}, bf16[2,2,128,768]{3,2,1,0:T(8,128)(2,1)}, u32[]{:S(2)}, u32[]{:S(2)}) collective-permute-start(bf16[2,2,128,768]{3,2,1,0:T(8,128)(2,1)S(1)} %pad_maximum_fusion.refs_8_.refs_0_), channel_id=1, source_target_pairs={{0,1},{1,0},{2,3},{3,2},{4,5},{5,4},{6,7},{7,6},{8,9},{9,8},{10,11... | collective-permute-start | bytes 2359304 | tf_op jit(solution)/shard_map/ppermute | solution.py:390
  92.9 34.2 %collective-permute-start.2 = (bf16[2,2,128,768]{3,2,1,0:T(8,128)(2,1)}, bf16[2,2,128,768]{3,2,1,0:T(8,128)(2,1)S(1)}, u32[]{:S(2)}, u32[]{:S(2)}) collective-permute-start(bf16[2,2,128,768]{3,2,1,0:T(8,128)(2,1)} %collective-permute-done.refs_9_.refs_1_), channel_id=1, source_target_pairs={{0,2},{1,3},{2,0},{3,1},{4,6},{5,7},{6,4},{7,5},{8,10},{9,11},{10,... | collective-permute-start | bytes 2359304 | tf_op jit(solution)/shard_map/ppermute | solution.py:390
  111.4 35.9 %collective-permute-start.34 = (bf16[192,768]{1,0:T(8,128)(2,1)}, bf16[192,768]{1,0:T(8,128)(2,1)S(1)}, u32[]{:S(2)}, u32[]{:S(2)}) collective-permute-start(bf16[192,768]{1,0:T(8,128)(2,1)} %copy-done.50), channel_id=1, source_target_pairs={{0,4},{1,5},{2,6},{3,7},{4,0},{5,1},{6,2},{7,3},{8,12},{9,13},{10,... | collective-permute-start | bytes 884744 | tf_op jit(solution)/shard_map/ppermute | solution.py:390
  113.0 34.4 %collective-permute-start.35 = (bf16[192,768]{1,0:T(8,128)(2,1)}, bf16[192,768]{1,0:T(8,128)(2,1)S(1)}, u32[]{:S(2)}, u32[]{:S(2)}) collective-permute-start(bf16[192,768]{1,0:T(8,128)(2,1)} %copy-done.51), channel_id=1, source_target_pairs={{0,4},{1,5},{2,6},{3,7},{4,0},{5,1},{6,2},{7,3},{8,12},{9,13},{10,... | collective-permute-start | bytes 884744 | tf_op jit(solution)/shard_map/ppermute | solution.py:390
  113.5 34.0 %collective-permute-start.4 = (bf16[2,2,128,768]{3,2,1,0:T(8,128)(2,1)}, bf16[2,2,128,768]{3,2,1,0:T(8,128)(2,1)S(1)}, u32[]{:S(2)}, u32[]{:S(2)}) collective-permute-start(bf16[2,2,128,768]{3,2,1,0:T(8,128)(2,1)} %collective-permute-done.refs_9_.refs_1_), channel_id=1, source_target_pairs={{0,1},{1,0},{2,3},{3,2},{4,5},{5,4},{6,7},{7,6},{8,9},{9,8},{10,11... | collective-permute-start | bytes 2359304 | tf_op jit(solution)/shard_map/ppermute | solution.py:390
  113.5 34.0 %collective-permute-start.5 = (bf16[2,2,128,768]{3,2,1,0:T(8,128)(2,1)}, bf16[2,2,128,768]{3,2,1,0:T(8,128)(2,1)S(1)}, u32[]{:S(2)}, u32[]{:S(2)}) collective-permute-start(bf16[2,2,128,768]{3,2,1,0:T(8,128)(2,1)} %collective-permute-done.1.refs_10_.refs_2_), channel_id=1, source_target_pairs={{0,1},{1,0},{2,3},{3,2},{4,5},{5,4},{6,7},{7,6},{8,9},{9,8},{10,11... | collective-permute-start | bytes 2359304 | tf_op jit(solution)/shard_map/ppermute | solution.py:390
  127.1 20.3 %collective-permute-start.6 = (bf16[2,2,128,768]{3,2,1,0:T(8,128)(2,1)S(1)}, bf16[2,2,128,768]{3,2,1,0:T(8,128)(2,1)S(1)}, u32[]{:S(2)}, u32[]{:S(2)}) collective-permute-start(bf16[2,2,128,768]{3,2,1,0:T(8,128)(2,1)S(1)} %collective-permute-done.2.refs_11_.refs_3_), channel_id=1, source_target_pairs={{0,1},{1,0},{2,3},{3,2},{4,5},{5,4},{6,7},{7,6},{8,9},{9,8},{10,11... | collective-permute-start | bytes 2359304 | tf_op jit(solution)/shard_map/ppermute | solution.py:390
  230.0 19.7 %collective-permute-start.45 = (bf16[5,96,768]{2,1,0:T(8,128)(2,1)}, bf16[5,96,768]{2,1,0:T(8,128)(2,1)}, u32[]{:S(2)}, u32[]{:S(2)}) collective-permute-start(bf16[5,96,768]{2,1,0:T(8,128)(2,1)} %get-tuple-element.88), channel_id=1, source_target_pairs={{0,4},{1,5},{2,6},{3,7},{4,0},{5,1},{6,2},{7,3},{8,12},{9,13},{10,... | collective-permute-start | bytes 2211848 | tf_op jit(solution)/shard_map/ppermute | solution.py:390
  231.6 59.9 %collective-permute-start.49 = (bf16[4,208,768]{2,1,0:T(8,128)(2,1)}, bf16[4,208,768]{2,1,0:T(8,128)(2,1)S(1)}, u32[]{:S(2)}, u32[]{:S(2)}) collective-permute-start(bf16[4,208,768]{2,1,0:T(8,128)(2,1)} %get-tuple-element.90), channel_id=1, source_target_pairs={{0,4},{1,5},{2,6},{3,7},{4,0},{5,1},{6,2},{7,3},{8,12},{9,13},{10,... | collective-permute-start | bytes 3833864 | tf_op jit(solution)/shard_map/ppermute | solution.py:390
  232.1 61.7 %collective-permute-start.42 = (bf16[4,2,128,768]{3,2,1,0:T(8,128)(2,1)}, bf16[4,2,128,768]{3,2,1,0:T(8,128)(2,1)S(1)}, u32[]{:S(2)}, u32[]{:S(2)}) collective-permute-start(bf16[4,2,128,768]{3,2,1,0:T(8,128)(2,1)} %get-tuple-element.80), channel_id=1, source_target_pairs={{0,1},{1,0},{2,3},{3,2},{4,5},{5,4},{6,7},{7,6},{8,9},{9,8},{10,11... | collective-permute-start | bytes 4718600 | tf_op jit(solution)/shard_map/ppermute | solution.py:390
  232.1 65.7 %collective-permute-start.39 = (bf16[4,2,128,768]{3,2,1,0:T(8,128)(2,1)}, bf16[4,2,128,768]{3,2,1,0:T(8,128)(2,1)}, u32[]{:S(2)}, u32[]{:S(2)}) collective-permute-start(bf16[4,2,128,768]{3,2,1,0:T(8,128)(2,1)} %get-tuple-element.78), channel_id=1, source_target_pairs={{0,1},{1,0},{2,3},{3,2},{4,5},{5,4},{6,7},{7,6},{8,9},{9,8},{10,11... | collective-permute-start | bytes 4718600 | tf_op jit(solution)/shard_map/ppermute | solution.py:390
  274.6 24.8 %collective-permute-start.36 = (bf16[4,2,128,768]{3,2,1,0:T(8,128)(2,1)}, bf16[4,2,128,768]{3,2,1,0:T(8,128)(2,1)}, u32[]{:S(2)}, u32[]{:S(2)}) collective-permute-start(bf16[4,2,128,768]{3,2,1,0:T(8,128)(2,1)} %get-tuple-element.76), channel_id=1, source_target_pairs={{0,1},{1,0},{2,3},{3,2},{4,5},{5,4},{6,7},{7,6},{8,9},{9,8},{10,11... | collective-permute-start | bytes 4718600 | tf_op jit(solution)/shard_map/ppermute | solution.py:390
  297.8 20.5 %collective-permute-start.43 = (bf16[2,2,128,768]{3,2,1,0:T(8,128)(2,1)S(1)}, bf16[2,2,128,768]{3,2,1,0:T(8,128)(2,1)S(1)}, u32[]{:S(2)}, u32[]{:S(2)}) collective-permute-start(bf16[2,2,128,768]{3,2,1,0:T(8,128)(2,1)S(1)} %add_convert_fusion), channel_id=1, source_target_pairs={{0,2},{1,3},{2,0},{3,1},{4,6},{5,7},{6,4},{7,5},{8,10},{9,11},{10,... | collective-permute-start | bytes 2359304 | tf_op jit(solution)/shard_map/ppermute | solution.py:390
  299.3 35.8 %collective-permute-start.40 = (bf16[2,2,128,768]{3,2,1,0:T(8,128)(2,1)S(1)}, bf16[2,2,128,768]{3,2,1,0:T(8,128)(2,1)S(1)}, u32[]{:S(2)}, u32[]{:S(2)}) collective-permute-start(bf16[2,2,128,768]{3,2,1,0:T(8,128)(2,1)S(1)} %add_convert_fusion.1), channel_id=1, source_target_pairs={{0,2},{1,3},{2,0},{3,1},{4,6},{5,7},{6,4},{7,5},{8,10},{9,11},{10,... | collective-permute-start | bytes 2359304 | tf_op jit(solution)/shard_map/ppermute | solution.py:390
  302.7 46.4 %collective-permute-start.37 = (bf16[2,2,128,768]{3,2,1,0:T(8,128)(2,1)S(1)}, bf16[2,2,128,768]{3,2,1,0:T(8,128)(2,1)S(1)}, u32[]{:S(2)}, u32[]{:S(2)}) collective-permute-start(bf16[2,2,128,768]{3,2,1,0:T(8,128)(2,1)S(1)} %add_convert_fusion.2), channel_id=1, source_target_pairs={{0,2},{1,3},{2,0},{3,1},{4,6},{5,7},{6,4},{7,5},{8,10},{9,11},{10,... | collective-permute-start | bytes 2359304 | tf_op jit(solution)/shard_map/ppermute | solution.py:390
  311.3 40.8 %collective-permute-start.56 = (bf16[2,24,2176]{2,1,0:T(8,128)(2,1)S(1)}, bf16[2,24,2176]{2,1,0:T(8,128)(2,1)S(1)}, u32[]{:S(2)}, u32[]{:S(2)}) collective-permute-start(bf16[2,24,2176]{2,1,0:T(8,128)(2,1)S(1)} %get-tuple-element.127), channel_id=1, source_target_pairs={{0,2},{1,3},{2,0},{3,1},{4,6},{5,7},{6,4},{7,5},{8,10},{9,11},{10,... | collective-permute-start | bytes 626696 | tf_op jit(solution)/shard_map/ppermute | solution.py:390
  318.4 39.3 %collective-permute-start.44 = (bf16[1,2,128,768]{3,2,1,0:T(8,128)(2,1)S(1)}, bf16[1,2,128,768]{3,2,1,0:T(8,128)(2,1)S(1)}, u32[]{:S(2)}, u32[]{:S(2)}) collective-permute-start(bf16[1,2,128,768]{3,2,1,0:T(8,128)(2,1)S(1)} %add_convert_fusion.3), channel_id=1, source_target_pairs={{0,4},{1,5},{2,6},{3,7},{4,0},{5,1},{6,2},{7,3},{8,12},{9,13},{10,... | collective-permute-start | bytes 1179656 | tf_op jit(solution)/shard_map/ppermute | solution.py:390
  336.6 25.2 %collective-permute-start.41 = (bf16[1,2,128,768]{3,2,1,0:T(8,128)(2,1)S(1)}, bf16[1,2,128,768]{3,2,1,0:T(8,128)(2,1)S(1)}, u32[]{:S(2)}, u32[]{:S(2)}) collective-permute-start(bf16[1,2,128,768]{3,2,1,0:T(8,128)(2,1)S(1)} %add_convert_fusion.4), channel_id=1, source_target_pairs={{0,4},{1,5},{2,6},{3,7},{4,0},{5,1},{6,2},{7,3},{8,12},{9,13},{10,... | collective-permute-start | bytes 1179656 | tf_op jit(solution)/shard_map/ppermute | solution.py:390
  (91 other events, 1071.6 us)

commit v5 on v4

--- a/solution.py
+++ b/solution.py
@@ -630,7 +630,7 @@
         partial, norm_ref, pq_ref, po_ref, pv_ref = [refs.pop(0) for _ in range(5)]
     if last:
         mv_ref, at_ref, col_ref = [refs.pop(0) for _ in range(3)]
-        send_ref, keep_ref, qsend_ref, qkeep_ref = [refs.pop(0) for _ in range(4)]
+        send_ref, keep_ref, qsend_ref, qkeep_ref, osend_ref, okeep_ref = [refs.pop(0) for _ in range(6)]
     else:
         send_ref, keep_ref, gq_ref, go_ref, vec_ref = [refs.pop(0) for _ in range(5)]
     if not has_prev:
@@ -884,10 +884,10 @@
             for zz in range(4):
                 at = zz * 2 + (row_ref[24] ^ half)
                 rows = pl.ds(pl.multiple_of(at * 96, 16), 96)
-                target[zz, :, :640] = gq_s[rows, :].astype(target.dtype)
-                target[zz, :, 640:] = jnp.zeros((96, 128), target.dtype)
+                target[zz] = gq_s[rows, :].astype(target.dtype)
+        for half, target in ((0, okeep_ref), (1, osend_ref)):
             rows = pl.ds(pl.multiple_of((row_ref[24] ^ half) * 96, 16), 96)
-            target[4] = go_s[rows, :].astype(target.dtype)
+            target[...] = go_s[rows, :].astype(target.dtype)
     else:
         gq_ref[...] = g_query
         go_ref[...] = g_out
@@ -909,7 +909,7 @@
     half = (4, 2, ROWS, width)
     shapes = [(half, bf16), (half, bf16)]
     if last:
-        shapes += [((5, 96, width), bf16), ((5, 96, width), f32)]
+        shapes += [((4, 96, 640), bf16), ((4, 96, 640), f32), ((96, width), bf16), ((96, width), f32)]
     else:
         shapes += [((width, 640), f32), ((192, width), f32), ((8, width), f32)]
     out_specs = [anywhere] * 2 + [whole(shape) for shape, _ in shapes[2:]]
@@ -1382,16 +1382,16 @@
     mlp_rows = reduce_z((g_keep, g_got), 768)
     grad_w_mlp = mlp_rows(96, 96)
     grad_b_in = mlp_rows(192, 1)[0, :96]
-    send, keep, q_send, q_keep = attention(
+    send, keep, q_send, q_keep, o_send, o_keep = attention(
         2, (rest_part, rest_norm), (g_q, g_o, vec), (mlp_vec, at_rows, at_cols)
     )
     terms.append(scatter(send, keep))
     done = None
     for seq in range(3):
         done = finish((seq,), terms[seq : seq + 1], done)
-    q_got = swap(q_send, 4)
+    q_got, o_got = swap(q_send, 4), swap(o_send, 4)
     q_rows = reduce_z((q_keep, q_got), 640)
-    o_sum = q_keep[4] + q_got[4].astype(f32)
+    o_sum = o_keep + o_got.astype(f32)
     o_grad = to_owner_z(o_sum)
     low = [part.astype(bf16) for part in (q_rows(0, 96), mlp_rows(0, 96), o_grad)]
     blocks = jnp.concatenate(low, axis=1).reshape(4, 24, 2176)

time: 375 us -> 364 us (0.971)
  waiting for transfers between devices: 146 us -> 140 us
  starting transfers between devices: 64.2 us -> 59.6 us
    ppermute x40 -> x41, waiting for transfers between devices: 102 us -> 83 us  [swap(): return lax.ppermute(value, 'ctx', [(i, i ^ bit) for i in range(8)])]
    ppermute x15, waiting for transfers between devices: 31 us -> 43.9 us  [shift_z(): return lax.ppermute(value, 'fsdp', [(i, (i + step) % 4) for i in range(4)])]
    ppermute x15, starting transfers between devices: 25.7 us -> 17 us  [shift_z(): return lax.ppermute(value, 'fsdp', [(i, (i + step) % 4) for i in range(4)])]
    ppermute x40 -> x41, starting transfers between devices: 34.6 us -> 38.7 us  [swap(): return lax.ppermute(value, 'ctx', [(i, i ^ bit) for i in range(8)])]
    unnamed x115 -> x109, local copies, waits for them, and re-layouts: 9.13 us -> 7.73 us
  transfers between devices with their start and end apart: 58 -> 59, of which waited for: 22 -> 23; matrix products, arithmetic and copies ran while one was open for 5% -> 6% of each run, Pallas kernels for 12% -> 12%
where the time goes in v5:
time: 364 us; the launch traced here: 359 us
  waiting for transfers between devices  140 us (38%)
  Pallas kernels  128 us (35%)
  starting transfers between devices  59.6 us (16%)
  other arithmetic  16.5 us (5%)
  local copies, waits for them, and re-layouts  13.7 us (4%)
    ppermute x41, waiting for transfers between devices, swap(): return lax.ppermute(value, 'ctx', [(i, i ^ bit) for i in range(8)])  83 us
    pallas_call x3, Pallas kernels, attn_call(): pl.pallas_call(functools.partial(attn_kernel, has_prev, last, seq, inside...  64.6 us
    ppermute x15, waiting for transfers between devices, shift_z(): return lax.ppermute(value, 'fsdp', [(i, (i + step) % 4) for i in range(4)])  43.9 us
    ppermute x41, starting transfers between devices, swap(): return lax.ppermute(value, 'ctx', [(i, i ^ bit) for i in range(8)])  38.7 us
    pallas_call x1, Pallas kernels, mlp_call(): pl.pallas_call(functools.partial(mlp_kernel, chunks), grid_spec=pltpu.Pre...  36.7 us
    ppermute x15, starting transfers between devices, shift_z(): return lax.ppermute(value, 'fsdp', [(i, (i + step) % 4) for i in range(4)])  17 us
    ppermute x3, waiting for transfers between devices, to_owner_z(): total = total + lax.ppermute(low, ('fsdp', 'ctx'), pairs).astype(f32)  13 us
    pallas_call x3, Pallas kernels, finish_call(): pl.pallas_call(functools.partial(finish_kernel, seqs), grid_spec=pltpu.Pr...  9.82 us
  transfers between devices with their start and end apart: 59, of which 23 were waited for; matrix products, arithmetic and copies ran while one was open for 6% of the time, Pallas kernels for 12%

profile of v5, /device:TPU:0, one launch (start us, length us, event | category | flops | bytes accessed | tf_op | source)
XLA Modules:
  0.0 359.3 jit_solution(1526748799839823457)
XLA Ops:
  36.0 3.4 collective-permute-done.21.refs_17_
  42.5 5.3 %collective-permute-done.10.refs_2_.refs_10_ = bf16[96,640]{1,0:T(8,128)(2,1)S(1)} collective-permute-done((bf16[96,640]{1,0:T(8,128)(2,1)S(1)}, bf16[96,640]{1,0:T(8,128)(2,1)S(1)}, u32[]{:S(2)}, u32[]{:S(2)}) %collective-permute-start.10) | collective-permute-done | bytes 122912 | tf_op jit(solution)/shard_map/ppermute | solution.py:394
  49.8 19.2 %collective-permute-done.12.refs_4_.refs_12_ = bf16[96,640]{1,0:T(8,128)(2,1)S(1)} collective-permute-done((bf16[96,640]{1,0:T(8,128)(2,1)S(1)}, bf16[96,640]{1,0:T(8,128)(2,1)S(1)}, u32[]{:S(2)}, u32[]{:S(2)}) %collective-permute-start.12) | collective-permute-done | bytes 122912 | tf_op jit(solution)/shard_map/ppermute | solution.py:390
  83.7 7.2 %collective-permute-done.30.refs_18_ = bf16[192,768]{1,0:T(8,128)(2,1)S(1)} collective-permute-done((bf16[192,768]{1,0:T(8,128)(2,1)S(1)}, bf16[192,768]{1,0:T(8,128)(2,1)S(1)}, u32[]{:S(2)}, u32[]{:S(2)}) %collective-permute-start.30) | collective-permute-done | bytes 294944 | tf_op jit(solution)/shard_map/ppermute | solution.py:394
  97.5 4.5 %vectors.1.refs_18_.refs_24_.refs_4_ = f32[8,768]{1,0:T(8,128)} custom-call(s32[29]{0:T(128)} %concatenate.9.at_ref.row_ref, bf16[96,640]{1,0:T(8,128)(2,1)} %get-tuple-element.61.refs_0_.refs_8_, bf16[96,640]{1,0:T(8,128)(2,1)} %copy-done.19, bf16[96,640]{1,0:T(8,128)(2,1)} %copy-done.20, bf16[96,640]{1,0:T(8,128)(2,1)} %copy-done.21, ...), custom_call_target="tpu_custom_call" | custom-call | tf_op jit(solution)/shard_map/vectors/pallas_call | solution.py:1192
  102.0 9.4 %collective-permute-done.1.refs_10_.refs_2_ = bf16[2,2,128,768]{3,2,1,0:T(8,128)(2,1)} collective-permute-done((bf16[2,2,128,768]{3,2,1,0:T(8,128)(2,1)S(1)}, bf16[2,2,128,768]{3,2,1,0:T(8,128)(2,1)}, u32[]{:S(2)}, u32[]{:S(2)}) %collective-permute-start.1) | collective-permute-done | bytes 786464 | tf_op jit(solution)/shard_map/ppermute | solution.py:390
  113.9 13.2 %collective-permute-done.2.refs_11_.refs_3_ = bf16[2,2,128,768]{3,2,1,0:T(8,128)(2,1)S(1)} collective-permute-done((bf16[2,2,128,768]{3,2,1,0:T(8,128)(2,1)}, bf16[2,2,128,768]{3,2,1,0:T(8,128)(2,1)S(1)}, u32[]{:S(2)}, u32[]{:S(2)}) %collective-permute-start.2) | collective-permute-done | bytes 786464 | tf_op jit(solution)/shard_map/ppermute | solution.py:390
  127.1 20.2 %attn.3 = (bf16[4,2,128,768]{3,2,1,0:T(8,128)(2,1)}, bf16[4,2,128,768]{3,2,1,0:T(8,128)(2,1)}, f32[768,640]{1,0:T(8,128)}, f32[192,768]{1,0:T(8,128)}, f32[8,768]{1,0:T(8,128)}, /*index=5*/f32[1024,768]{1,0:T(8,128)}) custom-call(s32[29]{0:T(128)} %concatenate.9.at_ref.row_ref, bf16[2,1,128,768]{3,2,1,0:T(8,128)(2,1)} %copy-done.13, ...), custom_call_target="tpu_custom_call" | custom-call | flops 24000000000 | bytes 15000000 | tf_op jit(solution)/shard_map/attn/pallas_call | solution.py:959
  148.9 36.7 %mlp.1 = (bf16[4,2,128,768]{3,2,1,0:T(8,128)(2,1)}, bf16[4,2,128,768]{3,2,1,0:T(8,128)(2,1)}, bf16[2,8,2,128,768]{4,3,2,1,0:T(8,128)(2,1)}, f32[2,1024,768]{2,1,...) custom-call(s32[29]{0:T(128)} %concatenate.9.at_ref.row_ref, ...), custom_call_target="tpu_custom_call" | custom-call | flops 30000001024 | bytes 30000000 | tf_op jit(solution)/shard_map/mlp/pallas_call | solution.py:575
  185.6 21.3 %attn.4 = (bf16[4,2,128,768]{3,2,1,0:T(8,128)(2,1)}, bf16[4,2,128,768]{3,2,1,0:T(8,128)(2,1)}, f32[768,640]{1,0:T(8,128)}, f32[192,768]{1,0:T(8,128)}, f32[8,768]{1,0:T(8,128)}) custom-call(s32[29]{0:T(128)} %concatenate.9.at_ref.row_ref, bf16[2,2,128,768]{3,2,1,0:T(8,128)(2,1)} %copy-done.9, bf16[2,2,128,768]{3,2,1,0:T(8,128)(2,1)} %collective-permute-done.refs_9_.refs_1_, ...), custom_call_target="tpu_custom_call" | custom-call | flops 24000000000 | bytes 15000000 | tf_op jit(solution)/shard_map/attn/pallas_call | solution.py:959
  206.8 23.1 %attn.5 = (bf16[4,2,128,768]{3,2,1,0:T(8,128)(2,1)}, bf16[4,2,128,768]{3,2,1,0:T(8,128)(2,1)}, bf16[4,96,640]{2,1,0:T(8,128)(2,1)}, f32[4,96,640]{2,1,0:T(8,128)...) custom-call(s32[29]{0:T(128)} %concatenate.9.at_ref.row_ref, bf16[2,2,128,768]{3,2,1,0:T(8,128)(2,1)} %copy-done.9, ...), custom_call_target="tpu_custom_call" | custom-call | flops 24000000000 | bytes 15000000 | tf_op jit(solution)/shard_map/attn/pallas_call | solution.py:959
  233.6 3.4 collective-permute-done.53
  242.0 6.6 %collective-permute-done.54 = bf16[96,768]{1,0:T(8,128)(2,1)S(1)} collective-permute-done((bf16[96,768]{1,0:T(8,128)(2,1)}, bf16[96,768]{1,0:T(8,128)(2,1)S(1)}, u32[]{:S(2)}, u32[]{:S(2)}) %collective-permute-start.54) | collective-permute-done | bytes 147488 | tf_op jit(solution)/shard_map/ppermute | solution.py:1359
  253.3 4.9 %collective-permute-done.55 = bf16[96,768]{1,0:T(8,128)(2,1)} collective-permute-done((bf16[96,768]{1,0:T(8,128)(2,1)}, bf16[96,768]{1,0:T(8,128)(2,1)}, u32[]{:S(2)}, u32[]{:S(2)}) %collective-permute-start.55) | collective-permute-done | bytes 147488 | tf_op jit(solution)/shard_map/ppermute | solution.py:1359
  259.7 6.7 %collective-permute-done.46 = bf16[96,640]{1,0:T(8,128)(2,1)} collective-permute-done((bf16[96,640]{1,0:T(8,128)(2,1)S(1)}, bf16[96,640]{1,0:T(8,128)(2,1)}, u32[]{:S(2)}, u32[]{:S(2)}) %collective-permute-start.46) | collective-permute-done | bytes 122912 | tf_op jit(solution)/shard_map/ppermute | solution.py:394
  266.4 6.2 %collective-permute-done.47 = bf16[96,640]{1,0:T(8,128)(2,1)} collective-permute-done((bf16[96,640]{1,0:T(8,128)(2,1)}, bf16[96,640]{1,0:T(8,128)(2,1)}, u32[]{:S(2)}, u32[]{:S(2)}) %collective-permute-start.47) | collective-permute-done | bytes 122912 | tf_op jit(solution)/shard_map/ppermute | solution.py:394
  273.7 4.0 %collective-permute-done.48 = bf16[96,640]{1,0:T(8,128)(2,1)S(1)} collective-permute-done((bf16[96,640]{1,0:T(8,128)(2,1)}, bf16[96,640]{1,0:T(8,128)(2,1)S(1)}, u32[]{:S(2)}, u32[]{:S(2)}) %collective-permute-start.48) | collective-permute-done | bytes 122912 | tf_op jit(solution)/shard_map/ppermute | solution.py:394
  290.1 3.3 collective-permute-done.50
  293.4 9.7 %collective-permute-done.51 = bf16[208,768]{1,0:T(8,128)(2,1)S(1)} collective-permute-done((bf16[208,768]{1,0:T(8,128)(2,1)S(1)}, bf16[208,768]{1,0:T(8,128)(2,1)S(1)}, u32[]{:S(2)}, u32[]{:S(2)}) %collective-permute-start.51) | collective-permute-done | bytes 319520 | tf_op jit(solution)/shard_map/ppermute | solution.py:394
  308.2 14.4 %collective-permute-done.40.refs_2_ = bf16[2,2,128,768]{3,2,1,0:T(8,128)(2,1)S(1)} collective-permute-done((bf16[2,2,128,768]{3,2,1,0:T(8,128)(2,1)S(1)}, bf16[2,2,128,768]{3,2,1,0:T(8,128)(2,1)S(1)}, u32[]{:S(2)}, u32[]{:S(2)}) %collective-permute-start.40) | collective-permute-done | bytes 786464 | tf_op jit(solution)/shard_map/ppermute | solution.py:390
  325.7 12.1 %collective-permute-done.37.refs_2_ = bf16[2,2,128,768]{3,2,1,0:T(8,128)(2,1)S(1)} collective-permute-done((bf16[2,2,128,768]{3,2,1,0:T(8,128)(2,1)S(1)}, bf16[2,2,128,768]{3,2,1,0:T(8,128)(2,1)S(1)}, u32[]{:S(2)}, u32[]{:S(2)}) %collective-permute-start.37) | collective-permute-done | bytes 786464 | tf_op jit(solution)/shard_map/ppermute | solution.py:390
  347.2 3.3 finish.3
  351.3 3.3 finish.4
  355.3 3.3 finish.5
  (256 shorter events, 113.1 us)
Async XLA Ops:
  2.1 68.5 %collective-permute-start.23 = (bf16[2,1,128,768]{3,2,1,0:T(8,128)(2,1)S(1)}, bf16[2,1,128,768]{3,2,1,0:T(8,128)(2,1)S(1)}, u32[]{:S(2)}, u32[]{:S(2)}) collective-permute-start(bf16[2,1,128,768]{3,2,1,0:T(8,128)(2,1)S(1)} %pad_maximum_fusion.3.refs_0_), channel_id=1, source_target_pairs={{0,2},{1,3},{2,0},{3,1},{4,6},{5,7},{6,4},{7,5},{8,10},{9,11},{10,... | collective-permute-start | bytes 1179656 | tf_op jit(solution)/shard_map/ppermute | solution.py:390
  5.2 65.9 %collective-permute-start.25 = (bf16[2,1,128,768]{3,2,1,0:T(8,128)(2,1)S(1)}, bf16[2,1,128,768]{3,2,1,0:T(8,128)(2,1)}, u32[]{:S(2)}, u32[]{:S(2)}) collective-permute-start(bf16[2,1,128,768]{3,2,1,0:T(8,128)(2,1)S(1)} %pad_maximum_fusion.3.refs_0_), channel_id=1, source_target_pairs={{0,1},{1,0},{2,3},{3,2},{4,5},{5,4},{6,7},{7,6},{8,9},{9,8},{10,11... | collective-permute-start | bytes 1179656 | tf_op jit(solution)/shard_map/ppermute | solution.py:390
  25.1 43.9 %collective-permute-start.22 = (bf16[2,1,128,768]{3,2,1,0:T(8,128)(2,1)S(1)}, bf16[2,1,128,768]{3,2,1,0:T(8,128)(2,1)}, u32[]{:S(2)}, u32[]{:S(2)}) collective-permute-start(bf16[2,1,128,768]{3,2,1,0:T(8,128)(2,1)S(1)} %pad_maximum_fusion.4), channel_id=1, source_target_pairs={{0,4},{1,5},{2,6},{3,7},{4,0},{5,1},{6,2},{7,3},{8,12},{9,13},{10,... | collective-permute-start | bytes 1179656 | tf_op jit(solution)/shard_map/ppermute | solution.py:390
  47.8 45.1 %collective-permute-start = (bf16[2,2,128,768]{3,2,1,0:T(8,128)(2,1)S(1)}, bf16[2,2,128,768]{3,2,1,0:T(8,128)(2,1)}, u32[]{:S(2)}, u32[]{:S(2)}) collective-permute-start(bf16[2,2,128,768]{3,2,1,0:T(8,128)(2,1)S(1)} %pad_maximum_fusion.1), channel_id=1, source_target_pairs={{0,4},{1,5},{2,6},{3,7},{4,0},{5,1},{6,2},{7,3},{8,12},{9,13},{10,... | collective-permute-start | bytes 2359304 | tf_op jit(solution)/shard_map/ppermute | solution.py:390
  49.3 19.7 %collective-permute-start.12 = (bf16[96,640]{1,0:T(8,128)(2,1)S(1)}, bf16[96,640]{1,0:T(8,128)(2,1)S(1)}, u32[]{:S(2)}, u32[]{:S(2)}) collective-permute-start(bf16[96,640]{1,0:T(8,128)(2,1)S(1)} %copy-done.18), channel_id=1, source_target_pairs={{0,4},{1,5},{2,6},{3,7},{4,0},{5,1},{6,2},{7,3},{8,12},{9,13},{10,... | collective-permute-start | bytes 368648 | tf_op jit(solution)/shard_map/ppermute | solution.py:390
  90.9 20.5 %collective-permute-start.1 = (bf16[2,2,128,768]{3,2,1,0:T(8,128)(2,1)S(1)}, bf16[2,2,128,768]{3,2,1,0:T(8,128)(2,1)}, u32[]{:S(2)}, u32[]{:S(2)}) collective-permute-start(bf16[2,2,128,768]{3,2,1,0:T(8,128)(2,1)S(1)} %pad_maximum_fusion.refs_8_.refs_0_), channel_id=1, source_target_pairs={{0,2},{1,3},{2,0},{3,1},{4,6},{5,7},{6,4},{7,5},{8,10},{9,11},{10,... | collective-permute-start | bytes 2359304 | tf_op jit(solution)/shard_map/ppermute | solution.py:390
  92.4 20.5 %collective-permute-start.3 = (bf16[2,2,128,768]{3,2,1,0:T(8,128)(2,1)S(1)}, bf16[2,2,128,768]{3,2,1,0:T(8,128)(2,1)}, u32[]{:S(2)}, u32[]{:S(2)}) collective-permute-start(bf16[2,2,128,768]{3,2,1,0:T(8,128)(2,1)S(1)} %pad_maximum_fusion.refs_8_.refs_0_), channel_id=1, source_target_pairs={{0,1},{1,0},{2,3},{3,2},{4,5},{5,4},{6,7},{7,6},{8,9},{9,8},{10,11... | collective-permute-start | bytes 2359304 | tf_op jit(solution)/shard_map/ppermute | solution.py:390
  92.9 34.2 %collective-permute-start.2 = (bf16[2,2,128,768]{3,2,1,0:T(8,128)(2,1)}, bf16[2,2,128,768]{3,2,1,0:T(8,128)(2,1)S(1)}, u32[]{:S(2)}, u32[]{:S(2)}) collective-permute-start(bf16[2,2,128,768]{3,2,1,0:T(8,128)(2,1)} %collective-permute-done.refs_9_.refs_1_), channel_id=1, source_target_pairs={{0,2},{1,3},{2,0},{3,1},{4,6},{5,7},{6,4},{7,5},{8,10},{9,11},{10,... | collective-permute-start | bytes 2359304 | tf_op jit(solution)/shard_map/ppermute | solution.py:390
  111.4 36.0 %collective-permute-start.34 = (bf16[192,768]{1,0:T(8,128)(2,1)}, bf16[192,768]{1,0:T(8,128)(2,1)S(1)}, u32[]{:S(2)}, u32[]{:S(2)}) collective-permute-start(bf16[192,768]{1,0:T(8,128)(2,1)} %copy-done.47), channel_id=1, source_target_pairs={{0,4},{1,5},{2,6},{3,7},{4,0},{5,1},{6,2},{7,3},{8,12},{9,13},{10,... | collective-permute-start | bytes 884744 | tf_op jit(solution)/shard_map/ppermute | solution.py:390
  112.9 34.4 %collective-permute-start.35 = (bf16[192,768]{1,0:T(8,128)(2,1)}, bf16[192,768]{1,0:T(8,128)(2,1)S(1)}, u32[]{:S(2)}, u32[]{:S(2)}) collective-permute-start(bf16[192,768]{1,0:T(8,128)(2,1)} %copy-done.48), channel_id=1, source_target_pairs={{0,4},{1,5},{2,6},{3,7},{4,0},{5,1},{6,2},{7,3},{8,12},{9,13},{10,... | collective-permute-start | bytes 884744 | tf_op jit(solution)/shard_map/ppermute | solution.py:390
  113.4 34.0 %collective-permute-start.4 = (bf16[2,2,128,768]{3,2,1,0:T(8,128)(2,1)}, bf16[2,2,128,768]{3,2,1,0:T(8,128)(2,1)S(1)}, u32[]{:S(2)}, u32[]{:S(2)}) collective-permute-start(bf16[2,2,128,768]{3,2,1,0:T(8,128)(2,1)} %collective-permute-done.refs_9_.refs_1_), channel_id=1, source_target_pairs={{0,1},{1,0},{2,3},{3,2},{4,5},{5,4},{6,7},{7,6},{8,9},{9,8},{10,11... | collective-permute-start | bytes 2359304 | tf_op jit(solution)/shard_map/ppermute | solution.py:390
  113.4 34.0 %collective-permute-start.5 = (bf16[2,2,128,768]{3,2,1,0:T(8,128)(2,1)}, bf16[2,2,128,768]{3,2,1,0:T(8,128)(2,1)S(1)}, u32[]{:S(2)}, u32[]{:S(2)}) collective-permute-start(bf16[2,2,128,768]{3,2,1,0:T(8,128)(2,1)} %collective-permute-done.1.refs_10_.refs_2_), channel_id=1, source_target_pairs={{0,1},{1,0},{2,3},{3,2},{4,5},{5,4},{6,7},{7,6},{8,9},{9,8},{10,11... | collective-permute-start | bytes 2359304 | tf_op jit(solution)/shard_map/ppermute | solution.py:390
  127.1 20.3 %collective-permute-start.6 = (bf16[2,2,128,768]{3,2,1,0:T(8,128)(2,1)S(1)}, bf16[2,2,128,768]{3,2,1,0:T(8,128)(2,1)S(1)}, u32[]{:S(2)}, u32[]{:S(2)}) collective-permute-start(bf16[2,2,128,768]{3,2,1,0:T(8,128)(2,1)S(1)} %collective-permute-done.2.refs_11_.refs_3_), channel_id=1, source_target_pairs={{0,1},{1,0},{2,3},{3,2},{4,5},{5,4},{6,7},{7,6},{8,9},{9,8},{10,11... | collective-permute-start | bytes 2359304 | tf_op jit(solution)/shard_map/ppermute | solution.py:390
  232.1 46.9 %collective-permute-start.49 = (bf16[4,208,768]{2,1,0:T(8,128)(2,1)}, bf16[4,208,768]{2,1,0:T(8,128)(2,1)S(1)}, u32[]{:S(2)}, u32[]{:S(2)}) collective-permute-start(bf16[4,208,768]{2,1,0:T(8,128)(2,1)} %get-tuple-element.92), channel_id=1, source_target_pairs={{0,4},{1,5},{2,6},{3,7},{4,0},{5,1},{6,2},{7,3},{8,12},{9,13},{10,... | collective-permute-start | bytes 3833864 | tf_op jit(solution)/shard_map/ppermute | solution.py:390
  233.6 49.9 %collective-permute-start.42 = (bf16[4,2,128,768]{3,2,1,0:T(8,128)(2,1)}, bf16[4,2,128,768]{3,2,1,0:T(8,128)(2,1)S(1)}, u32[]{:S(2)}, u32[]{:S(2)}) collective-permute-start(bf16[4,2,128,768]{3,2,1,0:T(8,128)(2,1)} %get-tuple-element.82), channel_id=1, source_target_pairs={{0,1},{1,0},{2,3},{3,2},{4,5},{5,4},{6,7},{7,6},{8,9},{9,8},{10,11... | collective-permute-start | bytes 4718600 | tf_op jit(solution)/shard_map/ppermute | solution.py:390
  239.9 45.3 %collective-permute-start.39 = (bf16[4,2,128,768]{3,2,1,0:T(8,128)(2,1)}, bf16[4,2,128,768]{3,2,1,0:T(8,128)(2,1)}, u32[]{:S(2)}, u32[]{:S(2)}) collective-permute-start(bf16[4,2,128,768]{3,2,1,0:T(8,128)(2,1)} %get-tuple-element.80), channel_id=1, source_target_pairs={{0,1},{1,0},{2,3},{3,2},{4,5},{5,4},{6,7},{7,6},{8,9},{9,8},{10,11... | collective-permute-start | bytes 4718600 | tf_op jit(solution)/shard_map/ppermute | solution.py:390
  259.7 27.3 %collective-permute-start.36 = (bf16[4,2,128,768]{3,2,1,0:T(8,128)(2,1)}, bf16[4,2,128,768]{3,2,1,0:T(8,128)(2,1)}, u32[]{:S(2)}, u32[]{:S(2)}) collective-permute-start(bf16[4,2,128,768]{3,2,1,0:T(8,128)(2,1)} %get-tuple-element.78), channel_id=1, source_target_pairs={{0,1},{1,0},{2,3},{3,2},{4,5},{5,4},{6,7},{7,6},{8,9},{9,8},{10,11... | collective-permute-start | bytes 4718600 | tf_op jit(solution)/shard_map/ppermute | solution.py:390
  281.1 22.0 %collective-permute-start.51 = (bf16[208,768]{1,0:T(8,128)(2,1)S(1)}, bf16[208,768]{1,0:T(8,128)(2,1)S(1)}, u32[]{:S(2)}, u32[]{:S(2)}) collective-permute-start(bf16[208,768]{1,0:T(8,128)(2,1)S(1)} %get-tuple-element.108), channel_id=1, source_target_pairs={{0,16},{8,24},{16,0},{24,8},{1,17},{9,25},{17,1},{25,9},{2,18},{10... | collective-permute-start | bytes 958472 | tf_op jit(solution)/shard_map/ppermute | solution.py:394
  285.2 21.1 %collective-permute-start.43 = (bf16[2,2,128,768]{3,2,1,0:T(8,128)(2,1)S(1)}, bf16[2,2,128,768]{3,2,1,0:T(8,128)(2,1)S(1)}, u32[]{:S(2)}, u32[]{:S(2)}) collective-permute-start(bf16[2,2,128,768]{3,2,1,0:T(8,128)(2,1)S(1)} %add_convert_fusion), channel_id=1, source_target_pairs={{0,2},{1,3},{2,0},{3,1},{4,6},{5,7},{6,4},{7,5},{8,10},{9,11},{10,... | collective-permute-start | bytes 2359304 | tf_op jit(solution)/shard_map/ppermute | solution.py:390
  287.0 35.5 %collective-permute-start.40 = (bf16[2,2,128,768]{3,2,1,0:T(8,128)(2,1)S(1)}, bf16[2,2,128,768]{3,2,1,0:T(8,128)(2,1)S(1)}, u32[]{:S(2)}, u32[]{:S(2)}) collective-permute-start(bf16[2,2,128,768]{3,2,1,0:T(8,128)(2,1)S(1)} %add_convert_fusion.1), channel_id=1, source_target_pairs={{0,2},{1,3},{2,0},{3,1},{4,6},{5,7},{6,4},{7,5},{8,10},{9,11},{10,... | collective-permute-start | bytes 2359304 | tf_op jit(solution)/shard_map/ppermute | solution.py:390
  293.4 44.4 %collective-permute-start.37 = (bf16[2,2,128,768]{3,2,1,0:T(8,128)(2,1)S(1)}, bf16[2,2,128,768]{3,2,1,0:T(8,128)(2,1)S(1)}, u32[]{:S(2)}, u32[]{:S(2)}) collective-permute-start(bf16[2,2,128,768]{3,2,1,0:T(8,128)(2,1)S(1)} %add_convert_fusion.2), channel_id=1, source_target_pairs={{0,2},{1,3},{2,0},{3,1},{4,6},{5,7},{6,4},{7,5},{8,10},{9,11},{10,... | collective-permute-start | bytes 2359304 | tf_op jit(solution)/shard_map/ppermute | solution.py:390
  304.1 36.8 %collective-permute-start.57 = (bf16[2,24,2176]{2,1,0:T(8,128)(2,1)S(1)}, bf16[2,24,2176]{2,1,0:T(8,128)(2,1)S(1)}, u32[]{:S(2)}, u32[]{:S(2)}) collective-permute-start(bf16[2,24,2176]{2,1,0:T(8,128)(2,1)S(1)} %get-tuple-element.125), channel_id=1, source_target_pairs={{0,2},{1,3},{2,0},{3,1},{4,6},{5,7},{6,4},{7,5},{8,10},{9,11},{10,... | collective-permute-start | bytes 626696 | tf_op jit(solution)/shard_map/ppermute | solution.py:390
  306.5 39.9 %collective-permute-start.44 = (bf16[1,2,128,768]{3,2,1,0:T(8,128)(2,1)S(1)}, bf16[1,2,128,768]{3,2,1,0:T(8,128)(2,1)S(1)}, u32[]{:S(2)}, u32[]{:S(2)}) collective-permute-start(bf16[1,2,128,768]{3,2,1,0:T(8,128)(2,1)S(1)} %add_convert_fusion.3), channel_id=1, source_target_pairs={{0,4},{1,5},{2,6},{3,7},{4,0},{5,1},{6,2},{7,3},{8,12},{9,13},{10,... | collective-permute-start | bytes 1179656 | tf_op jit(solution)/shard_map/ppermute | solution.py:390
  324.0 26.5 %collective-permute-start.41 = (bf16[1,2,128,768]{3,2,1,0:T(8,128)(2,1)S(1)}, bf16[1,2,128,768]{3,2,1,0:T(8,128)(2,1)S(1)}, u32[]{:S(2)}, u32[]{:S(2)}) collective-permute-start(bf16[1,2,128,768]{3,2,1,0:T(8,128)(2,1)S(1)} %add_convert_fusion.4), channel_id=1, source_target_pairs={{0,4},{1,5},{2,6},{3,7},{4,0},{5,1},{6,2},{7,3},{8,12},{9,13},{10,... | collective-permute-start | bytes 1179656 | tf_op jit(solution)/shard_map/ppermute | solution.py:390
  (89 other events, 1109.1 us)

commit v6 on v3

--- a/solution.py
+++ b/solution.py
@@ -974,56 +974,51 @@
     )(row_offsets, *operands)
 
 
-def finish_kernel(seqs, half_ref, x_ref, c_ref, *refs):
+def finish_kernel(half_ref, x_ref, c_ref, *refs):
     refs = list(refs)
-    terms = [[refs.pop(0) for _ in range(4)] for _ in seqs]
-    bias = refs.pop(0)
-    out_ref, grad_ref = refs[-2:]
+    terms = [[refs.pop(0) for _ in range(4)] for _ in range(3)]
+    bias, out_ref, grad_ref = refs
     f32 = jnp.float32
 
-    def write(sources):
+    def write(seq, sources):
         total = [source[0].astype(f32) for source in sources]
         total = sum(total[1:], total[0])
-        x = x_ref[0].astype(f32)
+        x = x_ref[seq].astype(f32)
         normed, inverse = normalize(x)
-        out_ref[0] = x + bias[4:5, :] + total[0]
+        out_ref[seq] = x + bias[4:5, :] + total[0]
         s = total[1]
         mean_s = jnp.mean(s, axis=-1, keepdims=True)
         mean_sn = jnp.mean(s * normed, axis=-1, keepdims=True)
-        grad_ref[0] = c_ref[0] + inverse * (s - mean_s - normed * mean_sn)
-
-    for at in range(len(seqs)):
-        for other in range(2):
-            @pl.when(pl.program_id(0) == at * 2 + other)
-            def _(at=at, other=other):
-                write(terms[at][3:] if other else terms[at][:3])
-
-
-def finish_call(half, seqs, x, cot, terms, bias, done):
+        grad_ref[seq] = c_ref[seq] + inverse * (s - mean_s - normed * mean_sn)
+
+    @pl.when(pl.program_id(0) == 0)
+    def _():
+        for seq in range(3):
+            write(seq, terms[seq][:3])
+
+    @pl.when(pl.program_id(0) == 1)
+    def _():
+        for seq in range(3):
+            write(seq, terms[seq][3:])
+
+
+def finish_call(half, x, cot, terms, bias):
     _, rows, width = x.shape
     f32 = jnp.float32
-    seq_spec = pl.BlockSpec(
-        (1, rows, width),
-        lambda i, at: (jnp.where(i % 2 == 0, at[0], 1 - at[0]) * 3 + seqs[0] + i // 2, 0, 0),
-    )
+    seq_spec = pl.BlockSpec((3, rows, width), lambda i, at: (jnp.where(i == 0, at[0], 1 - at[0]), 0, 0))
     part_spec = pl.BlockSpec((1, 2, rows, width), lambda i, at: (0, 0, 0, 0))
-    before = list(done) if done is not None else []
     operands = [x, cot, *[a for parts in terms for a in parts], bias]
     return pl.pallas_call(
-        functools.partial(finish_kernel, seqs),
+        finish_kernel,
         grid_spec=pltpu.PrefetchScalarGridSpec(
             num_scalar_prefetch=1,
-            grid=(2 * len(seqs),),
-            in_specs=[seq_spec, seq_spec]
-            + [part_spec] * (4 * len(seqs))
-            + [whole(bias.shape)]
-            + [pl.BlockSpec(memory_space=pl.ANY)] * len(before),
+            grid=(2,),
+            in_specs=[seq_spec, seq_spec] + [part_spec] * 12 + [whole(bias.shape)],
             out_specs=[seq_spec, seq_spec],
         ),
         out_shape=[jax.ShapeDtypeStruct(x.shape, f32)] * 2,
-        input_output_aliases={len(operands) + 1: 0, len(operands) + 2: 1} if before else {},
         name="finish",
-    )(half, *operands, *before)
+    )(half, *operands)
 
 
 def pick(value, index, axis=0):
@@ -1357,9 +1352,6 @@
         far = (keep[1:2].astype(f32) + got[1:2].astype(f32) + side[1:2].astype(f32)).astype(bf16)
         return keep, got, side, swap(far, 4)
 
-    def finish(seqs, terms, done):
-        return finish_call(half, seqs, inputs, cotangent, terms, vecs, done)
-
     first_send, first_keep, g_q, g_o, vec, first_norm = attention(0, None, None)
     prev = (g_q, g_o, vec)
     send, keep, rest_part, rest_norm, g_send, g_keep, mlp_vec = mlp_call(
@@ -1377,9 +1369,7 @@
         2, (rest_part, rest_norm), (g_q, g_o, vec), (mlp_vec, at_rows, at_cols)
     )
     terms.append(scatter(send, keep))
-    done = None
-    for seq in range(3):
-        done = finish((seq,), terms[seq : seq + 1], done)
+    done = finish_call(half, inputs, cotangent, terms, vecs)
     q_grad = reduce_z((q_keep, swap(q_send, 4)))
     q_low = q_grad.astype(bf16).reshape(4, 24, 640)
     q_pair = exchange_four(q_low, x, c)

time: 371 us -> 369 us (level)
  Pallas kernels: 128 us -> 124 us
    pallas_call x3 -> x1, Pallas kernels: 9.82 us -> 6.37 us  [finish_call(): pl.pallas_call(finish_kernel, grid_spec=pltpu.PrefetchScalarGridSpec(num_...]
    unnamed x113 -> x109, local copies, waits for them, and re-layouts: 8.37 us -> 9.73 us
  transfers between devices with their start and end apart: 63 -> 63, of which waited for: 24 -> 24; matrix products, arithmetic and copies ran while one was open for 7% -> 8% of each run, Pallas kernels for 12% -> 10%
where the time goes in v6:
time: 369 us; the launch traced here: 365 us
  waiting for transfers between devices  136 us (37%)
  Pallas kernels  124 us (34%)
  starting transfers between devices  65.5 us (18%)
  other arithmetic  19.5 us (5%)
  local copies, waits for them, and re-layouts  17.7 us (5%)
    ppermute x45, waiting for transfers between devices, swap(): return lax.ppermute(value, 'ctx', [(i, i ^ bit) for i in range(8)])  85.1 us
    pallas_call x3, Pallas kernels, attn_call(): pl.pallas_call(functools.partial(attn_kernel, has_prev, last, seq, inside...  64.4 us
    ppermute x18, waiting for transfers between devices, shift_z(): return lax.ppermute(value, 'fsdp', [(i, (i + step) % 4) for i in range(4)])  51 us
    ppermute x45, starting transfers between devices, swap(): return lax.ppermute(value, 'ctx', [(i, i ^ bit) for i in range(8)])  39.4 us
    pallas_call x1, Pallas kernels, mlp_call(): pl.pallas_call(functools.partial(mlp_kernel, chunks), grid_spec=pltpu.Pre...  36.6 us
    ppermute x18, starting transfers between devices, shift_z(): return lax.ppermute(value, 'fsdp', [(i, (i + step) % 4) for i in range(4)])  26 us
    unnamed x109, local copies, waits for them, and re-layouts  9.73 us
  transfers between devices with their start and end apart: 63, of which 24 were waited for; matrix products, arithmetic and copies ran while one was open for 8% of the time, Pallas kernels for 10%

profile of v6, /device:TPU:0, one launch (start us, length us, event | category | flops | bytes accessed | tf_op | source)
XLA Modules:
  0.0 364.6 jit_solution(3854227744235137778)
XLA Ops:
  0.7 3.1 collective-permute-start.30
  36.0 3.4 collective-permute-done.35.refs_17_
  42.6 5.3 %collective-permute-done.24.refs_2_.refs_10_ = bf16[96,640]{1,0:T(8,128)(2,1)S(1)} collective-permute-done((bf16[96,640]{1,0:T(8,128)(2,1)S(1)}, bf16[96,640]{1,0:T(8,128)(2,1)S(1)}, u32[]{:S(2)}, u32[]{:S(2)}) %collective-permute-start.24) | collective-permute-done | bytes 122912 | tf_op jit(solution)/shard_map/ppermute | solution.py:394
  49.9 19.2 %collective-permute-done.26.refs_4_.refs_12_ = bf16[96,640]{1,0:T(8,128)(2,1)S(1)} collective-permute-done((bf16[96,640]{1,0:T(8,128)(2,1)S(1)}, bf16[96,640]{1,0:T(8,128)(2,1)S(1)}, u32[]{:S(2)}, u32[]{:S(2)}) %collective-permute-start.26) | collective-permute-done | bytes 122912 | tf_op jit(solution)/shard_map/ppermute | solution.py:390
  75.3 3.1 collective-permute-start.17
  83.7 7.2 %collective-permute-done.17.refs_18_ = bf16[192,768]{1,0:T(8,128)(2,1)S(1)} collective-permute-done((bf16[192,768]{1,0:T(8,128)(2,1)S(1)}, bf16[192,768]{1,0:T(8,128)(2,1)S(1)}, u32[]{:S(2)}, u32[]{:S(2)}) %collective-permute-start.17) | collective-permute-done | bytes 294944 | tf_op jit(solution)/shard_map/ppermute | solution.py:394
  97.5 4.5 %vectors.1.refs_18_.refs_24_.refs_12_ = f32[8,768]{1,0:T(8,128)} custom-call(s32[29]{0:T(128)} %concatenate.9.at_ref.row_ref, bf16[96,640]{1,0:T(8,128)(2,1)} %get-tuple-element.57.refs_0_.refs_8_, bf16[96,640]{1,0:T(8,128)(2,1)} %copy-done.18, bf16[96,640]{1,0:T(8,128)(2,1)} %copy-done.19, bf16[96,640]{1,0:T(8,128)(2,1)} %copy-done.20, ...), custom_call_target="tpu_custom_call" | custom-call | tf_op jit(solution)/shard_map/vectors/pallas_call | solution.py:1187
  101.9 9.4 %collective-permute-done.8.refs_10_.refs_2_ = bf16[2,2,128,768]{3,2,1,0:T(8,128)(2,1)} collective-permute-done((bf16[2,2,128,768]{3,2,1,0:T(8,128)(2,1)S(1)}, bf16[2,2,128,768]{3,2,1,0:T(8,128)(2,1)}, u32[]{:S(2)}, u32[]{:S(2)}) %collective-permute-start.8) | collective-permute-done | bytes 786464 | tf_op jit(solution)/shard_map/ppermute | solution.py:390
  113.9 13.2 %collective-permute-done.9.refs_11_.refs_3_ = bf16[2,2,128,768]{3,2,1,0:T(8,128)(2,1)S(1)} collective-permute-done((bf16[2,2,128,768]{3,2,1,0:T(8,128)(2,1)S(1)}, bf16[2,2,128,768]{3,2,1,0:T(8,128)(2,1)S(1)}, u32[]{:S(2)}, u32[]{:S(2)}) %collective-permute-start.9) | collective-permute-done | bytes 786464 | tf_op jit(solution)/shard_map/ppermute | solution.py:390
  127.1 20.2 %attn.3 = (bf16[4,2,128,768]{3,2,1,0:T(8,128)(2,1)}, bf16[4,2,128,768]{3,2,1,0:T(8,128)(2,1)}, f32[768,640]{1,0:T(8,128)}, f32[192,768]{1,0:T(8,128)}, f32[8,768]{1,0:T(8,128)}, /*index=5*/f32[1024,768]{1,0:T(8,128)}) custom-call(s32[29]{0:T(128)} %concatenate.9.at_ref.row_ref, bf16[2,1,128,768]{3,2,1,0:T(8,128)(2,1)} %copy-done.10, ...), custom_call_target="tpu_custom_call" | custom-call | flops 24000000000 | bytes 15000000 | tf_op jit(solution)/shard_map/attn/pallas_call | solution.py:959
  148.9 36.6 %mlp.1 = (bf16[4,2,128,768]{3,2,1,0:T(8,128)(2,1)}, bf16[4,2,128,768]{3,2,1,0:T(8,128)(2,1)}, bf16[2,8,2,128,768]{4,3,2,1,0:T(8,128)(2,1)}, f32[2,1024,768]{2,1,...) custom-call(s32[29]{0:T(128)} %concatenate.9.at_ref.row_ref, ...), custom_call_target="tpu_custom_call" | custom-call | flops 30000001024 | bytes 30000000 | tf_op jit(solution)/shard_map/mlp/pallas_call | solution.py:575
  185.5 21.2 %attn.4 = (bf16[4,2,128,768]{3,2,1,0:T(8,128)(2,1)}, bf16[4,2,128,768]{3,2,1,0:T(8,128)(2,1)}, f32[768,640]{1,0:T(8,128)}, f32[192,768]{1,0:T(8,128)}, f32[8,768]{1,0:T(8,128)}) custom-call(s32[29]{0:T(128)} %concatenate.9.at_ref.row_ref, bf16[2,2,128,768]{3,2,1,0:T(8,128)(2,1)} %copy-done.9, bf16[2,2,128,768]{3,2,1,0:T(8,128)(2,1)} %copy-done.41, ...), custom_call_target="tpu_custom_call" | custom-call | flops 24000000000 | bytes 15000000 | tf_op jit(solution)/shard_map/attn/pallas_call | solution.py:959
  206.7 23.0 %attn.5 = (bf16[4,2,128,768]{3,2,1,0:T(8,128)(2,1)}, bf16[4,2,128,768]{3,2,1,0:T(8,128)(2,1)}, bf16[4,96,640]{2,1,0:T(8,128)(2,1)}, f32[4,96,640]{2,1,0:T(8,128)...) custom-call(s32[29]{0:T(128)} %concatenate.9.at_ref.row_ref, bf16[2,2,128,768]{3,2,1,0:T(8,128)(2,1)} %copy-done.9, ...), custom_call_target="tpu_custom_call" | custom-call | flops 24000000000 | bytes 15000000 | tf_op jit(solution)/shard_map/attn/pallas_call | solution.py:959
  231.9 4.9 %collective-permute-done.57 = bf16[96,768]{1,0:T(8,128)(2,1)S(1)} collective-permute-done((bf16[96,768]{1,0:T(8,128)(2,1)}, bf16[96,768]{1,0:T(8,128)(2,1)S(1)}, u32[]{:S(2)}, u32[]{:S(2)}) %collective-permute-start.57) | collective-permute-done | bytes 147488 | tf_op jit(solution)/shard_map/ppermute | solution.py:390
  249.8 4.8 %collective-permute-done.60 = bf16[24,768]{1,0:T(8,128)(2,1)S(1)} collective-permute-done((bf16[24,768]{1,0:T(8,128)(2,1)S(1)}, bf16[24,768]{1,0:T(8,128)(2,1)S(1)}, u32[]{:S(2)}, u32[]{:S(2)}) %collective-permute-start.60) | collective-permute-done | bytes 36896 | tf_op jit(solution)/shard_map/ppermute | solution.py:394
  254.8 4.9 %collective-permute-done.61 = bf16[24,768]{1,0:T(8,128)(2,1)} collective-permute-done((bf16[24,768]{1,0:T(8,128)(2,1)}, bf16[24,768]{1,0:T(8,128)(2,1)}, u32[]{:S(2)}, u32[]{:S(2)}) %collective-permute-start.61) | collective-permute-done | bytes 36896 | tf_op jit(solution)/shard_map/ppermute | solution.py:394
  263.9 7.2 %collective-permute-done.46 = bf16[96,640]{1,0:T(8,128)(2,1)} collective-permute-done((bf16[96,640]{1,0:T(8,128)(2,1)S(1)}, bf16[96,640]{1,0:T(8,128)(2,1)}, u32[]{:S(2)}, u32[]{:S(2)}) %collective-permute-start.46) | collective-permute-done | bytes 122912 | tf_op jit(solution)/shard_map/ppermute | solution.py:394
  271.1 7.0 %collective-permute-done.47 = bf16[96,640]{1,0:T(8,128)(2,1)} collective-permute-done((bf16[96,640]{1,0:T(8,128)(2,1)}, bf16[96,640]{1,0:T(8,128)(2,1)}, u32[]{:S(2)}, u32[]{:S(2)}) %collective-permute-start.47) | collective-permute-done | bytes 122912 | tf_op jit(solution)/shard_map/ppermute | solution.py:394
  287.3 4.4 %collective-permute-start.53 = (bf16[208,768]{1,0:T(8,128)(2,1)S(1)}, bf16[208,768]{1,0:T(8,128)(2,1)S(1)}, u32[]{:S(2)}, u32[]{:S(2)}) collective-permute-start(bf16[208,768]{1,0:T(8,128)(2,1)S(1)} %get-tuple-element.98), channel_id=1, source_target_pairs={{0,16},{8,24},{16,0},{24,8},{1,17},{9,25},{17,1},{25,9},{2,18},{10... | collective-permute-start | bytes 958472 | tf_op jit(solution)/shard_map/ppermute | solution.py:394
  301.2 9.9 %collective-permute-done.53 = bf16[208,768]{1,0:T(8,128)(2,1)S(1)} collective-permute-done((bf16[208,768]{1,0:T(8,128)(2,1)S(1)}, bf16[208,768]{1,0:T(8,128)(2,1)S(1)}, u32[]{:S(2)}, u32[]{:S(2)}) %collective-permute-start.53) | collective-permute-done | bytes 319520 | tf_op jit(solution)/shard_map/ppermute | solution.py:394
  317.7 12.8 %collective-permute-done.40.refs_6_ = bf16[2,2,128,768]{3,2,1,0:T(8,128)(2,1)S(1)} collective-permute-done((bf16[2,2,128,768]{3,2,1,0:T(8,128)(2,1)S(1)}, bf16[2,2,128,768]{3,2,1,0:T(8,128)(2,1)S(1)}, u32[]{:S(2)}, u32[]{:S(2)}) %collective-permute-start.40) | collective-permute-done | bytes 786464 | tf_op jit(solution)/shard_map/ppermute | solution.py:390
  333.6 12.7 %collective-permute-done.37.refs_2_ = bf16[2,2,128,768]{3,2,1,0:T(8,128)(2,1)S(1)} collective-permute-done((bf16[2,2,128,768]{3,2,1,0:T(8,128)(2,1)S(1)}, bf16[2,2,128,768]{3,2,1,0:T(8,128)(2,1)S(1)}, u32[]{:S(2)}, u32[]{:S(2)}) %collective-permute-start.37) | collective-permute-done | bytes 786464 | tf_op jit(solution)/shard_map/ppermute | solution.py:390
  353.2 2.6 spread.1
  357.5 6.4 %finish.1 = (f32[6,128,768]{2,1,0:T(8,128)}, f32[6,128,768]{2,1,0:T(8,128)}) custom-call(s32[1]{0:T(128)} %bitcast.half_ref, bf16[6,128,768]{2,1,0:T(8,128)(2,1)} %x_ref.1, f32[6,128,768]{2,1,0:T(8,128)} %c_ref.1, bf16[4,2,128,768]{3,2,1,0:T(8,128)(2,1)} %get-tuple-element.63.refs_0_, bf16[4,2,128,768]{3,2,1,0:T(8,128)(2,1)} %collective-permute-done.36.refs_1_, ...), custom_call_target="tpu_custom_call" | custom-call | tf_op jit(solution)/shard_map/finish/pallas_call | solution.py:1011
  (264 shorter events, 116.0 us)
Async XLA Ops:
  9.1 61.6 %collective-permute-start.1 = (bf16[2,1,128,768]{3,2,1,0:T(8,128)(2,1)S(1)}, bf16[2,1,128,768]{3,2,1,0:T(8,128)(2,1)}, u32[]{:S(2)}, u32[]{:S(2)}) collective-permute-start(bf16[2,1,128,768]{3,2,1,0:T(8,128)(2,1)S(1)} %pad_maximum_fusion.2.refs_0_), channel_id=1, source_target_pairs={{0,2},{1,3},{2,0},{3,1},{4,6},{5,7},{6,4},{7,5},{8,10},{9,11},{10,... | collective-permute-start | bytes 1179656 | tf_op jit(solution)/shard_map/ppermute | solution.py:390
  10.7 60.5 %collective-permute-start.3 = (bf16[2,1,128,768]{3,2,1,0:T(8,128)(2,1)S(1)}, bf16[2,1,128,768]{3,2,1,0:T(8,128)(2,1)}, u32[]{:S(2)}, u32[]{:S(2)}) collective-permute-start(bf16[2,1,128,768]{3,2,1,0:T(8,128)(2,1)S(1)} %pad_maximum_fusion.2.refs_0_), channel_id=1, source_target_pairs={{0,1},{1,0},{2,3},{3,2},{4,5},{5,4},{6,7},{7,6},{8,9},{9,8},{10,11... | collective-permute-start | bytes 1179656 | tf_op jit(solution)/shard_map/ppermute | solution.py:390
  25.2 43.9 %collective-permute-start = (bf16[2,1,128,768]{3,2,1,0:T(8,128)(2,1)S(1)}, bf16[2,1,128,768]{3,2,1,0:T(8,128)(2,1)}, u32[]{:S(2)}, u32[]{:S(2)}) collective-permute-start(bf16[2,1,128,768]{3,2,1,0:T(8,128)(2,1)S(1)} %pad_maximum_fusion.3), channel_id=1, source_target_pairs={{0,4},{1,5},{2,6},{3,7},{4,0},{5,1},{6,2},{7,3},{8,12},{9,13},{10,... | collective-permute-start | bytes 1179656 | tf_op jit(solution)/shard_map/ppermute | solution.py:390
  47.9 45.0 %collective-permute-start.7 = (bf16[2,2,128,768]{3,2,1,0:T(8,128)(2,1)S(1)}, bf16[2,2,128,768]{3,2,1,0:T(8,128)(2,1)S(1)}, u32[]{:S(2)}, u32[]{:S(2)}) collective-permute-start(bf16[2,2,128,768]{3,2,1,0:T(8,128)(2,1)S(1)} %pad_maximum_fusion.1), channel_id=1, source_target_pairs={{0,4},{1,5},{2,6},{3,7},{4,0},{5,1},{6,2},{7,3},{8,12},{9,13},{10,... | collective-permute-start | bytes 2359304 | tf_op jit(solution)/shard_map/ppermute | solution.py:390
  92.4 20.5 %collective-permute-start.10 = (bf16[2,2,128,768]{3,2,1,0:T(8,128)(2,1)S(1)}, bf16[2,2,128,768]{3,2,1,0:T(8,128)(2,1)}, u32[]{:S(2)}, u32[]{:S(2)}) collective-permute-start(bf16[2,2,128,768]{3,2,1,0:T(8,128)(2,1)S(1)} %pad_maximum_fusion.refs_8_.refs_0_), channel_id=1, source_target_pairs={{0,1},{1,0},{2,3},{3,2},{4,5},{5,4},{6,7},{7,6},{8,9},{9,8},{10,11... | collective-permute-start | bytes 2359304 | tf_op jit(solution)/shard_map/ppermute | solution.py:390
  92.9 34.2 %collective-permute-start.9 = (bf16[2,2,128,768]{3,2,1,0:T(8,128)(2,1)S(1)}, bf16[2,2,128,768]{3,2,1,0:T(8,128)(2,1)S(1)}, u32[]{:S(2)}, u32[]{:S(2)}) collective-permute-start(bf16[2,2,128,768]{3,2,1,0:T(8,128)(2,1)S(1)} %collective-permute-done.7.refs_9_.refs_1_), channel_id=1, source_target_pairs={{0,2},{1,3},{2,0},{3,1},{4,6},{5,7},{6,4},{7,5},{8,10},{9,11},{10,... | collective-permute-start | bytes 2359304 | tf_op jit(solution)/shard_map/ppermute | solution.py:390
  111.4 35.9 %collective-permute-start.21 = (bf16[192,768]{1,0:T(8,128)(2,1)}, bf16[192,768]{1,0:T(8,128)(2,1)S(1)}, u32[]{:S(2)}, u32[]{:S(2)}) collective-permute-start(bf16[192,768]{1,0:T(8,128)(2,1)} %copy-done.47), channel_id=1, source_target_pairs={{0,4},{1,5},{2,6},{3,7},{4,0},{5,1},{6,2},{7,3},{8,12},{9,13},{10,... | collective-permute-start | bytes 884744 | tf_op jit(solution)/shard_map/ppermute | solution.py:390
  112.9 34.4 %collective-permute-start.22 = (bf16[192,768]{1,0:T(8,128)(2,1)}, bf16[192,768]{1,0:T(8,128)(2,1)S(1)}, u32[]{:S(2)}, u32[]{:S(2)}) collective-permute-start(bf16[192,768]{1,0:T(8,128)(2,1)} %copy-done.48), channel_id=1, source_target_pairs={{0,4},{1,5},{2,6},{3,7},{4,0},{5,1},{6,2},{7,3},{8,12},{9,13},{10,... | collective-permute-start | bytes 884744 | tf_op jit(solution)/shard_map/ppermute | solution.py:390
  113.4 33.9 %collective-permute-start.11 = (bf16[2,2,128,768]{3,2,1,0:T(8,128)(2,1)S(1)}, bf16[2,2,128,768]{3,2,1,0:T(8,128)(2,1)S(1)}, u32[]{:S(2)}, u32[]{:S(2)}) collective-permute-start(bf16[2,2,128,768]{3,2,1,0:T(8,128)(2,1)S(1)} %collective-permute-done.7.refs_9_.refs_1_), channel_id=1, source_target_pairs={{0,1},{1,0},{2,3},{3,2},{4,5},{5,4},{6,7},{7,6},{8,9},{9,8},{10,11... | collective-permute-start | bytes 2359304 | tf_op jit(solution)/shard_map/ppermute | solution.py:390
  113.4 33.9 %collective-permute-start.12 = (bf16[2,2,128,768]{3,2,1,0:T(8,128)(2,1)}, bf16[2,2,128,768]{3,2,1,0:T(8,128)(2,1)S(1)}, u32[]{:S(2)}, u32[]{:S(2)}) collective-permute-start(bf16[2,2,128,768]{3,2,1,0:T(8,128)(2,1)} %collective-permute-done.8.refs_10_.refs_2_), channel_id=1, source_target_pairs={{0,1},{1,0},{2,3},{3,2},{4,5},{5,4},{6,7},{7,6},{8,9},{9,8},{10,11... | collective-permute-start | bytes 2359304 | tf_op jit(solution)/shard_map/ppermute | solution.py:390
  231.4 28.3 %collective-permute-start.45 = (bf16[4,96,640]{2,1,0:T(8,128)(2,1)}, bf16[4,96,640]{2,1,0:T(8,128)(2,1)S(1)}, u32[]{:S(2)}, u32[]{:S(2)}) collective-permute-start(bf16[4,96,640]{2,1,0:T(8,128)(2,1)} %get-tuple-element.81), channel_id=1, source_target_pairs={{0,4},{1,5},{2,6},{3,7},{4,0},{5,1},{6,2},{7,3},{8,12},{9,13},{10,... | collective-permute-start | bytes 1474568 | tf_op jit(solution)/shard_map/ppermute | solution.py:390
  231.9 59.9 %collective-permute-start.42 = (bf16[4,2,128,768]{3,2,1,0:T(8,128)(2,1)}, bf16[4,2,128,768]{3,2,1,0:T(8,128)(2,1)S(1)}, u32[]{:S(2)}, u32[]{:S(2)}) collective-permute-start(bf16[4,2,128,768]{3,2,1,0:T(8,128)(2,1)} %get-tuple-element.77), channel_id=1, source_target_pairs={{0,1},{1,0},{2,3},{3,2},{4,5},{5,4},{6,7},{7,6},{8,9},{9,8},{10,11... | collective-permute-start | bytes 4718600 | tf_op jit(solution)/shard_map/ppermute | solution.py:390
  239.9 44.4 %collective-permute-start.51 = (bf16[4,208,768]{2,1,0:T(8,128)(2,1)}, bf16[4,208,768]{2,1,0:T(8,128)(2,1)S(1)}, u32[]{:S(2)}, u32[]{:S(2)}) collective-permute-start(bf16[4,208,768]{2,1,0:T(8,128)(2,1)} %get-tuple-element.83), channel_id=1, source_target_pairs={{0,4},{1,5},{2,6},{3,7},{4,0},{5,1},{6,2},{7,3},{8,12},{9,13},{10,... | collective-permute-start | bytes 3833864 | tf_op jit(solution)/shard_map/ppermute | solution.py:390
  245.1 48.1 %collective-permute-start.39 = (bf16[4,2,128,768]{3,2,1,0:T(8,128)(2,1)}, bf16[4,2,128,768]{3,2,1,0:T(8,128)(2,1)}, u32[]{:S(2)}, u32[]{:S(2)}) collective-permute-start(bf16[4,2,128,768]{3,2,1,0:T(8,128)(2,1)} %get-tuple-element.71), channel_id=1, source_target_pairs={{0,1},{1,0},{2,3},{3,2},{4,5},{5,4},{6,7},{7,6},{8,9},{9,8},{10,11... | collective-permute-start | bytes 4718600 | tf_op jit(solution)/shard_map/ppermute | solution.py:390
  259.7 36.4 %collective-permute-start.36 = (bf16[4,2,128,768]{3,2,1,0:T(8,128)(2,1)}, bf16[4,2,128,768]{3,2,1,0:T(8,128)(2,1)}, u32[]{:S(2)}, u32[]{:S(2)}) collective-permute-start(bf16[4,2,128,768]{3,2,1,0:T(8,128)(2,1)} %get-tuple-element.64), channel_id=1, source_target_pairs={{0,1},{1,0},{2,3},{3,2},{4,5},{5,4},{6,7},{7,6},{8,9},{9,8},{10,11... | collective-permute-start | bytes 4718600 | tf_op jit(solution)/shard_map/ppermute | solution.py:390
  287.3 23.8 %collective-permute-start.53 = (bf16[208,768]{1,0:T(8,128)(2,1)S(1)}, bf16[208,768]{1,0:T(8,128)(2,1)S(1)}, u32[]{:S(2)}, u32[]{:S(2)}) collective-permute-start(bf16[208,768]{1,0:T(8,128)(2,1)S(1)} %get-tuple-element.98), channel_id=1, source_target_pairs={{0,16},{8,24},{16,0},{24,8},{1,17},{9,25},{17,1},{25,9},{2,18},{10... | collective-permute-start | bytes 958472 | tf_op jit(solution)/shard_map/ppermute | solution.py:394
  291.7 21.0 %collective-permute-start.54 = (bf16[208,768]{1,0:T(8,128)(2,1)S(1)}, bf16[208,768]{1,0:T(8,128)(2,1)S(1)}, u32[]{:S(2)}, u32[]{:S(2)}) collective-permute-start(bf16[208,768]{1,0:T(8,128)(2,1)S(1)} %get-tuple-element.97), channel_id=1, source_target_pairs={{0,24},{8,0},{16,8},{24,16},{1,25},{9,1},{17,9},{25,17},{2,26},{10... | collective-permute-start | bytes 958472 | tf_op jit(solution)/shard_map/ppermute | solution.py:394
  293.2 21.5 %collective-permute-start.43 = (bf16[2,2,128,768]{3,2,1,0:T(8,128)(2,1)S(1)}, bf16[2,2,128,768]{3,2,1,0:T(8,128)(2,1)S(1)}, u32[]{:S(2)}, u32[]{:S(2)}) collective-permute-start(bf16[2,2,128,768]{3,2,1,0:T(8,128)(2,1)S(1)} %add_convert_fusion), channel_id=1, source_target_pairs={{0,2},{1,3},{2,0},{3,1},{4,6},{5,7},{6,4},{7,5},{8,10},{9,11},{10,... | collective-permute-start | bytes 2359304 | tf_op jit(solution)/shard_map/ppermute | solution.py:390
  296.1 34.4 %collective-permute-start.40 = (bf16[2,2,128,768]{3,2,1,0:T(8,128)(2,1)S(1)}, bf16[2,2,128,768]{3,2,1,0:T(8,128)(2,1)S(1)}, u32[]{:S(2)}, u32[]{:S(2)}) collective-permute-start(bf16[2,2,128,768]{3,2,1,0:T(8,128)(2,1)S(1)} %add_convert_fusion.1), channel_id=1, source_target_pairs={{0,2},{1,3},{2,0},{3,1},{4,6},{5,7},{6,4},{7,5},{8,10},{9,11},{10,... | collective-permute-start | bytes 2359304 | tf_op jit(solution)/shard_map/ppermute | solution.py:390
  299.7 49.8 %collective-permute-start.49 = (bf16[2,24,640]{2,1,0:T(8,128)(2,1)S(1)}, bf16[2,24,640]{2,1,0:T(8,128)(2,1)S(1)}, u32[]{:S(2)}, u32[]{:S(2)}) collective-permute-start(bf16[2,24,640]{2,1,0:T(8,128)(2,1)S(1)} %get-tuple-element.123), channel_id=1, source_target_pairs={{0,2},{1,3},{2,0},{3,1},{4,6},{5,7},{6,4},{7,5},{8,10},{9,11},{10,... | collective-permute-start | bytes 184328 | tf_op jit(solution)/shard_map/ppermute | solution.py:390
  311.1 35.2 %collective-permute-start.37 = (bf16[2,2,128,768]{3,2,1,0:T(8,128)(2,1)S(1)}, bf16[2,2,128,768]{3,2,1,0:T(8,128)(2,1)S(1)}, u32[]{:S(2)}, u32[]{:S(2)}) collective-permute-start(bf16[2,2,128,768]{3,2,1,0:T(8,128)(2,1)S(1)} %add_convert_fusion.2), channel_id=1, source_target_pairs={{0,2},{1,3},{2,0},{3,1},{4,6},{5,7},{6,4},{7,5},{8,10},{9,11},{10,... | collective-permute-start | bytes 2359304 | tf_op jit(solution)/shard_map/ppermute | solution.py:390
  314.1 36.0 %collective-permute-start.55 = (bf16[2,24,768]{2,1,0:T(8,128)(2,1)S(1)}, bf16[2,24,768]{2,1,0:T(8,128)(2,1)S(1)}, u32[]{:S(2)}, u32[]{:S(2)}) collective-permute-start(bf16[2,24,768]{2,1,0:T(8,128)(2,1)S(1)} %get-tuple-element.119), channel_id=1, source_target_pairs={{0,2},{1,3},{2,0},{3,1},{4,6},{5,7},{6,4},{7,5},{8,10},{9,11},{10,... | collective-permute-start | bytes 221192 | tf_op jit(solution)/shard_map/ppermute | solution.py:390
  316.0 39.8 %collective-permute-start.44 = (bf16[1,2,128,768]{3,2,1,0:T(8,128)(2,1)S(1)}, bf16[1,2,128,768]{3,2,1,0:T(8,128)(2,1)S(1)}, u32[]{:S(2)}, u32[]{:S(2)}) collective-permute-start(bf16[1,2,128,768]{3,2,1,0:T(8,128)(2,1)S(1)} %add_convert_fusion.3), channel_id=1, source_target_pairs={{0,4},{1,5},{2,6},{3,7},{4,0},{5,1},{6,2},{7,3},{8,12},{9,13},{10,... | collective-permute-start | bytes 1179656 | tf_op jit(solution)/shard_map/ppermute | solution.py:390
  331.9 23.9 %collective-permute-start.41 = (bf16[1,2,128,768]{3,2,1,0:T(8,128)(2,1)S(1)}, bf16[1,2,128,768]{3,2,1,0:T(8,128)(2,1)S(1)}, u32[]{:S(2)}, u32[]{:S(2)}) collective-permute-start(bf16[1,2,128,768]{3,2,1,0:T(8,128)(2,1)S(1)} %add_convert_fusion.4), channel_id=1, source_target_pairs={{0,4},{1,5},{2,6},{3,7},{4,0},{5,1},{6,2},{7,3},{8,12},{9,13},{10,... | collective-permute-start | bytes 1179656 | tf_op jit(solution)/shard_map/ppermute | solution.py:390
  (93 other events, 1036.8 us)
